TPU v7x, 256 devices: a whole 4x4x8 slice. The times are simulated.
256 devices in a mesh: sp: 64 (over y, z, x_hi), ch: 4 (over x_lo, core).
Axes of the slice: x: 4 (x_hi: 2, x_lo: 2; x = x_hi * 2 + x_lo), y: 4, z: 8, core: 2. Of those that a mesh axis runs over, the one named last changes fastest.
Arguments:
- field: bfloat16 [32, 64, 32, 4096], P('ch', 'sp'), may hold values from -6 to 6
- spectral_weight: bfloat16 [16, 2048, 1024], P(None, ('sp', 'ch')), may hold values from -1 to 1
- point_weight: bfloat16 [32, 32], replicated, may hold values from -1 to 1
- bias: float32 [32], replicated, may hold values from -3 to 3
- cotangent: bfloat16 [32, 64, 32, 4096], P('ch', 'sp'), may hold values from -6 to 6
Outputs:
- activated: bfloat16 [32, 64, 32, 4096], P('ch', 'sp')
- field_grad: bfloat16 [32, 64, 32, 4096], P('ch', 'sp')
- spectral_grad: float32 [16, 2048, 1024], P(None, ('sp', 'ch'))
- weight_grad: float32 [32, 32], replicated
- bias_grad: float32 [32], replicated
All inputs are finite; a program needn't handle non-finite values.
Results may differ from a plain program's by a relative error of at most 0.0065.
Values sent between devices are 32-bit elements; how exact they have to be, the bound alone decides.
A program may use at most 64 MiB of HBM per device.

v0:
```python
import math

import jax
import jax.numpy as jnp
from jax import lax
from jax.sharding import PartitionSpec as P

KX = 16
KY = 16
KZ = 16
KT = 8
GY = 64
GZ = 64
GT = 32
KYZ = 256
Q = 2048
LANES = 128
SUB = 8


PRECISE = lax.Precision.HIGHEST
SQRT_HALF = 0.7071067811865476
INV_ROOT_TWO_PI = 0.3989422804014327


def wave_table(length, kept_rows, positions):
    row_ids = jnp.arange(kept_rows, dtype=jnp.int32)
    half_kept = kept_rows // 2
    frequency = jnp.where(row_ids <= half_kept, row_ids, row_ids - half_kept)
    phase_ids = frequency[:, None] * positions[None, :] % length
    angles = 2.0 * math.pi / length * phase_ids.astype(jnp.float32)
    waves = jnp.where((row_ids <= half_kept)[:, None], jnp.cos(angles), jnp.sin(angles))
    return math.sqrt(2.0 / length) * waves


def exact_spread(rows, selector):
    total = None
    rest = rows
    for _ in range(3):
        piece = rest.astype(jnp.bfloat16)
        rest = rest - piece.astype(jnp.float32)
        part = jnp.dot(piece, selector, preferred_element_type=jnp.float32)
        total = part if total is None else total + part
    return total


def plane_table():
    wave_y = wave_table(GY, KY, jnp.arange(GY, dtype=jnp.int32))
    wave_z = wave_table(GZ, KZ, jnp.arange(GZ, dtype=jnp.int32))
    y_rows = jnp.repeat(wave_y, KZ, axis=0)
    z_rows = jnp.tile(wave_z, (KY, 1))
    cells = jnp.arange(GY * GZ, dtype=jnp.int32)
    y_rows, z_rows, cells = lax.optimization_barrier((y_rows, z_rows, cells))
    pick_y = (cells[None, :] // GZ == jnp.arange(GY, dtype=jnp.int32)[:, None]).astype(jnp.bfloat16)
    pick_z = (cells[None, :] % GZ == jnp.arange(GZ, dtype=jnp.int32)[:, None]).astype(jnp.bfloat16)
    product = exact_spread(y_rows, pick_y) * exact_spread(z_rows, pick_z)
    return product.astype(jnp.bfloat16)


def split_dot(values, table):
    high = values.astype(jnp.bfloat16)
    low = (values - high.astype(jnp.float32)).astype(jnp.bfloat16)
    return jnp.dot(high, table, preferred_element_type=jnp.float32) + jnp.dot(
        low, table, preferred_element_type=jnp.float32
    )


def to_spectrum(values, yz_table, time_table, x_table, extra=None):
    steps_here, planes, channels, plane_cells = values.shape
    sp_count = lax.axis_size("sp")
    flat = jnp.einsum(
        "qc,rc->qr", yz_table, values.reshape(-1, plane_cells), preferred_element_type=jnp.float32
    ).reshape(KYZ, steps_here, channels)
    partial = jnp.einsum("kt,ptc->kpc", time_table, flat, precision=PRECISE)
    send = partial.reshape(sp_count, SUB, LANES)
    if extra is not None:
        rider = jnp.zeros((sp_count, SUB, LANES), jnp.float32)
        rider = rider.at[:, 0, : Q // sp_count].set(extra.reshape(sp_count, -1))
        send = jnp.concatenate([send, rider], axis=1)
    arrived = lax.all_to_all(send, "sp", 0, 0, tiled=True)
    modes = jnp.einsum("kx,xrl->krl", x_table, arrived[:, :SUB], precision=PRECISE)
    if extra is not None:
        rider_sum = jnp.sum(arrived[:, SUB, : Q // sp_count], axis=0)
        ch_count = lax.axis_size("ch")
        row = jnp.zeros((ch_count, SUB // ch_count, LANES), jnp.float32)
        row = row.at[:, 0, : rider_sum.shape[0] // ch_count].set(rider_sum.reshape(ch_count, -1))
        modes = jnp.concatenate([modes, row.reshape(1, SUB, LANES)], axis=0)
    scattered = lax.psum_scatter(modes, "ch", scatter_dimension=1, tiled=True)
    owned = scattered[:KX].reshape(KX, -1, channels)
    if extra is None:
        return owned
    return owned, scattered[KX, 0, : Q // (sp_count * lax.axis_size("ch"))]


def to_planes(block, x_table, time_table, yz_table, steps_here, extra=None):
    channels = block.shape[2]
    sp_count = lax.axis_size("sp")
    ch_count = lax.axis_size("ch")
    rows = block.reshape(KX, SUB // ch_count, LANES)
    if extra is not None:
        row = jnp.zeros((1, SUB // ch_count, LANES), jnp.float32).at[0, 0, : extra.shape[0]].set(extra)
        rows = jnp.concatenate([rows, row], axis=0)
    gathered = lax.all_gather(rows, "ch", axis=1, tiled=True)
    spread = jnp.einsum("kx,krl->xrl", x_table, gathered[:KX], precision=PRECISE)
    if extra is not None:
        rider = jnp.broadcast_to(gathered[KX][None], (sp_count, SUB, LANES))
        spread = jnp.concatenate([spread, rider], axis=1)
    returned = lax.all_to_all(spread, "sp", 0, 0, tiled=True)
    total = None
    if extra is not None:
        pieces = returned[:, SUB:].reshape(sp_count, ch_count, SUB // ch_count, LANES)
        total = pieces[:, :, 0, : extra.shape[0]].reshape(-1)
    modes = returned[:, :SUB].reshape(KT, KYZ, channels)
    time_spread = jnp.einsum("kt,kpo->top", time_table, modes, precision=PRECISE)
    result = split_dot(time_spread.reshape(-1, KYZ), yz_table)
    return result.reshape(steps_here, 1, channels, -1), total


def shards(field, spectral_weight, point_weight, bias, cotangent):
    steps_here, planes, channels, plane_cells = field.shape
    sp_count = lax.axis_size("sp")
    grid_x = planes * sp_count
    forward_x = wave_table(grid_x, KX, jnp.arange(grid_x, dtype=jnp.int32))
    inverse_x = forward_x * math.sqrt(grid_x / KX)
    time_ids = lax.axis_index("ch") * steps_here + jnp.arange(steps_here, dtype=jnp.int32)
    forward_t = wave_table(GT, KT, time_ids)
    inverse_t = forward_t * math.sqrt(GT / KT)
    inverse_t4 = inverse_t * float(math.sqrt(GY / KY) * math.sqrt(GZ / KZ))
    yz_table = plane_table()
    coeffs = to_spectrum(field, yz_table, forward_t, forward_x)
    weights = spectral_weight.reshape(KX, -1, channels, channels).astype(jnp.float32)
    mixed_modes = jnp.einsum("kqi,kqio->kqo", coeffs, weights, precision=PRECISE)
    spatial, _ = to_planes(mixed_modes, inverse_x, inverse_t4, yz_table, steps_here)
    field_rows = field.reshape(-1, channels, plane_cells)
    linear = jnp.einsum(
        "io,riy->roy", point_weight, field_rows, preferred_element_type=jnp.float32
    ).reshape(spatial.shape)
    preact = spatial + linear + bias[None, None, :, None]
    normal_cdf = 0.5 * (1.0 + lax.erf(preact * SQRT_HALF))
    activated = (preact * normal_cdf).astype(jnp.bfloat16)
    slope = normal_cdf + preact * jnp.exp(-0.5 * preact * preact) * INV_ROOT_TWO_PI
    slopes = (cotangent.astype(jnp.float32) * slope).astype(jnp.bfloat16)
    slope_rows = slopes.reshape(-1, channels, plane_cells)
    weight_part = jnp.einsum("riy,roy->io", field_rows, slope_rows, preferred_element_type=jnp.float32)
    bias_part = jnp.sum(slopes.astype(jnp.float32), axis=(0, 1, 3))
    packed = jnp.concatenate([weight_part.reshape(-1), bias_part])
    packed = jnp.pad(packed, (0, Q - packed.shape[0]))
    slope_modes, packed_part = to_spectrum(slopes, yz_table, inverse_t4, inverse_x, extra=packed)
    spec_scale = math.sqrt(KX * Q / (grid_x * GY * GZ * GT))
    spectral_grad = (spec_scale * jnp.einsum("kqi,kqo->kqio", coeffs, slope_modes)).reshape(
        KX, -1, channels * channels
    )
    coeff_grad = jnp.einsum("kqio,kqo->kqi", weights, slope_modes, precision=PRECISE)
    grad_spatial, packed_sum = to_planes(
        coeff_grad, forward_x, forward_t, yz_table, steps_here, extra=packed_part
    )
    cell_scale = 1.0 / math.sqrt(grid_x * GY * GZ * GT)
    weight_grad = cell_scale * packed_sum[: channels * channels].reshape(channels, channels)
    bias_grad = cell_scale * packed_sum[channels * channels : channels * channels + channels]
    point_part = jnp.einsum(
        "io,roy->riy", point_weight, slope_rows, preferred_element_type=jnp.float32
    ).reshape(grad_spatial.shape)
    field_grad = (grad_spatial + point_part).astype(jnp.bfloat16)
    return (activated, field_grad, spectral_grad, weight_grad, bias_grad)


def solution(mesh):
    return jax.shard_map(
        shards,
        mesh=mesh,
        in_specs=(
            P("ch", "sp", None, None),
            P(None, ("sp", "ch"), None),
            P(),
            P(),
            P("ch", "sp", None, None),
        ),
        out_specs=(
            P("ch", "sp", None, None),
            P("ch", "sp", None, None),
            P(None, ("sp", "ch"), None),
            P(),
            P(),
        ),
        check_vma=False,
    )
```

profile of v0, /device:TPU:8, one launch (start us, length us, event | category | flops | bytes accessed | tf_op | source)
XLA Modules:
  0.0 211.3 jit_solution(1526137942910750889)
XLA Ops:
  7.3 0.1 broadcast_multiply_fusion
  7.5 0.7 fusion.22
  8.2 0.7 convolution_add_fusion.5
  8.9 2.7 %convolution_add_fusion.4 = f32[256,4096]{1,0:T(8,128)} fusion(f32[256,4096]{1,0:T(8,128)S(1)} %convolution_add_fusion.5, s32[4096]{0:T(1024)S(1)} %get-tuple-element.81, f32[256,64]{1,0:T(8,128)S(1)} %bitcast.143), kind=kOutput, calls=%fused_computation.10 | convolution fusion | flops 135643136 | bytes 8470528 | tf_op jit(solution)/shard_map/dot_general | solution.py:42
  11.6 0.7 fusion.21
  12.3 2.7 %convolution_add_fusion.3 = f32[256,4096]{1,0:T(8,128)} fusion(f32[256,4096]{1,0:T(8,128)S(1)} %fusion.21, s32[4096]{0:T(1024)S(1)} %get-tuple-element.80, f32[256,64]{1,0:T(8,128)S(1)} %bitcast.145), kind=kOutput, calls=%fused_computation.9 | convolution fusion | flops 135593984 | bytes 8470528 | tf_op jit(solution)/shard_map/dot_general | solution.py:42
  15.0 4.2 %fusion.4 = bf16[256,4096]{1,0:T(8,128)(2,1)S(1)} fusion(f32[256,4096]{1,0:T(8,128)} %convolution_add_fusion.4, f32[256,4096]{1,0:T(8,128)} %convolution_add_fusion.3, s32[4096]{0:T(1024)S(1)} %get-tuple-element.80, f32[256,64]{1,0:T(8,128)S(1)} %bitcast.146), kind=kOutput, calls=%fused_computation.13 | convolution fusion | flops 137740288 | bytes 10567680 | tf_op jit(solution)/shard_map/dot_general | solution.py:42
  19.2 1.5 fusion.17
  20.7 0.5 fusion.67
  21.2 0.4 copy.102
  21.6 0.3 reshape.315
  21.8 27.4 %all_to_all.20 = f32[64,8,128]{2,1,0:T(8,128)S(1)} all-to-all(f32[64,8,128]{2,1,0:T(8,128)S(1)} %reshape.315), channel_id=1, replica_groups=mesh['sp'=64,'ch'=4] {'sp'}, dimensions={0} | all-to-all | bytes 524288 | tf_op jit(solution)/shard_map/all_to_all | solution.py:80
  49.2 1.0 fusion.33
  50.3 1.8 reshape.317
  52.1 12.6 %reduce-scatter.3.cloned.1.call-done = f32[16,2,128]{2,0,1:T(8,128)} async-done(((f32[16,8,128]{2,0,1:T(8,128)}), f32[16,2,128]{2,0,1:T(8,128)}) %reduce-scatter.3.cloned.1.call-update) | async-done | bytes 16400 | tf_op jit(solution)/shard_map/reduce_scatter | solution.py:88
  64.7 0.7 copy.104
  65.4 0.1 reshape.337
  65.5 0.9 fusion.126
  66.5 0.1 reshape.318
  66.6 5.2 %all_gather.6 = f32[16,8,128]{2,0,1:T(8,128)S(1)} all-gather(f32[16,2,128]{2,0,1:T(8,128)S(1)} %copy.105), channel_id=1, replica_groups=mesh['sp'=64,'ch'=4] {'ch'}, dimensions={1}, use_global_device_ids=true | all-gather | bytes 81920 | tf_op jit(solution)/shard_map/all_gather | solution.py:103
  71.8 0.5 fusion.53
  72.4 0.2 copy.106
  72.5 25.8 %all_to_all.21 = f32[64,8,128]{2,1,0:T(8,128)S(1)} all-to-all(f32[64,8,128]{2,1,0:T(8,128)S(1)} %copy.106), channel_id=1, replica_groups=mesh['sp'=64,'ch'=4] {'sp'}, dimensions={0} | all-to-all | bytes 524288 | tf_op jit(solution)/shard_map/all_to_all | solution.py:108
  98.3 0.3 reshape.319
  98.6 0.3 copy.107
  99.0 0.5 convolution_bitcast_fusion.3
  99.4 0.1 copy.108
  99.6 2.3 %fusion.127 = f32[256,4096]{1,0:T(8,128)S(1)} fusion(bf16[256,256]{1,0:T(8,128)(2,1)S(1)} %get-tuple-element.77, bf16[256,4096]{1,0:T(8,128)(2,1)} %copy-done.1), kind=kOutput, calls=%fused_computation.182 | convolution fusion | flops 536870912 | bytes 6422528 | tf_op jit(solution)/shard_map/dot_general | solution.py:63
  102.0 0.8 convolution_add_fusion.1
  102.7 0.8 copy-done.8
  103.5 4.5 %convert_reduce_fusion = (f32[32]{0:T(128)S(1)}, bf16[8,1,32,4096]{3,2,0,1:T(8,128)(2,1)S(1)}, f32[8,32,4096]{2,1,0:T(8,128)}) fusion(bf16[8,1,32,4096]{3,2,1,0:T(8,128)(2,1)S(1)} %copy-done.8, f32[32]{0:T(128)S(1)} %copy-done.9, f32[8,32,4096]{2,1,0:T(8,128)S(1)} %bitcast.140, bf16[32,32]{1,0:T(8,128)(2,1)S(1)} %copy-done.7, ...), kind=kOutput, calls=%fused_computation.23 | convolution fusion | flops 82837472 | bytes 14682368 | tf_op jit(solution)/shard_map/io,riy->roy/dot_general | solution.py:135
  108.0 0.9 convolution_bitcast_fusion.4
  108.9 1.5 fusion.15
  110.4 0.5 fusion.63
  110.9 0.4 copy.113
  111.3 0.3 reshape.322
  111.9 24.6 %all_to_all.22 = f32[64,16,128]{2,1,0:T(8,128)S(1)} all-to-all(f32[64,16,128]{2,1,0:T(8,128)S(1)} %select_maximum_fusion), channel_id=1, replica_groups=mesh['sp'=64,'ch'=4] {'sp'}, dimensions={0} | all-to-all | bytes 1048576 | tf_op jit(solution)/shard_map/all_to_all | solution.py:80
  136.5 0.3 fusion.29
  137.0 0.7 pad_maximum_fusion.1
  137.7 0.1 reshape.316
  137.8 14.7 %reduce-scatter.5.cloned.1.call-done = f32[17,2,128]{2,0,1:T(8,128)} async-done(((f32[17,8,128]{2,0,1:T(8,128)}), f32[17,2,128]{2,0,1:T(8,128)}) %reduce-scatter.5.cloned.1.call-update) | async-done | bytes 17424 | tf_op jit(solution)/shard_map/reduce_scatter | solution.py:88
  152.5 0.7 slice.114
  153.3 0.1 reshape.344
  153.4 3.0 %fusion.128 = f32[16,8,1,32]{3,2,1,0:T(1,128)S(1)} fusion(f32[16,8,32,1]{2,3,1,0:T(1,128)S(1)} %bitcast.152, bf16[16,8,32,32]{3,2,1,0:T(8,128)(2,1)} %copy-done.6), kind=kOutput, calls=%fused_computation.183 | convolution fusion | flops 1572864 | bytes 294912 | tf_op jit(solution)/shard_map/kqio,kqo->kqi/dot_general | solution.py:153
  156.3 0.1 reshape.328
  156.4 0.7 slice.115
  157.1 5.3 %all_gather.7 = f32[17,8,128]{2,0,1:T(8,128)S(1)} all-gather(f32[17,2,128]{2,0,1:T(8,128)S(1)} %copy.120), channel_id=1, replica_groups=mesh['sp'=64,'ch'=4] {'ch'}, dimensions={1}, use_global_device_ids=true | all-gather | bytes 87040 | tf_op jit(solution)/shard_map/all_gather | solution.py:103
  162.5 0.5 fusion.41
  163.1 1.1 copy.121
  164.2 12.7 %all-to-all-start.3 = ((f32[64,16,128]{2,1,0:T(8,128)}), f32[64,16,128]{2,1,0:T(8,128)S(1)}, u32[]{:S(2)}, u32[]{:S(2)}) async-start(f32[64,16,128]{2,1,0:T(8,128)} %copy.121), calls=%async_computation.5 | async-start | bytes 1048576 | tf_op jit(solution)/shard_map/all_to_all | solution.py:108
  176.9 3.6 %fusion.14 = bf16[8,1,32,4096]{3,2,1,0:T(8,128)(2,1)} fusion(f32[8,32,4096]{2,1,0:T(8,128)} %get-tuple-element.82), kind=kLoop, calls=%fused_computation.26 | loop fusion | flops 5242880 | bytes 6291456
  180.5 0.1 reshape.327
  180.6 1.8 multiply_multiply_fusion.1
  182.3 3.1 %reshape.332 = f32[16,8,1024]{2,1,0:T(8,128)} reshape(f32[16,8,32,32]{3,2,1,0:T(8,128)} %multiply_multiply_fusion.1) | data formatting | bytes 1048576 | tf_op jit(solution)/shard_map/reshape | solution.py:150
  185.4 10.3 %all-to-all-done.3 = f32[64,16,128]{2,1,0:T(8,128)S(1)} async-done(((f32[64,16,128]{2,1,0:T(8,128)}), f32[64,16,128]{2,1,0:T(8,128)S(1)}, u32[]{:S(2)}, u32[]{:S(2)}) %all-to-all-start.3) | async-done | bytes 524320 | tf_op jit(solution)/shard_map/all_to_all | solution.py:108
  195.9 0.3 reshape.329
  196.2 0.3 copy.122
  196.5 0.5 convolution_bitcast_fusion.2
  197.1 2.3 %fusion.129 = f32[256,4096]{1,0:T(8,128)S(1)} fusion(bf16[256,256]{1,0:T(8,128)(2,1)S(1)} %get-tuple-element.73, bf16[256,4096]{1,0:T(8,128)(2,1)} %copy-done.1), kind=kOutput, calls=%fused_computation.184 | convolution fusion | flops 536870912 | bytes 6422528 | tf_op jit(solution)/shard_map/dot_general | solution.py:63
  199.5 0.7 convolution_add_fusion
  200.2 0.9 copy-done.5
  201.1 2.0 fusion.6
  203.2 0.7 copy.128
  203.8 0.6 mul.246
  (56 shorter events, 1.1 us)
Async XLA Ops:
  7.2 12.0 %copy-start = (bf16[8,1,32,4096]{3,2,1,0:T(8,128)(2,1)S(1)}, bf16[8,1,32,4096]{3,2,1,0:T(8,128)(2,1)}, u32[]{:S(2)}) copy-start(bf16[8,1,32,4096]{3,2,1,0:T(8,128)(2,1)} %param.11) | copy-start | bytes 6291460
  7.2 57.5 %reduce-scatter.3.cloned.1.call-start = ((), (), s32[]{:S(2)}) async-start(), calls=%async_computation.6 | async-start | bytes 81920 | tf_op jit(solution)/shard_map/reduce_scatter | solution.py:88
  19.1 1.5 copy-start.1
  50.2 102.3 %reduce-scatter.5.cloned.1.call-start = ((), (), s32[]{:S(2)}) async-start(), calls=%async_computation.7 | async-start | bytes 122880 | tf_op jit(solution)/shard_map/reduce_scatter | solution.py:88
  52.1 20.4 %copy-start.6 = (bf16[16,8,32,32]{3,2,1,0:T(8,128)(2,1)}, bf16[16,8,32,32]{3,2,1,0:T(8,128)(2,1)S(1)}, u32[]{:S(2)}) copy-start(bf16[16,8,32,32]{3,2,1,0:T(8,128)(2,1)S(1)} %reshape.317) | copy-start | bytes 786436
  98.9 3.0 %copy-start.2 = (bf16[256,4096]{1,0:T(8,128)(2,1)S(1)}, bf16[256,4096]{1,0:T(8,128)(2,1)}, u32[]{:S(2)}) copy-start(bf16[256,4096]{1,0:T(8,128)(2,1)} %copy-done.1) | copy-start | bytes 6291460
  101.9 0.8 copy-start.7
  101.9 1.6 copy-start.8
  101.9 1.6 copy-start.9
  108.0 2.4 %copy-start.4 = (bf16[8,1,32,4096]{3,2,0,1:T(8,128)(2,1)}, bf16[8,1,32,4096]{3,2,0,1:T(8,128)(2,1)S(1)}, u32[]{:S(2)}) copy-start(bf16[8,1,32,4096]{3,2,0,1:T(8,128)(2,1)S(1)} %get-tuple-element.75) | copy-start | bytes 6291460
  164.2 31.6 %all-to-all-start.3 = ((f32[64,16,128]{2,1,0:T(8,128)}), f32[64,16,128]{2,1,0:T(8,128)S(1)}, u32[]{:S(2)}, u32[]{:S(2)}) async-start(f32[64,16,128]{2,1,0:T(8,128)} %copy.121), calls=%async_computation.5 | async-start | bytes 1048576 | tf_op jit(solution)/shard_map/all_to_all | solution.py:108
  196.5 3.0 %copy-start.3 = (bf16[256,4096]{1,0:T(8,128)(2,1)S(1)}, bf16[256,4096]{1,0:T(8,128)(2,1)}, u32[]{:S(2)}) copy-start(bf16[256,4096]{1,0:T(8,128)(2,1)} %copy-done.1) | copy-start | bytes 6291460
  199.5 1.6 copy-start.5
Sparse Core Ops, SparseCore 0:
  50.3 14.3 reduce-scatter.2
  137.8 14.6 reduce-scatter.4
where the time goes:
time: 212 us; the launch traced here: 211 us
  blocking collectives  88.3 us (42%)
  waiting for transfers between devices  37.7 us (18%)
  matrix products  36.4 us (17%)
  local copies, waits for them, and re-layouts  15 us (7%)
  between operations  14.6 us (7%)
  starting transfers between devices  12.8 us (6%)
  other arithmetic  6.46 us (3%)
    all_to_all x2, blocking collectives, to_spectrum(): arrived = lax.all_to_all(send, 'sp', 0, 0, tiled=True)  52 us
    reduce_scatter x2, waiting for transfers between devices, to_spectrum(): scattered = lax.psum_scatter(modes, 'ch', scatter_dimension=1, tiled=True)  27.3 us
    all_to_all x1, blocking collectives, to_planes(): returned = lax.all_to_all(spread, 'sp', 0, 0, tiled=True)  25.8 us
    all_to_all x1, starting transfers between devices, to_planes(): returned = lax.all_to_all(spread, 'sp', 0, 0, tiled=True)  12.7 us
    dot_general x6, matrix products, exact_spread(): part = jnp.dot(piece, selector, preferred_element_type=jnp.float32)  11.6 us
    all_gather x2, blocking collectives, to_planes(): gathered = lax.all_gather(rows, 'ch', axis=1, tiled=True)  10.6 us
    all_to_all x1, waiting for transfers between devices, to_planes(): returned = lax.all_to_all(spread, 'sp', 0, 0, tiled=True)  10.3 us
    dot_general x2, matrix products, split_dot(): jnp.dot(high, table, preferred_element_type=jnp.float32)  4.68 us
  transfers between devices with their start and end apart: 3, of which 3 were waited for; matrix products, arithmetic and copies ran while one was open for 5% of the time, Pallas kernels for 0%

commit v1 on v0

--- a/solution.py
+++ b/solution.py
@@ -37,9 +37,9 @@
     total = None
     rest = rows
     for _ in range(3):
-        piece = rest.astype(jnp.bfloat16)
-        rest = rest - piece.astype(jnp.float32)
-        part = jnp.dot(piece, selector, preferred_element_type=jnp.float32)
+        piece = lax.reduce_precision(rest, exponent_bits=8, mantissa_bits=7)
+        rest = rest - piece
+        part = jnp.dot(piece.astype(jnp.bfloat16), selector, preferred_element_type=jnp.float32)
         total = part if total is None else total + part
     return total
 
@@ -58,9 +58,9 @@
 
 
 def split_dot(values, table):
-    high = values.astype(jnp.bfloat16)
-    low = (values - high.astype(jnp.float32)).astype(jnp.bfloat16)
-    return jnp.dot(high, table, preferred_element_type=jnp.float32) + jnp.dot(
+    high = lax.reduce_precision(values, exponent_bits=8, mantissa_bits=7)
+    low = (values - high).astype(jnp.bfloat16)
+    return jnp.dot(high.astype(jnp.bfloat16), table, preferred_element_type=jnp.float32) + jnp.dot(
         low, table, preferred_element_type=jnp.float32
     )
 

time: 212 us -> 212 us (level)
  no operation moved by 1% of the time
where the time goes in v1:
time: 212 us; the launch traced here: 211 us
  blocking collectives  88.4 us (42%)
  waiting for transfers between devices  37.7 us (18%)
  matrix products  36.4 us (17%)
  local copies, waits for them, and re-layouts  15 us (7%)
  between operations  14.6 us (7%)
  starting transfers between devices  12.8 us (6%)
  other arithmetic  6.48 us (3%)
    all_to_all x2, blocking collectives, to_spectrum(): arrived = lax.all_to_all(send, 'sp', 0, 0, tiled=True)  52 us
    reduce_scatter x2, waiting for transfers between devices, to_spectrum(): scattered = lax.psum_scatter(modes, 'ch', scatter_dimension=1, tiled=True)  27.4 us
    all_to_all x1, blocking collectives, to_planes(): returned = lax.all_to_all(spread, 'sp', 0, 0, tiled=True)  25.8 us
    all_to_all x1, starting transfers between devices, to_planes(): returned = lax.all_to_all(spread, 'sp', 0, 0, tiled=True)  12.7 us
    dot_general x6, matrix products, exact_spread(): jnp.dot(piece.astype(jnp.bfloat16), selector, preferred_element_type=jnp....  11.6 us
    all_gather x2, blocking collectives, to_planes(): gathered = lax.all_gather(rows, 'ch', axis=1, tiled=True)  10.6 us
    all_to_all x1, waiting for transfers between devices, to_planes(): returned = lax.all_to_all(spread, 'sp', 0, 0, tiled=True)  10.3 us
    dot_general x2, matrix products, split_dot(): jnp.dot(high.astype(jnp.bfloat16), table, preferred_element_type=jnp.floa...  4.68 us
  transfers between devices with their start and end apart: 3, of which 3 were waited for; matrix products, arithmetic and copies ran while one was open for 5% of the time, Pallas kernels for 0%

profile of v1, /device:TPU:8, one launch (start us, length us, event | category | flops | bytes accessed | tf_op | source)
XLA Modules:
  0.0 211.3 jit_solution(15377633663171127605)
XLA Ops:
  7.3 0.1 broadcast_multiply_fusion
  7.5 0.7 fusion.22
  8.2 0.7 convolution_add_fusion.5
  8.9 2.7 %convolution_add_fusion.4 = f32[256,4096]{1,0:T(8,128)} fusion(f32[256,4096]{1,0:T(8,128)S(1)} %convolution_add_fusion.5, s32[4096]{0:T(1024)S(1)} %get-tuple-element.81, f32[256,64]{1,0:T(8,128)S(1)} %bitcast.137), kind=kOutput, calls=%fused_computation.10 | convolution fusion | flops 135626752 | bytes 8470528 | tf_op jit(solution)/shard_map/dot_general | solution.py:42
  11.6 0.7 fusion.21
  12.3 2.7 %convolution_add_fusion.3 = f32[256,4096]{1,0:T(8,128)} fusion(f32[256,4096]{1,0:T(8,128)S(1)} %fusion.21, s32[4096]{0:T(1024)S(1)} %get-tuple-element.80, f32[256,64]{1,0:T(8,128)S(1)} %bitcast.139), kind=kOutput, calls=%fused_computation.9 | convolution fusion | flops 135593984 | bytes 8470528 | tf_op jit(solution)/shard_map/dot_general | solution.py:42
  15.0 4.2 %fusion.4 = bf16[256,4096]{1,0:T(8,128)(2,1)S(1)} fusion(f32[256,4096]{1,0:T(8,128)} %convolution_add_fusion.4, f32[256,4096]{1,0:T(8,128)} %convolution_add_fusion.3, s32[4096]{0:T(1024)S(1)} %get-tuple-element.80, f32[256,64]{1,0:T(8,128)S(1)} %bitcast.140), kind=kOutput, calls=%fused_computation.13 | convolution fusion | flops 137723904 | bytes 10567680 | tf_op jit(solution)/shard_map/dot_general | solution.py:42
  19.2 1.5 fusion.17
  20.7 0.5 fusion.67
  21.2 0.4 copy.102
  21.6 0.3 reshape.315
  21.9 27.4 %all_to_all.20 = f32[64,8,128]{2,1,0:T(8,128)S(1)} all-to-all(f32[64,8,128]{2,1,0:T(8,128)S(1)} %reshape.315), channel_id=1, replica_groups=mesh['sp'=64,'ch'=4] {'sp'}, dimensions={0} | all-to-all | bytes 524288 | tf_op jit(solution)/shard_map/all_to_all | solution.py:80
  49.2 1.0 fusion.33
  50.3 1.8 reshape.317
  52.1 12.6 %reduce-scatter.3.cloned.1.call-done = f32[16,2,128]{2,0,1:T(8,128)} async-done(((f32[16,8,128]{2,0,1:T(8,128)}), f32[16,2,128]{2,0,1:T(8,128)}) %reduce-scatter.3.cloned.1.call-update) | async-done | bytes 16400 | tf_op jit(solution)/shard_map/reduce_scatter | solution.py:88
  64.7 0.7 copy.104
  65.4 0.1 reshape.337
  65.5 0.9 fusion.126
  66.5 0.1 reshape.318
  66.6 5.2 %all_gather.6 = f32[16,8,128]{2,0,1:T(8,128)S(1)} all-gather(f32[16,2,128]{2,0,1:T(8,128)S(1)} %copy.105), channel_id=1, replica_groups=mesh['sp'=64,'ch'=4] {'ch'}, dimensions={1}, use_global_device_ids=true | all-gather | bytes 81920 | tf_op jit(solution)/shard_map/all_gather | solution.py:103
  71.8 0.5 fusion.53
  72.4 0.2 copy.106
  72.5 25.8 %all_to_all.21 = f32[64,8,128]{2,1,0:T(8,128)S(1)} all-to-all(f32[64,8,128]{2,1,0:T(8,128)S(1)} %copy.106), channel_id=1, replica_groups=mesh['sp'=64,'ch'=4] {'sp'}, dimensions={0} | all-to-all | bytes 524288 | tf_op jit(solution)/shard_map/all_to_all | solution.py:108
  98.4 0.3 reshape.319
  98.6 0.3 copy.107
  99.0 0.5 convolution_bitcast_fusion.3
  99.5 0.1 copy.108
  99.6 2.3 %fusion.127 = f32[256,4096]{1,0:T(8,128)S(1)} fusion(bf16[256,256]{1,0:T(8,128)(2,1)S(1)} %get-tuple-element.79, bf16[256,4096]{1,0:T(8,128)(2,1)} %copy-done.1), kind=kOutput, calls=%fused_computation.186 | convolution fusion | flops 536870912 | bytes 6422528 | tf_op jit(solution)/shard_map/dot_general | solution.py:63
  102.0 0.8 convolution_add_fusion.1
  102.8 0.8 copy-done.8
  103.6 4.5 %convert_reduce_fusion = (f32[32]{0:T(128)S(1)}, bf16[8,1,32,4096]{3,2,0,1:T(8,128)(2,1)S(1)}, f32[8,32,4096]{2,1,0:T(8,128)}) fusion(bf16[8,1,32,4096]{3,2,1,0:T(8,128)(2,1)S(1)} %copy-done.8, f32[32]{0:T(128)S(1)} %copy-done.9, f32[8,32,4096]{2,1,0:T(8,128)S(1)} %bitcast.134, bf16[32,32]{1,0:T(8,128)(2,1)S(1)} %copy-done.7, ...), kind=kOutput, calls=%fused_computation.23 | convolution fusion | flops 82837472 | bytes 14682368 | tf_op jit(solution)/shard_map/io,riy->roy/dot_general | solution.py:135
  108.0 0.9 convolution_bitcast_fusion.4
  108.9 1.5 fusion.15
  110.4 0.5 fusion.63
  110.9 0.4 copy.113
  111.3 0.3 reshape.322
  111.9 24.6 %all_to_all.22 = f32[64,16,128]{2,1,0:T(8,128)S(1)} all-to-all(f32[64,16,128]{2,1,0:T(8,128)S(1)} %select_maximum_fusion), channel_id=1, replica_groups=mesh['sp'=64,'ch'=4] {'sp'}, dimensions={0} | all-to-all | bytes 1048576 | tf_op jit(solution)/shard_map/all_to_all | solution.py:80
  136.5 0.3 fusion.31
  137.0 0.7 pad_maximum_fusion.1
  137.7 0.1 reshape.316
  137.8 14.8 %reduce-scatter.5.cloned.1.call-done = f32[17,2,128]{2,0,1:T(8,128)} async-done(((f32[17,8,128]{2,0,1:T(8,128)}), f32[17,2,128]{2,0,1:T(8,128)}) %reduce-scatter.5.cloned.1.call-update) | async-done | bytes 17424 | tf_op jit(solution)/shard_map/reduce_scatter | solution.py:88
  152.6 0.7 slice.114
  153.3 0.1 reshape.344
  153.4 3.0 %fusion.128 = f32[16,8,1,32]{3,2,1,0:T(1,128)S(1)} fusion(f32[16,8,32,1]{2,3,1,0:T(1,128)S(1)} %bitcast.146, bf16[16,8,32,32]{3,2,1,0:T(8,128)(2,1)} %copy-done.6), kind=kOutput, calls=%fused_computation.187 | convolution fusion | flops 1572864 | bytes 294912 | tf_op jit(solution)/shard_map/kqio,kqo->kqi/dot_general | solution.py:153
  156.4 0.1 reshape.328
  156.5 0.7 slice.115
  157.2 5.3 %all_gather.7 = f32[17,8,128]{2,0,1:T(8,128)S(1)} all-gather(f32[17,2,128]{2,0,1:T(8,128)S(1)} %copy.120), channel_id=1, replica_groups=mesh['sp'=64,'ch'=4] {'ch'}, dimensions={1}, use_global_device_ids=true | all-gather | bytes 87040 | tf_op jit(solution)/shard_map/all_gather | solution.py:103
  162.5 0.5 fusion.41
  163.1 1.1 copy.121
  164.2 12.7 %all-to-all-start.3 = ((f32[64,16,128]{2,1,0:T(8,128)}), f32[64,16,128]{2,1,0:T(8,128)S(1)}, u32[]{:S(2)}, u32[]{:S(2)}) async-start(f32[64,16,128]{2,1,0:T(8,128)} %copy.121), calls=%async_computation.5 | async-start | bytes 1048576 | tf_op jit(solution)/shard_map/all_to_all | solution.py:108
  177.0 3.6 %fusion.14 = bf16[8,1,32,4096]{3,2,1,0:T(8,128)(2,1)} fusion(f32[8,32,4096]{2,1,0:T(8,128)} %get-tuple-element.82), kind=kLoop, calls=%fused_computation.26 | loop fusion | flops 5242880 | bytes 6291456
  180.6 0.1 reshape.327
  180.6 1.8 multiply_multiply_fusion.1
  182.4 3.1 %reshape.332 = f32[16,8,1024]{2,1,0:T(8,128)} reshape(f32[16,8,32,32]{3,2,1,0:T(8,128)} %multiply_multiply_fusion.1) | data formatting | bytes 1048576 | tf_op jit(solution)/shard_map/reshape | solution.py:150
  185.5 10.3 %all-to-all-done.3 = f32[64,16,128]{2,1,0:T(8,128)S(1)} async-done(((f32[64,16,128]{2,1,0:T(8,128)}), f32[64,16,128]{2,1,0:T(8,128)S(1)}, u32[]{:S(2)}, u32[]{:S(2)}) %all-to-all-start.3) | async-done | bytes 524320 | tf_op jit(solution)/shard_map/all_to_all | solution.py:108
  195.9 0.3 reshape.329
  196.2 0.3 copy.122
  196.6 0.5 convolution_bitcast_fusion.2
  197.2 2.3 %fusion.129 = f32[256,4096]{1,0:T(8,128)S(1)} fusion(bf16[256,256]{1,0:T(8,128)(2,1)S(1)} %get-tuple-element.77, bf16[256,4096]{1,0:T(8,128)(2,1)} %copy-done.1), kind=kOutput, calls=%fused_computation.188 | convolution fusion | flops 536870912 | bytes 6422528 | tf_op jit(solution)/shard_map/dot_general | solution.py:63
  199.5 0.7 convolution_add_fusion
  200.3 0.9 copy-done.5
  201.1 2.0 fusion.6
  203.2 0.7 copy.128
  203.9 0.6 mul.246
  (56 shorter events, 1.2 us)
Async XLA Ops:
  7.2 12.0 %copy-start = (bf16[8,1,32,4096]{3,2,1,0:T(8,128)(2,1)S(1)}, bf16[8,1,32,4096]{3,2,1,0:T(8,128)(2,1)}, u32[]{:S(2)}) copy-start(bf16[8,1,32,4096]{3,2,1,0:T(8,128)(2,1)} %param.11) | copy-start | bytes 6291460
  7.2 57.5 %reduce-scatter.3.cloned.1.call-start = ((), (), s32[]{:S(2)}) async-start(), calls=%async_computation.6 | async-start | bytes 81920 | tf_op jit(solution)/shard_map/reduce_scatter | solution.py:88
  19.2 1.5 copy-start.1
  50.2 102.4 %reduce-scatter.5.cloned.1.call-start = ((), (), s32[]{:S(2)}) async-start(), calls=%async_computation.7 | async-start | bytes 122880 | tf_op jit(solution)/shard_map/reduce_scatter | solution.py:88
  52.1 20.4 %copy-start.6 = (bf16[16,8,32,32]{3,2,1,0:T(8,128)(2,1)}, bf16[16,8,32,32]{3,2,1,0:T(8,128)(2,1)S(1)}, u32[]{:S(2)}) copy-start(bf16[16,8,32,32]{3,2,1,0:T(8,128)(2,1)S(1)} %reshape.317) | copy-start | bytes 786436
  99.0 3.0 %copy-start.2 = (bf16[256,4096]{1,0:T(8,128)(2,1)S(1)}, bf16[256,4096]{1,0:T(8,128)(2,1)}, u32[]{:S(2)}) copy-start(bf16[256,4096]{1,0:T(8,128)(2,1)} %copy-done.1) | copy-start | bytes 6291460
  101.9 0.8 copy-start.7
  102.0 1.6 copy-start.8
  102.0 1.6 copy-start.9
  108.0 2.4 %copy-start.4 = (bf16[8,1,32,4096]{3,2,0,1:T(8,128)(2,1)}, bf16[8,1,32,4096]{3,2,0,1:T(8,128)(2,1)S(1)}, u32[]{:S(2)}) copy-start(bf16[8,1,32,4096]{3,2,0,1:T(8,128)(2,1)S(1)} %get-tuple-element.73) | copy-start | bytes 6291460
  164.2 31.6 %all-to-all-start.3 = ((f32[64,16,128]{2,1,0:T(8,128)}), f32[64,16,128]{2,1,0:T(8,128)S(1)}, u32[]{:S(2)}, u32[]{:S(2)}) async-start(f32[64,16,128]{2,1,0:T(8,128)} %copy.121), calls=%async_computation.5 | async-start | bytes 1048576 | tf_op jit(solution)/shard_map/all_to_all | solution.py:108
  196.6 3.0 %copy-start.3 = (bf16[256,4096]{1,0:T(8,128)(2,1)S(1)}, bf16[256,4096]{1,0:T(8,128)(2,1)}, u32[]{:S(2)}) copy-start(bf16[256,4096]{1,0:T(8,128)(2,1)} %copy-done.1) | copy-start | bytes 6291460
  199.5 1.6 copy-start.5
Sparse Core Ops, SparseCore 0:
  50.3 14.3 reduce-scatter.2
  137.8 14.7 reduce-scatter.4

commit v2 on v1

--- a/solution.py
+++ b/solution.py
@@ -85,7 +85,9 @@
         row = jnp.zeros((ch_count, SUB // ch_count, LANES), jnp.float32)
         row = row.at[:, 0, : rider_sum.shape[0] // ch_count].set(rider_sum.reshape(ch_count, -1))
         modes = jnp.concatenate([modes, row.reshape(1, SUB, LANES)], axis=0)
-    scattered = lax.psum_scatter(modes, "ch", scatter_dimension=1, tiled=True)
+    ch_count = lax.axis_size("ch")
+    parts = lax.all_to_all(modes, "ch", 1, 0, tiled=True)
+    scattered = jnp.sum(parts.reshape(ch_count, -1, SUB // ch_count, LANES), axis=0)
     owned = scattered[:KX].reshape(KX, -1, channels)
     if extra is None:
         return owned
@@ -100,7 +102,8 @@
     if extra is not None:
         row = jnp.zeros((1, SUB // ch_count, LANES), jnp.float32).at[0, 0, : extra.shape[0]].set(extra)
         rows = jnp.concatenate([rows, row], axis=0)
-    gathered = lax.all_gather(rows, "ch", axis=1, tiled=True)
+    copies = jnp.broadcast_to(rows[:, None], (rows.shape[0], ch_count) + rows.shape[1:])
+    gathered = lax.all_to_all(copies, "ch", 1, 1, tiled=True).reshape(rows.shape[0], SUB, LANES)
     spread = jnp.einsum("kx,krl->xrl", x_table, gathered[:KX], precision=PRECISE)
     if extra is not None:
         rider = jnp.broadcast_to(gathered[KX][None], (sp_count, SUB, LANES))

time: 212 us -> 171 us (0.81)
  waiting for transfers between devices: 37.7 us -> 15.8 us
  between operations: 14.6 us -> 1.24 us
  blocking collectives: 88.4 us -> 83.8 us
    reduce_scatter x2 -> x0, waiting for transfers between devices: 27.4 us -> none  [to_spectrum(): scattered = lax.psum_scatter(modes, 'ch', scatter_dimension=1, tiled=True)]
    all_to_all x0 -> x2, blocking collectives: none -> 13.2 us  [the longest x1 6.67 us: to_spectrum(): parts = lax.all_to_all(modes, 'ch', 1, 0, tiled=True)]
    all_gather x2 -> x0, blocking collectives: 10.6 us -> none  [to_planes(): gathered = lax.all_gather(rows, 'ch', axis=1, tiled=True)]
    all_to_all x1, blocking collectives: 25.8 us -> 19.1 us  [to_planes(): returned = lax.all_to_all(spread, 'sp', 0, 0, tiled=True)]
    all_to_all x0 -> x2, starting transfers between devices: none -> 6.57 us  [the longest x1 3.29 us: to_planes(): lax.all_to_all(copies, 'ch', 1, 1, tiled=True)]
    all_to_all x0 -> x2, waiting for transfers between devices: none -> 6.24 us  [the longest x1 4.01 us: to_planes(): lax.all_to_all(copies, 'ch', 1, 1, tiled=True)]
    all_to_all x1, starting transfers between devices: 12.7 us -> 6.89 us  [to_planes(): returned = lax.all_to_all(spread, 'sp', 0, 0, tiled=True)]
  transfers between devices with their start and end apart: 3 -> 3, of which waited for: 3 -> 3; matrix products, arithmetic and copies ran while one was open for 5% -> 6% of each run, Pallas kernels for 0% -> 0%
where the time goes in v2:
time: 171 us; the launch traced here: 170 us
  blocking collectives  83.8 us (49%)
  matrix products  36.4 us (21%)
  waiting for transfers between devices  15.8 us (9%)
  local copies, waits for them, and re-layouts  13.6 us (8%)
  starting transfers between devices  13.5 us (8%)
  other arithmetic  5.86 us (3%)
    all_to_all x2, blocking collectives, to_spectrum(): arrived = lax.all_to_all(send, 'sp', 0, 0, tiled=True)  51.5 us
    all_to_all x1, blocking collectives, to_planes(): returned = lax.all_to_all(spread, 'sp', 0, 0, tiled=True)  19.1 us
    dot_general x6, matrix products, exact_spread(): jnp.dot(piece.astype(jnp.bfloat16), selector, preferred_element_type=jnp....  11.6 us
    all_to_all x1, waiting for transfers between devices, to_planes(): returned = lax.all_to_all(spread, 'sp', 0, 0, tiled=True)  9.52 us
    all_to_all x1, starting transfers between devices, to_planes(): returned = lax.all_to_all(spread, 'sp', 0, 0, tiled=True)  6.89 us
    all_to_all x1, blocking collectives, to_spectrum(): parts = lax.all_to_all(modes, 'ch', 1, 0, tiled=True)  6.67 us
    all_to_all x1, blocking collectives, to_planes(): lax.all_to_all(copies, 'ch', 1, 1, tiled=True)  6.49 us
    dot_general x2, matrix products, split_dot(): jnp.dot(high.astype(jnp.bfloat16), table, preferred_element_type=jnp.floa...  4.68 us
  transfers between devices with their start and end apart: 3, of which 3 were waited for; matrix products, arithmetic and copies ran while one was open for 6% of the time, Pallas kernels for 0%

profile of v2, /device:TPU:8, one launch (start us, length us, event | category | flops | bytes accessed | tf_op | source)
XLA Modules:
  0.0 170.1 jit_solution(1467995672817878582)
XLA Ops:
  0.7 0.1 broadcast_multiply_fusion
  0.9 0.7 fusion.22
  1.6 0.7 convolution_add_fusion.5
  2.3 2.7 %convolution_add_fusion.4 = f32[256,4096]{1,0:T(8,128)} fusion(f32[256,4096]{1,0:T(8,128)S(1)} %convolution_add_fusion.5, s32[4096]{0:T(1024)S(1)} %get-tuple-element.81, f32[256,64]{1,0:T(8,128)S(1)} %bitcast.142), kind=kOutput, calls=%fused_computation.10 | convolution fusion | flops 135626752 | bytes 8470528 | tf_op jit(solution)/shard_map/dot_general | solution.py:42
  5.0 0.7 fusion.21
  5.7 2.7 %convolution_add_fusion.3 = f32[256,4096]{1,0:T(8,128)} fusion(f32[256,4096]{1,0:T(8,128)S(1)} %fusion.21, s32[4096]{0:T(1024)S(1)} %get-tuple-element.80, f32[256,64]{1,0:T(8,128)S(1)} %bitcast.144), kind=kOutput, calls=%fused_computation.9 | convolution fusion | flops 135593984 | bytes 8470528 | tf_op jit(solution)/shard_map/dot_general | solution.py:42
  8.4 4.2 %fusion.4 = bf16[256,4096]{1,0:T(8,128)(2,1)S(1)} fusion(f32[256,4096]{1,0:T(8,128)} %convolution_add_fusion.4, f32[256,4096]{1,0:T(8,128)} %convolution_add_fusion.3, s32[4096]{0:T(1024)S(1)} %get-tuple-element.80, f32[256,64]{1,0:T(8,128)S(1)} %bitcast.145), kind=kOutput, calls=%fused_computation.13 | convolution fusion | flops 137723904 | bytes 10567680 | tf_op jit(solution)/shard_map/dot_general | solution.py:42
  12.6 1.5 fusion.17
  14.1 0.5 fusion.66
  14.6 0.4 copy.99
  15.0 0.3 reshape.325
  15.3 27.4 %all_to_all.54 = f32[64,8,128]{2,1,0:T(8,128)S(1)} all-to-all(f32[64,8,128]{2,1,0:T(8,128)S(1)} %reshape.325), channel_id=1, replica_groups=mesh['sp'=64,'ch'=4] {'sp'}, dimensions={0} | all-to-all | bytes 524288 | tf_op jit(solution)/shard_map/all_to_all | solution.py:80
  42.6 1.0 fusion.33
  43.6 3.3 %all-to-all-start.1 = ((f32[16,8,128]{2,0,1:T(8,128)}), f32[16,8,128]{2,0,1:T(8,128)S(1)}, u32[]{:S(2)}, u32[]{:S(2)}) async-start(f32[16,8,128]{2,0,1:T(8,128)} %fusion.33), calls=%async_computation.1 | async-start | bytes 131072 | tf_op jit(solution)/shard_map/all_to_all | solution.py:89
  46.9 1.8 %reshape.327 = bf16[16,8,32,32]{3,2,1,0:T(8,128)(2,1)S(1)} reshape(bf16[16,8,1024]{2,1,0:T(8,128)(2,1)} %param.12) | data formatting | bytes 524288 | tf_op jit(solution)/shard_map/reshape | solution.py:134
  48.8 2.2 %all-to-all-done.1 = f32[16,8,128]{2,0,1:T(8,128)S(1)} async-done(((f32[16,8,128]{2,0,1:T(8,128)}), f32[16,8,128]{2,0,1:T(8,128)S(1)}, u32[]{:S(2)}, u32[]{:S(2)}) %all-to-all-start.1) | async-done | bytes 65568 | tf_op jit(solution)/shard_map/all_to_all | solution.py:89
  51.0 0.1 reshape.347
  51.1 0.9 fusion.125
  52.0 0.1 broadcast_in_dim.78
  52.2 6.5 %all_to_all.55 = f32[16,4,2,128]{3,0,2,1:T(8,128)S(1)} all-to-all(f32[16,4,2,128]{3,0,2,1:T(8,128)S(1)} %broadcast_in_dim.79), channel_id=1, replica_groups=mesh['sp'=64,'ch'=4] {'ch'}, dimensions={1} | all-to-all | bytes 131072 | tf_op jit(solution)/shard_map/all_to_all | solution.py:106
  58.7 0.5 fusion.52
  59.2 0.2 copy.103
  59.4 19.1 %all_to_all.56 = f32[64,8,128]{2,1,0:T(8,128)S(1)} all-to-all(f32[64,8,128]{2,1,0:T(8,128)S(1)} %copy.103), channel_id=1, replica_groups=mesh['sp'=64,'ch'=4] {'sp'}, dimensions={0} | all-to-all | bytes 524288 | tf_op jit(solution)/shard_map/all_to_all | solution.py:111
  78.5 0.3 reshape.329
  78.7 0.3 copy.104
  79.1 0.5 convolution_bitcast_fusion.3
  79.6 0.1 copy.105
  79.7 2.3 %fusion.126 = f32[256,4096]{1,0:T(8,128)S(1)} fusion(bf16[256,256]{1,0:T(8,128)(2,1)S(1)} %get-tuple-element.79, bf16[256,4096]{1,0:T(8,128)(2,1)} %copy-done.1), kind=kOutput, calls=%fused_computation.185 | convolution fusion | flops 536870912 | bytes 6422528 | tf_op jit(solution)/shard_map/dot_general | solution.py:63
  82.1 0.8 convolution_add_fusion.1
  82.9 0.8 copy-done.8
  83.7 4.4 %convert_reduce_fusion = (f32[32]{0:T(128)S(1)}, bf16[8,1,32,4096]{3,2,0,1:T(8,128)(2,1)S(1)}, f32[8,32,4096]{2,1,0:T(8,128)}) fusion(bf16[8,1,32,4096]{3,2,1,0:T(8,128)(2,1)S(1)} %copy-done.8, f32[32]{0:T(128)S(1)} %copy-done.9, f32[8,32,4096]{2,1,0:T(8,128)S(1)} %bitcast.139, bf16[32,32]{1,0:T(8,128)(2,1)S(1)} %copy-done.7, ...), kind=kOutput, calls=%fused_computation.23 | convolution fusion | flops 82837472 | bytes 14682368 | tf_op jit(solution)/shard_map/io,riy->roy/dot_general | solution.py:138
  88.1 0.9 convolution_bitcast_fusion.4
  89.0 1.5 fusion.15
  90.5 0.5 fusion.62
  91.0 0.4 copy.110
  91.4 0.3 reshape.332
  91.9 24.2 %all_to_all.57 = f32[64,16,128]{2,1,0:T(8,128)S(1)} all-to-all(f32[64,16,128]{2,1,0:T(8,128)S(1)} %select_maximum_fusion), channel_id=1, replica_groups=mesh['sp'=64,'ch'=4] {'sp'}, dimensions={0} | all-to-all | bytes 1048576 | tf_op jit(solution)/shard_map/all_to_all | solution.py:80
  116.1 0.3 fusion.31
  116.7 6.7 %all_to_all.58 = f32[17,8,128]{2,0,1:T(8,128)S(1)} all-to-all(f32[17,8,128]{2,0,1:T(8,128)S(1)} %pad_maximum_fusion.1), channel_id=1, replica_groups=mesh['sp'=64,'ch'=4] {'ch'}, dimensions={1} | all-to-all | bytes 139264 | tf_op jit(solution)/shard_map/all_to_all | solution.py:89
  123.4 0.1 reshape.354
  123.5 3.0 %fusion.127 = f32[16,8,1,32]{3,2,1,0:T(1,128)S(1)} fusion(f32[16,8,32,1]{2,3,1,0:T(1,128)S(1)} %bitcast.155, bf16[16,8,32,32]{3,2,1,0:T(8,128)(2,1)} %copy-done.6), kind=kOutput, calls=%fused_computation.186 | convolution fusion | flops 1572864 | bytes 294912 | tf_op jit(solution)/shard_map/kqio,kqo->kqi/dot_general | solution.py:156
  126.5 0.1 reshape.338
  126.6 0.7 broadcast_in_dim.80
  127.2 3.3 %all-to-all-start.6 = ((f32[17,4,2,128]{3,2,0,1:T(2,128)}), f32[17,4,2,128]{3,2,0,1:T(2,128)S(1)}, u32[]{:S(2)}, u32[]{:S(2)}) async-start(f32[17,4,2,128]{3,2,0,1:T(2,128)} %broadcast_in_dim.80), calls=%async_computation.6 | async-start | bytes 139264 | tf_op jit(solution)/shard_map/all_to_all | solution.py:106
  130.5 0.1 reshape.326
  130.6 4.0 %all-to-all-done.6 = f32[17,4,2,128]{3,2,0,1:T(2,128)S(1)} async-done(((f32[17,4,2,128]{3,2,0,1:T(2,128)}), f32[17,4,2,128]{3,2,0,1:T(2,128)S(1)}, u32[]{:S(2)}, u32[]{:S(2)}) %all-to-all-start.6) | async-done | bytes 69664 | tf_op jit(solution)/shard_map/all_to_all | solution.py:106
  134.7 0.5 fusion.48
  135.3 1.1 copy.118
  136.4 6.9 %all-to-all-start.7 = ((f32[64,16,128]{2,1,0:T(8,128)}), f32[64,16,128]{2,1,0:T(8,128)S(1)}, u32[]{:S(2)}, u32[]{:S(2)}) async-start(f32[64,16,128]{2,1,0:T(8,128)} %copy.118), calls=%async_computation.7 | async-start | bytes 1048576 | tf_op jit(solution)/shard_map/all_to_all | solution.py:111
  143.3 3.6 %fusion.14 = bf16[8,1,32,4096]{3,2,1,0:T(8,128)(2,1)} fusion(f32[8,32,4096]{2,1,0:T(8,128)} %get-tuple-element.82), kind=kLoop, calls=%fused_computation.26 | loop fusion | flops 5242880 | bytes 6291456
  146.9 0.1 reshape.337
  147.0 1.8 %multiply_multiply_fusion.1 = f32[16,8,32,32]{3,2,1,0:T(8,128)} fusion(f32[16,8,32]{2,1,0:T(8,128)S(1)} %reshape.337, f32[16,8,32]{2,1,0:T(8,128)S(1)} %reshape.326), kind=kLoop, calls=%fused_computation.33 | loop fusion | flops 262144 | bytes 557056 | tf_op jit(solution)/shard_map/mul | solution.py:153
  148.8 3.1 %reshape.342 = f32[16,8,1024]{2,1,0:T(8,128)} reshape(f32[16,8,32,32]{3,2,1,0:T(8,128)} %multiply_multiply_fusion.1) | data formatting | bytes 1048576 | tf_op jit(solution)/shard_map/reshape | solution.py:153
  151.9 9.5 %all-to-all-done.7 = f32[64,16,128]{2,1,0:T(8,128)S(1)} async-done(((f32[64,16,128]{2,1,0:T(8,128)}), f32[64,16,128]{2,1,0:T(8,128)S(1)}, u32[]{:S(2)}, u32[]{:S(2)}) %all-to-all-start.7) | async-done | bytes 524320 | tf_op jit(solution)/shard_map/all_to_all | solution.py:111
  161.5 0.3 reshape.339
  161.8 0.3 copy.119
  162.1 0.5 convolution_bitcast_fusion.2
  162.6 0.1 copy.120
  162.8 2.3 %fusion.128 = f32[256,4096]{1,0:T(8,128)S(1)} fusion(bf16[256,256]{1,0:T(8,128)(2,1)S(1)} %get-tuple-element.77, bf16[256,4096]{1,0:T(8,128)(2,1)} %copy-done.1), kind=kOutput, calls=%fused_computation.187 | convolution fusion | flops 536870912 | bytes 6422528 | tf_op jit(solution)/shard_map/dot_general | solution.py:63
  165.1 0.7 convolution_add_fusion
  165.8 0.9 copy-done.5
  166.7 2.0 %fusion.6 = bf16[8,1,32,4096]{3,2,1,0:T(8,128)(2,1)} fusion(f32[8,32,4096]{2,1,0:T(8,128)S(1)} %bitcast.137, bf16[32,32]{1,0:T(8,128)(2,1)S(1)} %copy-done.7, bf16[8,1,32,4096]{3,2,0,1:T(8,128)(2,1)S(1)} %copy-done.5), kind=kOutput, calls=%fused_computation.15 | convolution fusion | flops 69206016 | bytes 8390656 | tf_op jit(solution)/shard_map/io,roy->riy/dot_general | solution.py:163
  168.8 0.7 copy.125
  169.5 0.6 mul.246
  (59 shorter events, 1.0 us)
Async XLA Ops:
  0.6 11.9 %copy-start = (bf16[8,1,32,4096]{3,2,1,0:T(8,128)(2,1)S(1)}, bf16[8,1,32,4096]{3,2,1,0:T(8,128)(2,1)}, u32[]{:S(2)}) copy-start(bf16[8,1,32,4096]{3,2,1,0:T(8,128)(2,1)} %param.11) | copy-start | bytes 6291460
  12.6 1.5 copy-start.1
  43.6 7.4 %all-to-all-start.1 = ((f32[16,8,128]{2,0,1:T(8,128)}), f32[16,8,128]{2,0,1:T(8,128)S(1)}, u32[]{:S(2)}, u32[]{:S(2)}) async-start(f32[16,8,128]{2,0,1:T(8,128)} %fusion.33), calls=%async_computation.1 | async-start | bytes 131072 | tf_op jit(solution)/shard_map/all_to_all | solution.py:89
  48.8 10.6 %copy-start.6 = (bf16[16,8,32,32]{3,2,1,0:T(8,128)(2,1)}, bf16[16,8,32,32]{3,2,1,0:T(8,128)(2,1)S(1)}, u32[]{:S(2)}) copy-start(bf16[16,8,32,32]{3,2,1,0:T(8,128)(2,1)S(1)} %reshape.327) | copy-start | bytes 786436
  79.1 3.0 %copy-start.2 = (bf16[256,4096]{1,0:T(8,128)(2,1)S(1)}, bf16[256,4096]{1,0:T(8,128)(2,1)}, u32[]{:S(2)}) copy-start(bf16[256,4096]{1,0:T(8,128)(2,1)} %copy-done.1) | copy-start | bytes 6291460
  82.1 0.8 copy-start.7
  82.1 1.6 copy-start.8
  82.1 1.6 copy-start.9
  88.1 2.4 %copy-start.4 = (bf16[8,1,32,4096]{3,2,0,1:T(8,128)(2,1)}, bf16[8,1,32,4096]{3,2,0,1:T(8,128)(2,1)S(1)}, u32[]{:S(2)}) copy-start(bf16[8,1,32,4096]{3,2,0,1:T(8,128)(2,1)S(1)} %get-tuple-element.73) | copy-start | bytes 6291460
  127.2 7.4 %all-to-all-start.6 = ((f32[17,4,2,128]{3,2,0,1:T(2,128)}), f32[17,4,2,128]{3,2,0,1:T(2,128)S(1)}, u32[]{:S(2)}, u32[]{:S(2)}) async-start(f32[17,4,2,128]{3,2,0,1:T(2,128)} %broadcast_in_dim.80), calls=%async_computation.6 | async-start | bytes 139264 | tf_op jit(solution)/shard_map/all_to_all | solution.py:106
  136.4 25.0 %all-to-all-start.7 = ((f32[64,16,128]{2,1,0:T(8,128)}), f32[64,16,128]{2,1,0:T(8,128)S(1)}, u32[]{:S(2)}, u32[]{:S(2)}) async-start(f32[64,16,128]{2,1,0:T(8,128)} %copy.118), calls=%async_computation.7 | async-start | bytes 1048576 | tf_op jit(solution)/shard_map/all_to_all | solution.py:111
  162.1 3.0 %copy-start.3 = (bf16[256,4096]{1,0:T(8,128)(2,1)S(1)}, bf16[256,4096]{1,0:T(8,128)(2,1)}, u32[]{:S(2)}) copy-start(bf16[256,4096]{1,0:T(8,128)(2,1)} %copy-done.1) | copy-start | bytes 6291460
  165.1 1.6 copy-start.5

commit v3 on v2

--- a/solution.py
+++ b/solution.py
@@ -65,9 +65,21 @@
     )
 
 
+def sp_size():
+    return lax.axis_size("sa") * lax.axis_size("sb")
+
+
+def sp_all_to_all(send):
+    outer, inner = lax.axis_size("sa"), lax.axis_size("sb")
+    blocks = send.reshape((outer, inner) + send.shape[1:])
+    blocks = lax.all_to_all(blocks, "sb", 1, 1, tiled=True)
+    blocks = lax.all_to_all(blocks, "sa", 0, 0, tiled=True)
+    return blocks.reshape(send.shape)
+
+
 def to_spectrum(values, yz_table, time_table, x_table, extra=None):
     steps_here, planes, channels, plane_cells = values.shape
-    sp_count = lax.axis_size("sp")
+    sp_count = sp_size()
     flat = jnp.einsum(
         "qc,rc->qr", yz_table, values.reshape(-1, plane_cells), preferred_element_type=jnp.float32
     ).reshape(KYZ, steps_here, channels)
@@ -77,7 +89,7 @@
         rider = jnp.zeros((sp_count, SUB, LANES), jnp.float32)
         rider = rider.at[:, 0, : Q // sp_count].set(extra.reshape(sp_count, -1))
         send = jnp.concatenate([send, rider], axis=1)
-    arrived = lax.all_to_all(send, "sp", 0, 0, tiled=True)
+    arrived = sp_all_to_all(send)
     modes = jnp.einsum("kx,xrl->krl", x_table, arrived[:, :SUB], precision=PRECISE)
     if extra is not None:
         rider_sum = jnp.sum(arrived[:, SUB, : Q // sp_count], axis=0)
@@ -96,7 +108,7 @@
 
 def to_planes(block, x_table, time_table, yz_table, steps_here, extra=None):
     channels = block.shape[2]
-    sp_count = lax.axis_size("sp")
+    sp_count = sp_size()
     ch_count = lax.axis_size("ch")
     rows = block.reshape(KX, SUB // ch_count, LANES)
     if extra is not None:
@@ -108,7 +120,7 @@
     if extra is not None:
         rider = jnp.broadcast_to(gathered[KX][None], (sp_count, SUB, LANES))
         spread = jnp.concatenate([spread, rider], axis=1)
-    returned = lax.all_to_all(spread, "sp", 0, 0, tiled=True)
+    returned = sp_all_to_all(spread)
     total = None
     if extra is not None:
         pieces = returned[:, SUB:].reshape(sp_count, ch_count, SUB // ch_count, LANES)
@@ -121,7 +133,7 @@
 
 def shards(field, spectral_weight, point_weight, bias, cotangent):
     steps_here, planes, channels, plane_cells = field.shape
-    sp_count = lax.axis_size("sp")
+    sp_count = sp_size()
     grid_x = planes * sp_count
     forward_x = wave_table(grid_x, KX, jnp.arange(grid_x, dtype=jnp.int32))
     inverse_x = forward_x * math.sqrt(grid_x / KX)
@@ -168,20 +180,26 @@
 
 
 def solution(mesh):
+    sp_count, ch_count = mesh.devices.shape
+    inner = 8 if sp_count % 8 == 0 else 1
+    split_mesh = jax.sharding.Mesh(
+        mesh.devices.reshape(sp_count // inner, inner, ch_count), ("sa", "sb", "ch")
+    )
+    sp = ("sa", "sb")
     return jax.shard_map(
         shards,
-        mesh=mesh,
+        mesh=split_mesh,
         in_specs=(
-            P("ch", "sp", None, None),
-            P(None, ("sp", "ch"), None),
-            P(),
-            P(),
-            P("ch", "sp", None, None),
+            P("ch", sp, None, None),
+            P(None, sp + ("ch",), None),
+            P(),
+            P(),
+            P("ch", sp, None, None),
         ),
         out_specs=(
-            P("ch", "sp", None, None),
-            P("ch", "sp", None, None),
-            P(None, ("sp", "ch"), None),
+            P("ch", sp, None, None),
+            P("ch", sp, None, None),
+            P(None, sp + ("ch",), None),
             P(),
             P(),
         ),

time: 171 us -> 221 us (1.29)
  blocking collectives: 83.8 us -> 117 us
  waiting for transfers between devices: 15.8 us -> 27.6 us
  starting transfers between devices: 13.5 us -> 17.5 us
    all_to_all x3 -> x6, blocking collectives: 70.6 us -> 104 us  [the longest x3 52.3 us: sp_all_to_all(): blocks = lax.all_to_all(blocks, 'sa', 0, 0, tiled=True)]
    all_to_all x1 -> x2, waiting for transfers between devices: 9.52 us -> 21.3 us  [the longest x1 14.2 us: sp_all_to_all(): blocks = lax.all_to_all(blocks, 'sb', 1, 1, tiled=True)]
    all_to_all x1 -> x2, starting transfers between devices: 6.89 us -> 11 us  [the longest x1 6.74 us: sp_all_to_all(): blocks = lax.all_to_all(blocks, 'sa', 0, 0, tiled=True)]
  transfers between devices with their start and end apart: 3 -> 4, of which waited for: 3 -> 4; matrix products, arithmetic and copies ran while one was open for 6% -> 5% of each run, Pallas kernels for 0% -> 0%
where the time goes in v3:
time: 221 us; the launch traced here: 219 us
  blocking collectives  117 us (53%)
  matrix products  35.2 us (16%)
  waiting for transfers between devices  27.6 us (12%)
  starting transfers between devices  17.5 us (8%)
  local copies, waits for them, and re-layouts  14.9 us (7%)
  other arithmetic  5.79 us (3%)
    all_to_all x3, blocking collectives, sp_all_to_all(): blocks = lax.all_to_all(blocks, 'sa', 0, 0, tiled=True)  52.3 us
    all_to_all x3, blocking collectives, sp_all_to_all(): blocks = lax.all_to_all(blocks, 'sb', 1, 1, tiled=True)  51.3 us
    all_to_all x1, waiting for transfers between devices, sp_all_to_all(): blocks = lax.all_to_all(blocks, 'sb', 1, 1, tiled=True)  14.2 us
    dot_general x6, matrix products, exact_spread(): jnp.dot(piece.astype(jnp.bfloat16), selector, preferred_element_type=jnp....  11.6 us
    all_to_all x1, waiting for transfers between devices, sp_all_to_all(): blocks = lax.all_to_all(blocks, 'sa', 0, 0, tiled=True)  7.11 us
    all_to_all x1, starting transfers between devices, sp_all_to_all(): blocks = lax.all_to_all(blocks, 'sa', 0, 0, tiled=True)  6.74 us
    all_to_all x1, blocking collectives, to_spectrum(): parts = lax.all_to_all(modes, 'ch', 1, 0, tiled=True)  6.67 us
    all_to_all x1, blocking collectives, to_planes(): lax.all_to_all(copies, 'ch', 1, 1, tiled=True)  6.51 us
  transfers between devices with their start and end apart: 4, of which 4 were waited for; matrix products, arithmetic and copies ran while one was open for 5% of the time, Pallas kernels for 0%

profile of v3, /device:TPU:8, one launch (start us, length us, event | category | flops | bytes accessed | tf_op | source)
XLA Modules:
  0.0 219.1 jit_solution(7110127049615025241)
XLA Ops:
  0.7 0.1 broadcast_multiply_fusion
  0.9 0.7 fusion.22
  1.6 0.7 convolution_add_fusion.5
  2.3 2.7 %convolution_add_fusion.4 = f32[256,4096]{1,0:T(8,128)} fusion(f32[256,4096]{1,0:T(8,128)S(1)} %convolution_add_fusion.5, s32[4096]{0:T(1024)S(1)} %get-tuple-element.86, f32[256,64]{1,0:T(8,128)S(1)} %bitcast.160), kind=kOutput, calls=%fused_computation.10 | convolution fusion | flops 135626752 | bytes 8470528 | tf_op jit(solution)/shard_map/dot_general | solution.py:42
  5.0 0.7 fusion.21
  5.7 2.7 %convolution_add_fusion.3 = f32[256,4096]{1,0:T(8,128)} fusion(f32[256,4096]{1,0:T(8,128)S(1)} %fusion.21, s32[4096]{0:T(1024)S(1)} %get-tuple-element.85, f32[256,64]{1,0:T(8,128)S(1)} %bitcast.162), kind=kOutput, calls=%fused_computation.9 | convolution fusion | flops 135593984 | bytes 8470528 | tf_op jit(solution)/shard_map/dot_general | solution.py:42
  8.4 4.2 %fusion.4 = bf16[256,4096]{1,0:T(8,128)(2,1)S(1)} fusion(f32[256,4096]{1,0:T(8,128)} %convolution_add_fusion.4, f32[256,4096]{1,0:T(8,128)} %convolution_add_fusion.3, s32[4096]{0:T(1024)S(1)} %get-tuple-element.85, f32[256,64]{1,0:T(8,128)S(1)} %bitcast.163), kind=kOutput, calls=%fused_computation.13 | convolution fusion | flops 137723904 | bytes 10567680 | tf_op jit(solution)/shard_map/dot_general | solution.py:42
  12.6 1.5 fusion.17
  14.1 0.5 fusion.85
  14.6 0.4 copy.145
  15.0 0.3 reshape_reshape.6
  15.3 18.6 %all_to_all.74 = f32[8,8,8,128]{3,2,0,1:T(8,128)S(1)} all-to-all(f32[8,8,8,128]{3,2,0,1:T(8,128)S(1)} %copy.146), channel_id=1, replica_groups=mesh['sa'=8,'sb'=8,'ch'=4] {'sb'}, dimensions={1} | all-to-all | bytes 524288 | tf_op jit(solution)/shard_map/all_to_all | solution.py:75
  33.9 18.3 %all_to_all.75 = f32[8,8,8,128]{3,2,1,0:T(8,128)S(1)} all-to-all(f32[8,8,8,128]{3,2,1,0:T(8,128)S(1)} %copy.147), channel_id=1, replica_groups=mesh['sa'=8,'sb'=8,'ch'=4] {'sa'}, dimensions={0} | all-to-all | bytes 524288 | tf_op jit(solution)/shard_map/all_to_all | solution.py:76
  52.2 1.0 fusion.33
  53.1 3.3 %all-to-all-start.2 = ((f32[16,8,128]{2,0,1:T(8,128)}), f32[16,8,128]{2,0,1:T(8,128)S(1)}, u32[]{:S(2)}, u32[]{:S(2)}) async-start(f32[16,8,128]{2,0,1:T(8,128)} %fusion.33), calls=%async_computation.2 | async-start | bytes 131072 | tf_op jit(solution)/shard_map/all_to_all | solution.py:101
  56.4 1.8 reshape.374
  58.3 2.2 %all-to-all-done.2 = f32[16,8,128]{2,0,1:T(8,128)S(1)} async-done(((f32[16,8,128]{2,0,1:T(8,128)}), f32[16,8,128]{2,0,1:T(8,128)S(1)}, u32[]{:S(2)}, u32[]{:S(2)}) %all-to-all-start.2) | async-done | bytes 65568 | tf_op jit(solution)/shard_map/all_to_all | solution.py:101
  60.6 0.9 fusion.143
  61.7 0.6 broadcast_in_dim.80
  62.3 3.3 %all-to-all-start.3 = ((f32[16,4,2,128]{3,0,2,1:T(8,128)}), f32[16,4,2,128]{3,0,2,1:T(8,128)S(1)}, u32[]{:S(2)}, u32[]{:S(2)}) async-start(f32[16,4,2,128]{3,0,2,1:T(8,128)} %broadcast_in_dim.80), calls=%async_computation.3 | async-start | bytes 131072 | tf_op jit(solution)/shard_map/all_to_all | solution.py:118
  65.6 4.1 %all-to-all-done.3 = f32[16,4,2,128]{3,0,2,1:T(8,128)S(1)} async-done(((f32[16,4,2,128]{3,0,2,1:T(8,128)}), f32[16,4,2,128]{3,0,2,1:T(8,128)S(1)}, u32[]{:S(2)}, u32[]{:S(2)}) %all-to-all-start.3) | async-done | bytes 65568 | tf_op jit(solution)/shard_map/all_to_all | solution.py:118
  69.7 0.6 fusion.45
  70.3 14.4 %all_to_all.76 = f32[8,8,8,128]{3,2,0,1:T(8,128)S(1)} all-to-all(f32[8,8,8,128]{3,2,0,1:T(8,128)S(1)} %copy.151), channel_id=1, replica_groups=mesh['sa'=8,'sb'=8,'ch'=4] {'sb'}, dimensions={1} | all-to-all | bytes 524288 | tf_op jit(solution)/shard_map/all_to_all | solution.py:75
  84.7 14.3 %all_to_all.77 = f32[8,8,8,128]{3,2,1,0:T(8,128)S(1)} all-to-all(f32[8,8,8,128]{3,2,1,0:T(8,128)S(1)} %copy.152), channel_id=1, replica_groups=mesh['sa'=8,'sb'=8,'ch'=4] {'sa'}, dimensions={0} | all-to-all | bytes 524288 | tf_op jit(solution)/shard_map/all_to_all | solution.py:76
  99.0 0.3 reshape_reshape.7
  99.2 0.3 copy.153
  99.6 0.5 convolution_bitcast_fusion.3
  100.2 2.3 %fusion.144 = f32[256,4096]{1,0:T(8,128)S(1)} fusion(bf16[256,256]{1,0:T(8,128)(2,1)S(1)} %get-tuple-element.84, bf16[256,4096]{1,0:T(8,128)(2,1)} %copy-done.1), kind=kOutput, calls=%fused_computation.209 | convolution fusion | flops 536870912 | bytes 6422528 | tf_op jit(solution)/shard_map/dot_general | solution.py:63
  102.6 0.8 convolution_add_fusion.1
  103.4 0.8 copy-done.9
  104.2 4.5 %convert_reduce_fusion = (f32[32]{0:T(128)S(1)}, bf16[8,1,32,4096]{3,2,0,1:T(8,128)(2,1)S(1)}, f32[8,32,4096]{2,1,0:T(8,128)}) fusion(bf16[8,1,32,4096]{3,2,1,0:T(8,128)(2,1)S(1)} %copy-done.9, f32[32]{0:T(128)S(1)} %copy-done.10, f32[8,32,4096]{2,1,0:T(8,128)S(1)} %bitcast.157, bf16[32,32]{1,0:T(8,128)(2,1)S(1)} %copy-done.8, ...), kind=kOutput, calls=%fused_computation.23 | convolution fusion | flops 82837472 | bytes 14682368 | tf_op jit(solution)/shard_map/io,riy->roy/dot_general | solution.py:150
  108.6 0.9 convolution_bitcast_fusion.4
  109.5 1.5 fusion.15
  111.0 0.5 fusion.81
  111.6 0.4 copy.159
  111.9 0.3 concatenate.26
  112.6 18.4 %all_to_all.78 = f32[8,8,16,128]{3,2,0,1:T(8,128)S(1)} all-to-all(f32[8,8,16,128]{3,2,0,1:T(8,128)S(1)} %copy.162), channel_id=1, replica_groups=mesh['sa'=8,'sb'=8,'ch'=4] {'sb'}, dimensions={1} | all-to-all | bytes 1048576 | tf_op jit(solution)/shard_map/all_to_all | solution.py:75
  131.0 19.8 %all_to_all.79 = f32[8,8,16,128]{3,2,1,0:T(8,128)S(1)} all-to-all(f32[8,8,16,128]{3,2,1,0:T(8,128)S(1)} %copy.163), channel_id=1, replica_groups=mesh['sa'=8,'sb'=8,'ch'=4] {'sa'}, dimensions={0} | all-to-all | bytes 1048576 | tf_op jit(solution)/shard_map/all_to_all | solution.py:76
  150.8 0.2 copy.204
  151.0 0.3 fusion.31
  151.5 6.7 %all_to_all.80 = f32[17,8,128]{2,0,1:T(8,128)S(1)} all-to-all(f32[17,8,128]{2,0,1:T(8,128)S(1)} %pad_maximum_fusion.1), channel_id=1, replica_groups=mesh['sa'=8,'sb'=8,'ch'=4] {'ch'}, dimensions={1} | all-to-all | bytes 139264 | tf_op jit(solution)/shard_map/all_to_all | solution.py:101
  158.3 1.7 fusion.145
  160.0 0.1 reshape.384
  160.2 6.5 %all_to_all.81 = f32[17,4,2,128]{3,2,0,1:T(2,128)S(1)} all-to-all(f32[17,4,2,128]{3,2,0,1:T(2,128)S(1)} %broadcast_in_dim.81), channel_id=1, replica_groups=mesh['sa'=8,'sb'=8,'ch'=4] {'ch'}, dimensions={1} | all-to-all | bytes 139264 | tf_op jit(solution)/shard_map/all_to_all | solution.py:118
  166.7 0.5 fusion.71
  167.3 0.9 copy.169
  168.2 4.2 %all-to-all-start.10 = ((f32[8,8,16,128]{3,0,2,1:T(8,128)}), f32[8,8,16,128]{3,0,2,1:T(8,128)S(1)}, u32[]{:S(2)}, u32[]{:S(2)}) async-start(f32[8,8,16,128]{3,0,2,1:T(8,128)} %copy.169), calls=%async_computation.10 | async-start | bytes 1048576 | tf_op jit(solution)/shard_map/all_to_all | solution.py:75
  172.6 14.2 %all-to-all-done.10 = f32[8,8,16,128]{3,0,2,1:T(8,128)S(1)} async-done(((f32[8,8,16,128]{3,0,2,1:T(8,128)}), f32[8,8,16,128]{3,0,2,1:T(8,128)S(1)}, u32[]{:S(2)}, u32[]{:S(2)}) %all-to-all-start.10) | async-done | bytes 524320 | tf_op jit(solution)/shard_map/all_to_all | solution.py:75
  186.8 1.1 copy.170
  187.9 6.7 %all-to-all-start.11 = ((f32[8,8,16,128]{3,1,2,0:T(8,128)}), f32[8,8,16,128]{3,1,2,0:T(8,128)S(1)}, u32[]{:S(2)}, u32[]{:S(2)}) async-start(f32[8,8,16,128]{3,1,2,0:T(8,128)} %copy.170), calls=%async_computation.11 | async-start | bytes 1048576 | tf_op jit(solution)/shard_map/all_to_all | solution.py:76
  194.6 3.6 %fusion.14 = bf16[8,1,32,4096]{3,2,1,0:T(8,128)(2,1)} fusion(f32[8,32,4096]{2,1,0:T(8,128)} %get-tuple-element.87), kind=kLoop, calls=%fused_computation.26 | loop fusion | flops 5242880 | bytes 6291456
  198.3 1.8 multiply_multiply_fusion.1
  200.1 3.1 %reshape.390 = f32[16,8,1024]{2,1,0:T(8,128)} reshape(f32[16,8,32,32]{3,2,1,0:T(8,128)} %multiply_multiply_fusion.1) | data formatting | bytes 1048576 | tf_op jit(solution)/shard_map/reshape | solution.py:165
  203.1 7.1 %all-to-all-done.11 = f32[8,8,16,128]{3,1,2,0:T(8,128)S(1)} async-done(((f32[8,8,16,128]{3,1,2,0:T(8,128)}), f32[8,8,16,128]{3,1,2,0:T(8,128)S(1)}, u32[]{:S(2)}, u32[]{:S(2)}) %all-to-all-start.11) | async-done | bytes 524320 | tf_op jit(solution)/shard_map/all_to_all | solution.py:76
  210.4 0.2 copy.172
  210.6 0.3 reshape.387
  210.8 0.3 copy.173
  211.2 0.5 convolution_bitcast_fusion.2
  211.8 2.3 %fusion.146 = f32[256,4096]{1,0:T(8,128)S(1)} fusion(bf16[256,256]{1,0:T(8,128)(2,1)S(1)} %get-tuple-element.82, bf16[256,4096]{1,0:T(8,128)(2,1)} %copy-done.1), kind=kOutput, calls=%fused_computation.211 | convolution fusion | flops 536870912 | bytes 6422528 | tf_op jit(solution)/shard_map/dot_general | solution.py:63
  214.2 0.7 convolution_add_fusion
  214.9 0.9 copy-done.5
  215.7 2.0 fusion.6
  217.8 0.7 copy.178
  218.5 0.6 mul.287
  (75 shorter events, 1.8 us)
Async XLA Ops:
  0.6 11.9 %copy-start = (bf16[8,1,32,4096]{3,2,1,0:T(8,128)(2,1)S(1)}, bf16[8,1,32,4096]{3,2,1,0:T(8,128)(2,1)}, u32[]{:S(2)}) copy-start(bf16[8,1,32,4096]{3,2,1,0:T(8,128)(2,1)} %param.11) | copy-start | bytes 6291460
  12.6 1.5 copy-start.1
  53.1 7.4 %all-to-all-start.2 = ((f32[16,8,128]{2,0,1:T(8,128)}), f32[16,8,128]{2,0,1:T(8,128)S(1)}, u32[]{:S(2)}, u32[]{:S(2)}) async-start(f32[16,8,128]{2,0,1:T(8,128)} %fusion.33), calls=%async_computation.2 | async-start | bytes 131072 | tf_op jit(solution)/shard_map/all_to_all | solution.py:101
  58.3 26.4 %copy-start.6 = (bf16[16,8,32,32]{3,2,1,0:T(8,128)(2,1)}, bf16[16,8,32,32]{3,2,1,0:T(8,128)(2,1)S(1)}, u32[]{:S(2)}) copy-start(bf16[16,8,32,32]{3,2,1,0:T(8,128)(2,1)S(1)} %reshape.374) | copy-start | bytes 786436
  62.3 7.4 %all-to-all-start.3 = ((f32[16,4,2,128]{3,0,2,1:T(8,128)}), f32[16,4,2,128]{3,0,2,1:T(8,128)S(1)}, u32[]{:S(2)}, u32[]{:S(2)}) async-start(f32[16,4,2,128]{3,0,2,1:T(8,128)} %broadcast_in_dim.80), calls=%async_computation.3 | async-start | bytes 131072 | tf_op jit(solution)/shard_map/all_to_all | solution.py:118
  99.6 3.0 %copy-start.2 = (bf16[256,4096]{1,0:T(8,128)(2,1)S(1)}, bf16[256,4096]{1,0:T(8,128)(2,1)}, u32[]{:S(2)}) copy-start(bf16[256,4096]{1,0:T(8,128)(2,1)} %copy-done.1) | copy-start | bytes 6291460
  102.6 0.8 copy-start.8
  102.6 1.6 copy-start.9
  102.6 1.6 copy-start.10
  108.6 2.4 %copy-start.4 = (bf16[8,1,32,4096]{3,2,0,1:T(8,128)(2,1)}, bf16[8,1,32,4096]{3,2,0,1:T(8,128)(2,1)S(1)}, u32[]{:S(2)}) copy-start(bf16[8,1,32,4096]{3,2,0,1:T(8,128)(2,1)S(1)} %get-tuple-element.78) | copy-start | bytes 6291460
  112.2 46.1 %copy-start.7 = (bf16[16,8,32,32]{3,2,1,0:T(8,128)(2,1)S(1)}, bf16[16,8,32,32]{3,2,1,0:T(8,128)(2,1)}, u32[]{:S(2)}) copy-start(bf16[16,8,32,32]{3,2,1,0:T(8,128)(2,1)} %copy-done.6) | copy-start | bytes 786436
  168.2 18.5 %all-to-all-start.10 = ((f32[8,8,16,128]{3,0,2,1:T(8,128)}), f32[8,8,16,128]{3,0,2,1:T(8,128)S(1)}, u32[]{:S(2)}, u32[]{:S(2)}) async-start(f32[8,8,16,128]{3,0,2,1:T(8,128)} %copy.169), calls=%async_computation.10 | async-start | bytes 1048576 | tf_op jit(solution)/shard_map/all_to_all | solution.py:75
  187.9 22.4 %all-to-all-start.11 = ((f32[8,8,16,128]{3,1,2,0:T(8,128)}), f32[8,8,16,128]{3,1,2,0:T(8,128)S(1)}, u32[]{:S(2)}, u32[]{:S(2)}) async-start(f32[8,8,16,128]{3,1,2,0:T(8,128)} %copy.170), calls=%async_computation.11 | async-start | bytes 1048576 | tf_op jit(solution)/shard_map/all_to_all | solution.py:76
  211.2 3.0 %copy-start.3 = (bf16[256,4096]{1,0:T(8,128)(2,1)S(1)}, bf16[256,4096]{1,0:T(8,128)(2,1)}, u32[]{:S(2)}) copy-start(bf16[256,4096]{1,0:T(8,128)(2,1)} %copy-done.1) | copy-start | bytes 6291460
  214.2 1.6 copy-start.5

commit v4 on v1

--- a/solution.py
+++ b/solution.py
@@ -67,51 +67,61 @@
 
 def to_spectrum(values, yz_table, time_table, x_table, extra=None):
     steps_here, planes, channels, plane_cells = values.shape
-    sp_count = lax.axis_size("sp")
+    sp_count, ch_count = lax.axis_size("sp"), lax.axis_size("ch")
+    own = Q // (sp_count * ch_count)
+    blocks = KYZ // (ch_count * own)
+    rows_per = own * channels // LANES
     flat = jnp.einsum(
         "qc,rc->qr", yz_table, values.reshape(-1, plane_cells), preferred_element_type=jnp.float32
-    ).reshape(KYZ, steps_here, channels)
-    partial = jnp.einsum("kt,ptc->kpc", time_table, flat, precision=PRECISE)
-    send = partial.reshape(sp_count, SUB, LANES)
+    ).reshape(blocks, ch_count, own, steps_here, channels)
+    partial = jnp.einsum("kt,bmqtc->mkbqc", time_table, flat, precision=PRECISE)
+    send = partial.reshape(ch_count, sp_count * rows_per, LANES)
     if extra is not None:
-        rider = jnp.zeros((sp_count, SUB, LANES), jnp.float32)
-        rider = rider.at[:, 0, : Q // sp_count].set(extra.reshape(sp_count, -1))
+        rider = extra.reshape(sp_count, ch_count, own).transpose(1, 0, 2)
+        rider = rider.reshape(ch_count, -1, LANES)
+        rider = jnp.pad(rider, ((0, 0), (0, SUB - rider.shape[1]), (0, 0)))
         send = jnp.concatenate([send, rider], axis=1)
-    arrived = lax.all_to_all(send, "sp", 0, 0, tiled=True)
-    modes = jnp.einsum("kx,xrl->krl", x_table, arrived[:, :SUB], precision=PRECISE)
+    summed = jnp.sum(lax.all_to_all(send, "ch", 0, 0, tiled=True), axis=0)
+    data = summed[: sp_count * rows_per].reshape(sp_count, rows_per, LANES)
     if extra is not None:
-        rider_sum = jnp.sum(arrived[:, SUB, : Q // sp_count], axis=0)
-        ch_count = lax.axis_size("ch")
-        row = jnp.zeros((ch_count, SUB // ch_count, LANES), jnp.float32)
-        row = row.at[:, 0, : rider_sum.shape[0] // ch_count].set(rider_sum.reshape(ch_count, -1))
-        modes = jnp.concatenate([modes, row.reshape(1, SUB, LANES)], axis=0)
-    scattered = lax.psum_scatter(modes, "ch", scatter_dimension=1, tiled=True)
-    owned = scattered[:KX].reshape(KX, -1, channels)
+        pieces = summed[sp_count * rows_per :].reshape(-1)[: sp_count * own].reshape(sp_count, own)
+        rider = jnp.zeros((sp_count, 1, LANES), jnp.float32).at[:, 0, :own].set(pieces)
+        data = jnp.concatenate([data, rider], axis=1)
+    arrived = lax.all_to_all(data, "sp", 0, 0, tiled=True)
+    owned = jnp.einsum("kx,xrl->krl", x_table, arrived[:, :rows_per], precision=PRECISE)
+    owned = owned.reshape(KX, own, channels)
     if extra is None:
         return owned
-    return owned, scattered[KX, 0, : Q // (sp_count * lax.axis_size("ch"))]
+    return owned, jnp.sum(arrived[:, rows_per, :own], axis=0)
 
 
 def to_planes(block, x_table, time_table, yz_table, steps_here, extra=None):
     channels = block.shape[2]
-    sp_count = lax.axis_size("sp")
-    ch_count = lax.axis_size("ch")
-    rows = block.reshape(KX, SUB // ch_count, LANES)
+    sp_count, ch_count = lax.axis_size("sp"), lax.axis_size("ch")
+    own = block.shape[1]
+    blocks = KYZ // (ch_count * own)
+    rows_per = own * channels // LANES
+    rows = block.reshape(KX, rows_per, LANES)
+    spread = jnp.einsum("kx,krl->xrl", x_table, rows, precision=PRECISE)
     if extra is not None:
-        row = jnp.zeros((1, SUB // ch_count, LANES), jnp.float32).at[0, 0, : extra.shape[0]].set(extra)
-        rows = jnp.concatenate([rows, row], axis=0)
-    gathered = lax.all_gather(rows, "ch", axis=1, tiled=True)
-    spread = jnp.einsum("kx,krl->xrl", x_table, gathered[:KX], precision=PRECISE)
-    if extra is not None:
-        rider = jnp.broadcast_to(gathered[KX][None], (sp_count, SUB, LANES))
+        rider = jnp.zeros((sp_count, 1, LANES), jnp.float32).at[:, 0, :own].set(
+            jnp.broadcast_to(extra[None], (sp_count, own))
+        )
         spread = jnp.concatenate([spread, rider], axis=1)
     returned = lax.all_to_all(spread, "sp", 0, 0, tiled=True)
+    local = returned[:, :rows_per].reshape(sp_count * rows_per, LANES)
+    if extra is not None:
+        pieces = returned[:, rows_per, :own].reshape(-1, LANES)
+        pieces = jnp.pad(pieces, ((0, SUB - pieces.shape[0]), (0, 0)))
+        local = jnp.concatenate([local, pieces], axis=0)
+    copies = jnp.broadcast_to(local[None], (ch_count,) + local.shape)
+    gathered = lax.all_to_all(copies, "ch", 0, 0, tiled=True)
     total = None
     if extra is not None:
-        pieces = returned[:, SUB:].reshape(sp_count, ch_count, SUB // ch_count, LANES)
-        total = pieces[:, :, 0, : extra.shape[0]].reshape(-1)
-    modes = returned[:, :SUB].reshape(KT, KYZ, channels)
-    time_spread = jnp.einsum("kt,kpo->top", time_table, modes, precision=PRECISE)
+        tail = gathered[:, sp_count * rows_per :].reshape(ch_count, -1)[:, : sp_count * own]
+        total = tail.reshape(ch_count, sp_count, own).transpose(1, 0, 2).reshape(-1)
+    modes = gathered[:, : sp_count * rows_per].reshape(ch_count, KT, blocks, own, channels)
+    time_spread = jnp.einsum("kt,mkbqo->tobmq", time_table, modes, precision=PRECISE)
     result = split_dot(time_spread.reshape(-1, KYZ), yz_table)
     return result.reshape(steps_here, 1, channels, -1), total
 

time: 212 us -> 165 us (0.78)
  blocking collectives: 88.4 us -> 41.4 us
  starting transfers between devices: 12.8 us -> 29 us
  between operations: 14.6 us -> 1.24 us
  waiting for transfers between devices: 37.7 us -> 29.6 us
  matrix products: 36.4 us -> 41 us
    reduce_scatter x2 -> x0, waiting for transfers between devices: 27.4 us -> none  [to_spectrum(): scattered = lax.psum_scatter(modes, 'ch', scatter_dimension=1, tiled=True)]
    all_to_all x2 -> x3, blocking collectives: 52 us -> 25.5 us  [the longest x2 17.1 us: to_spectrum(): summed = jnp.sum(lax.all_to_all(send, 'ch', 0, 0, tiled=True), axis=0)]
    all_to_all x0 -> x3, starting transfers between devices: none -> 23.4 us  [the longest x2 19.9 us: to_spectrum(): arrived = lax.all_to_all(data, 'sp', 0, 0, tiled=True)]
    all_to_all x0 -> x3, waiting for transfers between devices: none -> 22 us  [the longest x2 20.7 us: to_spectrum(): arrived = lax.all_to_all(data, 'sp', 0, 0, tiled=True)]
    all_gather x2 -> x0, blocking collectives: 10.6 us -> none  [to_planes(): gathered = lax.all_gather(rows, 'ch', axis=1, tiled=True)]
    all_to_all x1, blocking collectives: 25.8 us -> 15.9 us  [to_planes(): returned = lax.all_to_all(spread, 'sp', 0, 0, tiled=True)]
    all_to_all x1, starting transfers between devices: 12.7 us -> 5.68 us  [to_planes(): returned = lax.all_to_all(spread, 'sp', 0, 0, tiled=True)]
    all_to_all x1, waiting for transfers between devices: 10.3 us -> 7.57 us  [to_planes(): returned = lax.all_to_all(spread, 'sp', 0, 0, tiled=True)]
  transfers between devices with their start and end apart: 3 -> 4, of which waited for: 3 -> 4; matrix products, arithmetic and copies ran while one was open for 5% -> 6% of each run, Pallas kernels for 0% -> 0%
where the time goes in v4:
time: 165 us; the launch traced here: 163 us
  blocking collectives  41.4 us (25%)
  matrix products  41 us (25%)
  waiting for transfers between devices  29.6 us (18%)
  starting transfers between devices  29 us (18%)
  local copies, waits for them, and re-layouts  13.2 us (8%)
  other arithmetic  7.22 us (4%)
    all_to_all x2, waiting for transfers between devices, to_spectrum(): arrived = lax.all_to_all(data, 'sp', 0, 0, tiled=True)  20.7 us
    all_to_all x2, starting transfers between devices, to_spectrum(): arrived = lax.all_to_all(data, 'sp', 0, 0, tiled=True)  19.9 us
    all_to_all x2, blocking collectives, to_spectrum(): summed = jnp.sum(lax.all_to_all(send, 'ch', 0, 0, tiled=True), axis=0)  17.1 us
    all_to_all x1, blocking collectives, to_planes(): returned = lax.all_to_all(spread, 'sp', 0, 0, tiled=True)  15.9 us
    dot_general x6, matrix products, exact_spread(): jnp.dot(piece.astype(jnp.bfloat16), selector, preferred_element_type=jnp....  11.6 us
    all_to_all x1, blocking collectives, to_planes(): gathered = lax.all_to_all(copies, 'ch', 0, 0, tiled=True)  8.39 us
    all_to_all x1, waiting for transfers between devices, to_planes(): returned = lax.all_to_all(spread, 'sp', 0, 0, tiled=True)  7.57 us
    all_to_all x1, starting transfers between devices, to_planes(): returned = lax.all_to_all(spread, 'sp', 0, 0, tiled=True)  5.68 us
  transfers between devices with their start and end apart: 4, of which 4 were waited for; matrix products, arithmetic and copies ran while one was open for 6% of the time, Pallas kernels for 0%

profile of v4, /device:TPU:8, one launch (start us, length us, event | category | flops | bytes accessed | tf_op | source)
XLA Modules:
  0.0 162.7 jit_solution(12556233313118412340)
XLA Ops:
  0.7 0.1 broadcast_multiply_fusion
  0.9 0.7 fusion.34
  1.6 0.7 convolution_add_fusion.5
  2.3 2.7 %convolution_add_fusion.4 = f32[256,4096]{1,0:T(8,128)} fusion(f32[256,4096]{1,0:T(8,128)S(1)} %convolution_add_fusion.5, s32[4096]{0:T(1024)S(1)} %get-tuple-element.63, f32[256,64]{1,0:T(8,128)S(1)} %bitcast.165), kind=kOutput, calls=%fused_computation.10 | convolution fusion | flops 135626752 | bytes 8470528 | tf_op jit(solution)/shard_map/dot_general | solution.py:42
  5.0 0.7 fusion.33
  5.7 2.7 %convolution_add_fusion.3 = f32[256,4096]{1,0:T(8,128)} fusion(f32[256,4096]{1,0:T(8,128)S(1)} %fusion.33, s32[4096]{0:T(1024)S(1)} %get-tuple-element.62, f32[256,64]{1,0:T(8,128)S(1)} %bitcast.167), kind=kOutput, calls=%fused_computation.9 | convolution fusion | flops 135593984 | bytes 8470528 | tf_op jit(solution)/shard_map/dot_general | solution.py:42
  8.4 4.2 %fusion.4 = bf16[256,4096]{1,0:T(8,128)(2,1)S(1)} fusion(f32[256,4096]{1,0:T(8,128)} %convolution_add_fusion.4, f32[256,4096]{1,0:T(8,128)} %convolution_add_fusion.3, s32[4096]{0:T(1024)S(1)} %get-tuple-element.62, f32[256,64]{1,0:T(8,128)S(1)} %bitcast.168), kind=kOutput, calls=%fused_computation.13 | convolution fusion | flops 137723904 | bytes 10567680 | tf_op jit(solution)/shard_map/dot_general | solution.py:42
  12.6 2.3 %fusion.17 = f32[8,4,8,8,32]{4,2,3,1,0:T(8,128)S(1)} fusion(bf16[8,4,8,4096,1]{3,2,4,1,0:T(8,128)(2,1)S(1)} %bitcast.159, bf16[8,1,32,4096]{3,2,1,0:T(8,128)(2,1)S(1)} %copy-done), kind=kOutput, calls=%fused_computation.29 | convolution fusion | flops 536870912 | bytes 4456448 | tf_op jit(solution)/shard_map/qc,rc->qr/dot_general | solution.py:74
  14.9 1.2 convolution_bitcast_fusion.5
  16.2 0.2 copy.96
  16.4 0.3 reshape.305
  16.6 8.6 %all_to_all.40 = f32[4,128,128]{2,1,0:T(8,128)S(1)} all-to-all(f32[4,128,128]{2,1,0:T(8,128)S(1)} %reshape.305), channel_id=1, replica_groups=mesh['sp'=64,'ch'=4] {'ch'}, dimensions={0} | all-to-all | bytes 524288 | tf_op jit(solution)/shard_map/all_to_all | solution.py:84
  25.2 0.6 reduce_sum.36
  25.8 14.4 %all-to-all-start.1 = ((f32[64,2,128]{2,1,0:T(2,128)}), f32[64,2,128]{2,1,0:T(2,128)S(1)}, u32[]{:S(2)}, u32[]{:S(2)}) async-start(f32[64,2,128]{2,1,0:T(2,128)} %bitcast.12), calls=%async_computation.1 | async-start | bytes 131072 | tf_op jit(solution)/shard_map/all_to_all | solution.py:90
  40.2 1.8 %reshape.308 = bf16[16,8,32,32]{3,2,1,0:T(8,128)(2,1)S(1)} reshape(bf16[16,8,1024]{2,1,0:T(8,128)(2,1)} %param.10) | data formatting | bytes 524288 | tf_op jit(solution)/shard_map/reshape | solution.py:141
  42.1 9.2 %all-to-all-done.1 = f32[64,2,128]{2,1,0:T(2,128)S(1)} async-done(((f32[64,2,128]{2,1,0:T(2,128)}), f32[64,2,128]{2,1,0:T(2,128)S(1)}, u32[]{:S(2)}, u32[]{:S(2)}) %all-to-all-start.1) | async-done | bytes 65568 | tf_op jit(solution)/shard_map/all_to_all | solution.py:90
  51.3 0.3 fusion.55
  51.6 0.9 fusion.137
  52.7 0.4 fusion.61
  53.1 15.9 %all_to_all.41 = f32[64,2,128]{2,1,0:T(2,128)S(1)} all-to-all(f32[64,2,128]{2,1,0:T(2,128)S(1)} %copy.100), channel_id=1, replica_groups=mesh['sp'=64,'ch'=4] {'sp'}, dimensions={0} | all-to-all | bytes 131072 | tf_op jit(solution)/shard_map/all_to_all | solution.py:111
  69.1 8.4 %all_to_all.42 = f32[4,128,128]{2,1,0:T(8,128)S(1)} all-to-all(f32[4,128,128]{2,1,0:T(8,128)S(1)} %broadcast_in_dim.73), channel_id=1, replica_groups=mesh['sp'=64,'ch'=4] {'ch'}, dimensions={0} | all-to-all | bytes 524288 | tf_op jit(solution)/shard_map/all_to_all | solution.py:118
  77.5 0.3 reshape.310
  77.7 1.6 %convolution_bitcast_fusion.4 = f32[8,32,8,4,8]{1,0,4,2,3:T(8,128)S(1)} fusion(f32[4,8,8,8,32]{4,3,2,1,0:T(8,128)S(1)} %reshape.310, s32[8]{0:T(128)S(1)} %get-tuple-element.66, s32[8]{0:T(128)S(1)} %get-tuple-element.65, pred[8]{0:T(512)(128)(4,1)S(1)} %iota_compare_fusion.12), kind=kOutput, calls=%fused_computation.39 | convolution fusion | flops 6292480 | bytes 524360 | tf_op jit(solution)/shard_map/kt,mkbqo->tobmq/dot_general | solution.py:124
  79.5 0.3 reshape.311
  79.8 2.5 %fusion.49 = f32[256,4096]{1,0:T(8,128)S(1)} fusion(bf16[256,4096]{1,0:T(8,128)(2,1)} %copy-done.1, f32[256,256]{0,1:T(8,128)S(1)} %reshape.311), kind=kOutput, calls=%fused_computation.76 | convolution fusion | flops 537001984 | bytes 6553600 | tf_op jit(solution)/shard_map/dot_general | solution.py:63
  82.3 0.7 convolution_add_fusion.1
  83.1 0.8 copy-done.8
  83.9 4.5 %convert_reduce_fusion = (f32[32]{0:T(128)S(1)}, bf16[8,1,32,4096]{3,2,0,1:T(8,128)(2,1)S(1)}, f32[8,32,4096]{2,1,0:T(8,128)}) fusion(bf16[8,1,32,4096]{3,2,1,0:T(8,128)(2,1)S(1)} %copy-done.8, f32[32]{0:T(128)S(1)} %copy-done.9, f32[8,32,4096]{2,1,0:T(8,128)S(1)} %bitcast.162, bf16[32,32]{1,0:T(8,128)(2,1)S(1)} %copy-done.7, ...), kind=kOutput, calls=%fused_computation.23 | convolution fusion | flops 82837472 | bytes 14682368 | tf_op jit(solution)/shard_map/io,riy->roy/dot_general | solution.py:145
  88.4 2.4 %fusion.15 = f32[8,4,8,8,32]{4,2,3,1,0:T(8,128)S(1)} fusion(bf16[8,4,8,4096,1]{3,2,4,1,0:T(8,128)(2,1)S(1)} %bitcast.160, bf16[8,1,32,4096]{3,2,0,1:T(8,128)(2,1)S(1)} %get-tuple-element.61), kind=kOutput, calls=%fused_computation.27 | convolution fusion | flops 536870912 | bytes 4456448 | tf_op jit(solution)/shard_map/qc,rc->qr/dot_general | solution.py:74
  90.7 0.9 fusion.24
  91.6 1.2 convolution_bitcast_fusion.3
  92.8 0.2 copy.107
  93.0 0.3 reshape.313
  93.5 0.2 reshape.315
  93.7 0.1 reshape.316
  93.8 8.5 %all_to_all.43 = f32[4,136,128]{2,1,0:T(8,128)S(1)} all-to-all(f32[4,136,128]{2,1,0:T(8,128)S(1)} %select_maximum_fusion), channel_id=1, replica_groups=mesh['sp'=64,'ch'=4] {'ch'}, dimensions={0} | all-to-all | bytes 557056 | tf_op jit(solution)/shard_map/all_to_all | solution.py:84
  102.5 0.7 select_maximum_fusion.1
  103.2 5.5 %all-to-all-start.5 = ((f32[64,3,128]{2,1,0:T(4,128)}), f32[64,3,128]{2,1,0:T(4,128)S(1)}, u32[]{:S(2)}, u32[]{:S(2)}) async-start(f32[64,3,128]{2,1,0:T(4,128)} %select_maximum_fusion.1), calls=%async_computation.5 | async-start | bytes 262144 | tf_op jit(solution)/shard_map/all_to_all | solution.py:90
  108.9 11.5 %all-to-all-done.5 = f32[64,3,128]{2,1,0:T(4,128)S(1)} async-done(((f32[64,3,128]{2,1,0:T(4,128)}), f32[64,3,128]{2,1,0:T(4,128)S(1)}, u32[]{:S(2)}, u32[]{:S(2)}) %all-to-all-start.5) | async-done | bytes 98336 | tf_op jit(solution)/shard_map/all_to_all | solution.py:90
  120.4 0.3 fusion.53
  120.7 3.0 %fusion.138 = f32[16,8,1,32]{3,2,1,0:T(1,128)S(1)} fusion(f32[16,8,32,1]{2,3,1,0:T(1,128)S(1)} %bitcast.178, bf16[16,8,32,32]{3,2,1,0:T(8,128)(2,1)} %copy-done.6), kind=kOutput, calls=%fused_computation.197 | convolution fusion | flops 1572864 | bytes 294912 | tf_op jit(solution)/shard_map/kqio,kqo->kqi/dot_general | solution.py:163
  123.7 0.1 reshape.320
  123.8 0.4 fusion.59
  124.3 0.7 copy.114
  125.0 5.7 %all-to-all-start.6 = ((f32[64,3,128]{2,1,0:T(4,128)}), f32[64,3,128]{2,1,0:T(4,128)S(1)}, u32[]{:S(2)}, u32[]{:S(2)}) async-start(f32[64,3,128]{2,1,0:T(4,128)} %copy.114), calls=%async_computation.6 | async-start | bytes 262144 | tf_op jit(solution)/shard_map/all_to_all | solution.py:111
  130.7 3.6 %fusion.14 = bf16[8,1,32,4096]{3,2,1,0:T(8,128)(2,1)} fusion(f32[8,32,4096]{2,1,0:T(8,128)} %get-tuple-element.64), kind=kLoop, calls=%fused_computation.26 | loop fusion | flops 5242880 | bytes 6291456
  134.4 7.6 %all-to-all-done.6 = f32[64,3,128]{2,1,0:T(4,128)S(1)} async-done(((f32[64,3,128]{2,1,0:T(4,128)}), f32[64,3,128]{2,1,0:T(4,128)S(1)}, u32[]{:S(2)}, u32[]{:S(2)}) %all-to-all-start.6) | async-done | bytes 98336 | tf_op jit(solution)/shard_map/all_to_all | solution.py:111
  142.0 0.1 slice_reduce_fusion
  142.2 0.7 broadcast_in_dim.74
  143.0 3.4 %all-to-all-start.7 = ((f32[4,136,128]{2,1,0:T(8,128)}), f32[4,136,128]{2,1,0:T(8,128)S(1)}, u32[]{:S(2)}, u32[]{:S(2)}) async-start(f32[4,136,128]{2,1,0:T(8,128)} %broadcast_in_dim.74), calls=%async_computation.7 | async-start | bytes 557056 | tf_op jit(solution)/shard_map/all_to_all | solution.py:118
  146.4 1.8 %multiply_multiply_fusion.1 = f32[16,8,32,32]{3,2,1,0:T(8,128)} fusion(f32[16,8,32]{2,1,0:T(8,128)S(1)} %reshape.319, f32[16,8,32]{2,1,0:T(8,128)S(1)} %reshape.307), kind=kLoop, calls=%fused_computation.36 | loop fusion | flops 262144 | bytes 557056 | tf_op jit(solution)/shard_map/mul | solution.py:160
  148.2 3.1 %reshape.325 = f32[16,8,1024]{2,1,0:T(8,128)} reshape(f32[16,8,32,32]{3,2,1,0:T(8,128)} %multiply_multiply_fusion.1) | data formatting | bytes 1048576 | tf_op jit(solution)/shard_map/reshape | solution.py:160
  151.2 1.3 all-to-all-done.7
  152.6 0.1 reshape.327
  152.8 0.2 fusion.57
  153.0 0.3 reshape.322
  153.2 1.6 %convolution_bitcast_fusion.2 = f32[8,32,8,4,8]{1,0,4,2,3:T(8,128)S(1)} fusion(f32[4,8,8,8,32]{4,3,2,1,0:T(8,128)S(1)} %reshape.322, s32[8]{0:T(128)S(1)} %get-tuple-element.66, s32[8]{0:T(128)S(1)} %get-tuple-element.65, pred[8]{0:T(512)(128)(4,1)S(1)} %iota_compare_fusion.12), kind=kOutput, calls=%fused_computation.37 | convolution fusion | flops 6292480 | bytes 524360 | tf_op jit(solution)/shard_map/kt,mkbqo->tobmq/dot_general | solution.py:124
  155.0 0.3 reshape.323
  155.3 2.5 %fusion.50 = f32[256,4096]{1,0:T(8,128)S(1)} fusion(bf16[256,4096]{1,0:T(8,128)(2,1)} %copy-done.1, f32[256,256]{0,1:T(8,128)S(1)} %reshape.323), kind=kOutput, calls=%fused_computation.77 | convolution fusion | flops 537001984 | bytes 6553600 | tf_op jit(solution)/shard_map/dot_general | solution.py:63
  157.8 0.7 convolution_add_fusion
  158.6 0.8 copy-done.5
  159.4 2.0 %fusion.6 = bf16[8,1,32,4096]{3,2,1,0:T(8,128)(2,1)} fusion(f32[8,32,4096]{2,1,0:T(8,128)S(1)} %bitcast.161, bf16[8,1,32,4096]{3,2,0,1:T(8,128)(2,1)S(1)} %copy-done.5, bf16[32,32]{1,0:T(8,128)(2,1)S(1)} %copy-done.7), kind=kOutput, calls=%fused_computation.15 | convolution fusion | flops 69206016 | bytes 8390656 | tf_op jit(solution)/shard_map/io,roy->riy/dot_general | solution.py:170
  161.4 0.7 copy.120
  162.1 0.6 mul.246
  (60 shorter events, 1.5 us)
Async XLA Ops:
  0.6 11.9 %copy-start = (bf16[8,1,32,4096]{3,2,1,0:T(8,128)(2,1)S(1)}, bf16[8,1,32,4096]{3,2,1,0:T(8,128)(2,1)}, u32[]{:S(2)}) copy-start(bf16[8,1,32,4096]{3,2,1,0:T(8,128)(2,1)} %param.9) | copy-start | bytes 6291460
  12.6 2.4 %copy-start.1 = (bf16[256,4096]{1,0:T(8,128)(2,1)}, bf16[256,4096]{1,0:T(8,128)(2,1)S(1)}, u32[]{:S(2)}) copy-start(bf16[256,4096]{1,0:T(8,128)(2,1)S(1)} %fusion.4) | copy-start | bytes 6291460
  25.8 25.4 %all-to-all-start.1 = ((f32[64,2,128]{2,1,0:T(2,128)}), f32[64,2,128]{2,1,0:T(2,128)S(1)}, u32[]{:S(2)}, u32[]{:S(2)}) async-start(f32[64,2,128]{2,1,0:T(2,128)} %bitcast.12), calls=%async_computation.1 | async-start | bytes 131072 | tf_op jit(solution)/shard_map/all_to_all | solution.py:90
  42.1 27.0 %copy-start.6 = (bf16[16,8,32,32]{3,2,1,0:T(8,128)(2,1)}, bf16[16,8,32,32]{3,2,1,0:T(8,128)(2,1)S(1)}, u32[]{:S(2)}) copy-start(bf16[16,8,32,32]{3,2,1,0:T(8,128)(2,1)S(1)} %reshape.308) | copy-start | bytes 786436
  79.8 2.5 %copy-start.2 = (bf16[256,4096]{1,0:T(8,128)(2,1)S(1)}, bf16[256,4096]{1,0:T(8,128)(2,1)}, u32[]{:S(2)}) copy-start(bf16[256,4096]{1,0:T(8,128)(2,1)} %copy-done.1) | copy-start | bytes 6291460
  82.3 0.8 copy-start.7
  82.3 1.6 copy-start.8
  82.3 1.6 copy-start.9
  88.4 2.4 %copy-start.4 = (bf16[8,1,32,4096]{3,2,0,1:T(8,128)(2,1)}, bf16[8,1,32,4096]{3,2,0,1:T(8,128)(2,1)S(1)}, u32[]{:S(2)}) copy-start(bf16[8,1,32,4096]{3,2,0,1:T(8,128)(2,1)S(1)} %get-tuple-element.61) | copy-start | bytes 6291460
  103.2 17.1 %all-to-all-start.5 = ((f32[64,3,128]{2,1,0:T(4,128)}), f32[64,3,128]{2,1,0:T(4,128)S(1)}, u32[]{:S(2)}, u32[]{:S(2)}) async-start(f32[64,3,128]{2,1,0:T(4,128)} %select_maximum_fusion.1), calls=%async_computation.5 | async-start | bytes 262144 | tf_op jit(solution)/shard_map/all_to_all | solution.py:90
  125.0 17.0 %all-to-all-start.6 = ((f32[64,3,128]{2,1,0:T(4,128)}), f32[64,3,128]{2,1,0:T(4,128)S(1)}, u32[]{:S(2)}, u32[]{:S(2)}) async-start(f32[64,3,128]{2,1,0:T(4,128)} %copy.114), calls=%async_computation.6 | async-start | bytes 262144 | tf_op jit(solution)/shard_map/all_to_all | solution.py:111
  143.0 9.6 %all-to-all-start.7 = ((f32[4,136,128]{2,1,0:T(8,128)}), f32[4,136,128]{2,1,0:T(8,128)S(1)}, u32[]{:S(2)}, u32[]{:S(2)}) async-start(f32[4,136,128]{2,1,0:T(8,128)} %broadcast_in_dim.74), calls=%async_computation.7 | async-start | bytes 557056 | tf_op jit(solution)/shard_map/all_to_all | solution.py:118
  155.3 2.5 %copy-start.3 = (bf16[256,4096]{1,0:T(8,128)(2,1)S(1)}, bf16[256,4096]{1,0:T(8,128)(2,1)}, u32[]{:S(2)}) copy-start(bf16[256,4096]{1,0:T(8,128)(2,1)} %copy-done.1) | copy-start | bytes 6291460
  157.8 1.6 copy-start.5

commit v5 on v4

--- a/solution.py
+++ b/solution.py
@@ -34,14 +34,14 @@
 
 
 def exact_spread(rows, selector):
-    total = None
+    pieces = []
     rest = rows
     for _ in range(3):
         piece = lax.reduce_precision(rest, exponent_bits=8, mantissa_bits=7)
         rest = rest - piece
-        part = jnp.dot(piece.astype(jnp.bfloat16), selector, preferred_element_type=jnp.float32)
-        total = part if total is None else total + part
-    return total
+        pieces.append(piece.astype(jnp.bfloat16))
+    stacked = jnp.concatenate([selector] * 3, axis=0)
+    return jnp.dot(jnp.concatenate(pieces, axis=1), stacked, preferred_element_type=jnp.float32)
 
 
 def plane_table():

time: 165 us -> 155 us (0.939)
  matrix products: 41 us -> 30.9 us
    dot_general x6 -> x2, matrix products: 11.6 us -> 1.53 us  [exact_spread(): jnp.dot(jnp.concatenate(pieces, axis=1), stacked, preferred_element_type=...]
  transfers between devices with their start and end apart: 4 -> 4, of which waited for: 4 -> 4; matrix products, arithmetic and copies ran while one was open for 6% -> 7% of each run, Pallas kernels for 0% -> 0%
where the time goes in v5:
time: 155 us; the launch traced here: 153 us
  blocking collectives  41.4 us (27%)
  matrix products  30.9 us (20%)
  waiting for transfers between devices  29.6 us (19%)
  starting transfers between devices  29.2 us (19%)
  local copies, waits for them, and re-layouts  13.2 us (9%)
  other arithmetic  7.58 us (5%)
    all_to_all x2, waiting for transfers between devices, to_spectrum(): arrived = lax.all_to_all(data, 'sp', 0, 0, tiled=True)  20.7 us
    all_to_all x2, starting transfers between devices, to_spectrum(): arrived = lax.all_to_all(data, 'sp', 0, 0, tiled=True)  19.9 us
    all_to_all x2, blocking collectives, to_spectrum(): summed = jnp.sum(lax.all_to_all(send, 'ch', 0, 0, tiled=True), axis=0)  17.1 us
    all_to_all x1, blocking collectives, to_planes(): returned = lax.all_to_all(spread, 'sp', 0, 0, tiled=True)  15.9 us
    all_to_all x1, blocking collectives, to_planes(): gathered = lax.all_to_all(copies, 'ch', 0, 0, tiled=True)  8.39 us
    all_to_all x1, waiting for transfers between devices, to_planes(): returned = lax.all_to_all(spread, 'sp', 0, 0, tiled=True)  7.57 us
    all_to_all x1, starting transfers between devices, to_planes(): returned = lax.all_to_all(spread, 'sp', 0, 0, tiled=True)  5.9 us
    dot_general x2, matrix products, split_dot(): jnp.dot(high.astype(jnp.bfloat16), table, preferred_element_type=jnp.floa...  4.94 us
  transfers between devices with their start and end apart: 4, of which 4 were waited for; matrix products, arithmetic and copies ran while one was open for 7% of the time, Pallas kernels for 0%

profile of v5, /device:TPU:8, one launch (start us, length us, event | category | flops | bytes accessed | tf_op | source)
XLA Modules:
  0.0 153.1 jit_solution(11510047206234031671)
XLA Ops:
  0.7 0.1 broadcast_multiply_fusion
  1.0 0.3 iota_compare_fusion
  1.3 0.8 fusion.13
  2.0 0.8 fusion.3
  2.8 2.3 %fusion.27 = f32[8,4,8,8,32]{4,2,3,1,0:T(8,128)S(1)} fusion(bf16[8,4,8,4096,1]{3,2,4,1,0:T(8,128)(2,1)S(1)} %bitcast.159, bf16[8,1,32,4096]{3,2,1,0:T(8,128)(2,1)S(1)} %copy-done), kind=kOutput, calls=%fused_computation.36 | convolution fusion | flops 536870912 | bytes 4456448 | tf_op jit(solution)/shard_map/qc,rc->qr/dot_general | solution.py:74
  5.2 1.2 convolution_bitcast_fusion.5
  6.4 0.2 copy.96
  6.6 0.3 reshape.305
  6.9 8.6 %all_to_all.40 = f32[4,128,128]{2,1,0:T(8,128)S(1)} all-to-all(f32[4,128,128]{2,1,0:T(8,128)S(1)} %reshape.305), channel_id=1, replica_groups=mesh['sp'=64,'ch'=4] {'ch'}, dimensions={0} | all-to-all | bytes 524288 | tf_op jit(solution)/shard_map/all_to_all | solution.py:84
  15.5 0.6 reduce_sum.36
  16.1 14.4 %all-to-all-start.1 = ((f32[64,2,128]{2,1,0:T(2,128)}), f32[64,2,128]{2,1,0:T(2,128)S(1)}, u32[]{:S(2)}, u32[]{:S(2)}) async-start(f32[64,2,128]{2,1,0:T(2,128)} %bitcast.12), calls=%async_computation.1 | async-start | bytes 131072 | tf_op jit(solution)/shard_map/all_to_all | solution.py:90
  30.5 1.8 %reshape.308 = bf16[16,8,32,32]{3,2,1,0:T(8,128)(2,1)S(1)} reshape(bf16[16,8,1024]{2,1,0:T(8,128)(2,1)} %param.10) | data formatting | bytes 524288 | tf_op jit(solution)/shard_map/reshape | solution.py:141
  32.4 9.2 %all-to-all-done.1 = f32[64,2,128]{2,1,0:T(2,128)S(1)} async-done(((f32[64,2,128]{2,1,0:T(2,128)}), f32[64,2,128]{2,1,0:T(2,128)S(1)}, u32[]{:S(2)}, u32[]{:S(2)}) %all-to-all-start.1) | async-done | bytes 65568 | tf_op jit(solution)/shard_map/all_to_all | solution.py:90
  41.5 0.3 fusion.65
  41.8 0.1 reshape.332
  41.9 0.9 fusion.151
  42.8 0.1 reshape.309
  42.9 0.4 fusion.71
  43.4 15.9 %all_to_all.41 = f32[64,2,128]{2,1,0:T(2,128)S(1)} all-to-all(f32[64,2,128]{2,1,0:T(2,128)S(1)} %copy.100), channel_id=1, replica_groups=mesh['sp'=64,'ch'=4] {'sp'}, dimensions={0} | all-to-all | bytes 131072 | tf_op jit(solution)/shard_map/all_to_all | solution.py:111
  59.3 8.4 %all_to_all.42 = f32[4,128,128]{2,1,0:T(8,128)S(1)} all-to-all(f32[4,128,128]{2,1,0:T(8,128)S(1)} %broadcast_in_dim.73), channel_id=1, replica_groups=mesh['sp'=64,'ch'=4] {'ch'}, dimensions={0} | all-to-all | bytes 524288 | tf_op jit(solution)/shard_map/all_to_all | solution.py:118
  67.7 0.3 reshape.310
  68.0 1.6 %convolution_bitcast_fusion.4 = f32[8,32,8,4,8]{1,0,4,2,3:T(8,128)S(1)} fusion(f32[4,8,8,8,32]{4,3,2,1,0:T(8,128)S(1)} %reshape.310, s32[8]{0:T(128)S(1)} %get-tuple-element.77, s32[8]{0:T(128)S(1)} %get-tuple-element.76, pred[8]{0:T(512)(128)(4,1)S(1)} %iota_compare_fusion.6), kind=kOutput, calls=%fused_computation.46 | convolution fusion | flops 6292480 | bytes 524360 | tf_op jit(solution)/shard_map/kt,mkbqo->tobmq/dot_general | solution.py:124
  69.7 0.3 reshape.311
  70.0 2.5 %fusion.51 = f32[256,4096]{1,0:T(8,128)S(1)} fusion(bf16[256,4096]{1,0:T(8,128)(2,1)} %copy-done.1, f32[256,256]{0,1:T(8,128)S(1)} %reshape.311), kind=kOutput, calls=%fused_computation.75 | convolution fusion | flops 537001984 | bytes 6553600 | tf_op jit(solution)/shard_map/dot_general | solution.py:63
  72.6 0.7 convolution_add_fusion.1
  73.3 0.8 copy-done.8
  74.1 4.5 %convert_reduce_fusion = (f32[32]{0:T(128)S(1)}, bf16[8,1,32,4096]{3,2,0,1:T(8,128)(2,1)S(1)}, f32[8,32,4096]{2,1,0:T(8,128)}) fusion(bf16[8,1,32,4096]{3,2,1,0:T(8,128)(2,1)S(1)} %copy-done.8, f32[32]{0:T(128)S(1)} %copy-done.9, f32[8,32,4096]{2,1,0:T(8,128)S(1)} %bitcast.162, bf16[32,32]{1,0:T(8,128)(2,1)S(1)} %copy-done.7, ...), kind=kOutput, calls=%fused_computation.19 | convolution fusion | flops 82837472 | bytes 14682368 | tf_op jit(solution)/shard_map/io,riy->roy/dot_general | solution.py:145
  78.6 2.4 %fusion.25 = f32[8,4,8,8,32]{4,2,3,1,0:T(8,128)S(1)} fusion(bf16[8,4,8,4096,1]{3,2,4,1,0:T(8,128)(2,1)S(1)} %bitcast.160, bf16[8,1,32,4096]{3,2,0,1:T(8,128)(2,1)S(1)} %get-tuple-element.61), kind=kOutput, calls=%fused_computation.34 | convolution fusion | flops 536870912 | bytes 4456448 | tf_op jit(solution)/shard_map/qc,rc->qr/dot_general | solution.py:74
  81.0 0.9 fusion.34
  81.9 1.2 convolution_bitcast_fusion.3
  83.1 0.2 copy.107
  83.3 0.3 reshape.313
  83.7 0.2 reshape.315
  84.0 0.1 reshape.316
  84.1 8.5 %all_to_all.43 = f32[4,136,128]{2,1,0:T(8,128)S(1)} all-to-all(f32[4,136,128]{2,1,0:T(8,128)S(1)} %select_maximum_fusion), channel_id=1, replica_groups=mesh['sp'=64,'ch'=4] {'ch'}, dimensions={0} | all-to-all | bytes 557056 | tf_op jit(solution)/shard_map/all_to_all | solution.py:84
  92.8 0.7 select_maximum_fusion.1
  93.5 5.5 %all-to-all-start.5 = ((f32[64,3,128]{2,1,0:T(4,128)}), f32[64,3,128]{2,1,0:T(4,128)S(1)}, u32[]{:S(2)}, u32[]{:S(2)}) async-start(f32[64,3,128]{2,1,0:T(4,128)} %select_maximum_fusion.1), calls=%async_computation.5 | async-start | bytes 262144 | tf_op jit(solution)/shard_map/all_to_all | solution.py:90
  99.1 11.5 %all-to-all-done.5 = f32[64,3,128]{2,1,0:T(4,128)S(1)} async-done(((f32[64,3,128]{2,1,0:T(4,128)}), f32[64,3,128]{2,1,0:T(4,128)S(1)}, u32[]{:S(2)}, u32[]{:S(2)}) %all-to-all-start.5) | async-done | bytes 98336 | tf_op jit(solution)/shard_map/all_to_all | solution.py:90
  110.6 0.3 fusion.63
  111.0 3.0 %fusion.152 = f32[16,8,1,32]{3,2,1,0:T(1,128)S(1)} fusion(f32[16,8,32,1]{2,3,1,0:T(1,128)S(1)} %bitcast.174, bf16[16,8,32,32]{3,2,1,0:T(8,128)(2,1)} %copy-done.6), kind=kOutput, calls=%fused_computation.210 | convolution fusion | flops 1572864 | bytes 294912 | tf_op jit(solution)/shard_map/kqio,kqo->kqi/dot_general | solution.py:163
  113.9 0.1 reshape.320
  114.0 0.4 fusion.69
  114.5 0.7 copy.114
  115.3 5.9 %all-to-all-start.6 = ((f32[64,3,128]{2,1,0:T(4,128)}), f32[64,3,128]{2,1,0:T(4,128)S(1)}, u32[]{:S(2)}, u32[]{:S(2)}) async-start(f32[64,3,128]{2,1,0:T(4,128)} %copy.114), calls=%async_computation.6 | async-start | bytes 262144 | tf_op jit(solution)/shard_map/all_to_all | solution.py:111
  121.2 3.6 %fusion.24 = bf16[8,1,32,4096]{3,2,1,0:T(8,128)(2,1)} fusion(f32[8,32,4096]{2,1,0:T(8,128)} %get-tuple-element.70), kind=kLoop, calls=%fused_computation.33 | loop fusion | flops 5242880 | bytes 6291456
  124.9 7.6 %all-to-all-done.6 = f32[64,3,128]{2,1,0:T(4,128)S(1)} async-done(((f32[64,3,128]{2,1,0:T(4,128)}), f32[64,3,128]{2,1,0:T(4,128)S(1)}, u32[]{:S(2)}, u32[]{:S(2)}) %all-to-all-start.6) | async-done | bytes 98336 | tf_op jit(solution)/shard_map/all_to_all | solution.py:111
  132.4 0.1 slice_reduce_fusion
  132.5 0.1 reshape_squeeze.3
  132.7 0.7 broadcast_in_dim.74
  133.4 3.4 %all-to-all-start.7 = ((f32[4,136,128]{2,1,0:T(8,128)}), f32[4,136,128]{2,1,0:T(8,128)S(1)}, u32[]{:S(2)}, u32[]{:S(2)}) async-start(f32[4,136,128]{2,1,0:T(8,128)} %broadcast_in_dim.74), calls=%async_computation.7 | async-start | bytes 557056 | tf_op jit(solution)/shard_map/all_to_all | solution.py:118
  136.9 1.8 %multiply_multiply_fusion.1 = f32[16,8,32,32]{3,2,1,0:T(8,128)} fusion(f32[16,8,32]{2,1,0:T(8,128)S(1)} %reshape.319, f32[16,8,32]{2,1,0:T(8,128)S(1)} %reshape.307), kind=kLoop, calls=%fused_computation.43 | loop fusion | flops 262144 | bytes 557056 | tf_op jit(solution)/shard_map/mul | solution.py:160
  138.6 3.1 %reshape.325 = f32[16,8,1024]{2,1,0:T(8,128)} reshape(f32[16,8,32,32]{3,2,1,0:T(8,128)} %multiply_multiply_fusion.1) | data formatting | bytes 1048576 | tf_op jit(solution)/shard_map/reshape | solution.py:160
  141.7 1.3 all-to-all-done.7
  143.0 0.1 reshape.327
  143.2 0.2 fusion.67
  143.4 0.3 reshape.322
  143.7 1.6 %convolution_bitcast_fusion.2 = f32[8,32,8,4,8]{1,0,4,2,3:T(8,128)S(1)} fusion(f32[4,8,8,8,32]{4,3,2,1,0:T(8,128)S(1)} %reshape.322, s32[8]{0:T(128)S(1)} %get-tuple-element.77, s32[8]{0:T(128)S(1)} %get-tuple-element.76, pred[8]{0:T(512)(128)(4,1)S(1)} %iota_compare_fusion.6), kind=kOutput, calls=%fused_computation.44 | convolution fusion | flops 6292480 | bytes 524360 | tf_op jit(solution)/shard_map/kt,mkbqo->tobmq/dot_general | solution.py:124
  145.4 0.3 reshape.323
  145.8 2.5 %fusion.52 = f32[256,4096]{1,0:T(8,128)S(1)} fusion(bf16[256,4096]{1,0:T(8,128)(2,1)} %copy-done.1, f32[256,256]{0,1:T(8,128)S(1)} %reshape.323), kind=kOutput, calls=%fused_computation.76 | convolution fusion | flops 537001984 | bytes 6553600 | tf_op jit(solution)/shard_map/dot_general | solution.py:63
  148.2 0.7 convolution_add_fusion
  149.0 0.8 copy-done.5
  149.8 2.0 %fusion.5 = bf16[8,1,32,4096]{3,2,1,0:T(8,128)(2,1)} fusion(f32[8,32,4096]{2,1,0:T(8,128)S(1)} %bitcast.161, bf16[8,1,32,4096]{3,2,0,1:T(8,128)(2,1)S(1)} %copy-done.5, bf16[32,32]{1,0:T(8,128)(2,1)S(1)} %copy-done.7), kind=kOutput, calls=%fused_computation.11 | convolution fusion | flops 69206016 | bytes 8390656 | tf_op jit(solution)/shard_map/io,roy->riy/dot_general | solution.py:170
  151.8 0.7 copy.120
  152.5 0.6 mul.246
  (58 shorter events, 1.3 us)
Async XLA Ops:
  0.6 2.2 %copy-start = (bf16[8,1,32,4096]{3,2,1,0:T(8,128)(2,1)S(1)}, bf16[8,1,32,4096]{3,2,1,0:T(8,128)(2,1)}, u32[]{:S(2)}) copy-start(bf16[8,1,32,4096]{3,2,1,0:T(8,128)(2,1)} %param.9) | copy-start | bytes 6291460
  2.8 2.4 %copy-start.1 = (bf16[256,4096]{1,0:T(8,128)(2,1)}, bf16[256,4096]{1,0:T(8,128)(2,1)S(1)}, u32[]{:S(2)}) copy-start(bf16[256,4096]{1,0:T(8,128)(2,1)S(1)} %fusion.3) | copy-start | bytes 6291460
  16.1 25.4 %all-to-all-start.1 = ((f32[64,2,128]{2,1,0:T(2,128)}), f32[64,2,128]{2,1,0:T(2,128)S(1)}, u32[]{:S(2)}, u32[]{:S(2)}) async-start(f32[64,2,128]{2,1,0:T(2,128)} %bitcast.12), calls=%async_computation.1 | async-start | bytes 131072 | tf_op jit(solution)/shard_map/all_to_all | solution.py:90
  32.4 27.0 %copy-start.6 = (bf16[16,8,32,32]{3,2,1,0:T(8,128)(2,1)}, bf16[16,8,32,32]{3,2,1,0:T(8,128)(2,1)S(1)}, u32[]{:S(2)}) copy-start(bf16[16,8,32,32]{3,2,1,0:T(8,128)(2,1)S(1)} %reshape.308) | copy-start | bytes 786436
  70.0 2.5 %copy-start.2 = (bf16[256,4096]{1,0:T(8,128)(2,1)S(1)}, bf16[256,4096]{1,0:T(8,128)(2,1)}, u32[]{:S(2)}) copy-start(bf16[256,4096]{1,0:T(8,128)(2,1)} %copy-done.1) | copy-start | bytes 6291460
  72.5 0.8 copy-start.7
  72.5 1.6 %copy-start.8 = (bf16[8,1,32,4096]{3,2,1,0:T(8,128)(2,1)S(1)}, bf16[8,1,32,4096]{3,2,1,0:T(8,128)(2,1)}, u32[]{:S(2)}) copy-start(bf16[8,1,32,4096]{3,2,1,0:T(8,128)(2,1)} %param.13) | copy-start | bytes 6291460
  72.5 1.6 %copy-start.9 = (f32[32]{0:T(128)S(1)}, f32[32]{0:T(128)}, u32[]{:S(2)}) copy-start(f32[32]{0:T(128)} %param.12) | copy-start | bytes 388
  78.6 2.4 %copy-start.4 = (bf16[8,1,32,4096]{3,2,0,1:T(8,128)(2,1)}, bf16[8,1,32,4096]{3,2,0,1:T(8,128)(2,1)S(1)}, u32[]{:S(2)}) copy-start(bf16[8,1,32,4096]{3,2,0,1:T(8,128)(2,1)S(1)} %get-tuple-element.61) | copy-start | bytes 6291460
  93.5 17.1 %all-to-all-start.5 = ((f32[64,3,128]{2,1,0:T(4,128)}), f32[64,3,128]{2,1,0:T(4,128)S(1)}, u32[]{:S(2)}, u32[]{:S(2)}) async-start(f32[64,3,128]{2,1,0:T(4,128)} %select_maximum_fusion.1), calls=%async_computation.5 | async-start | bytes 262144 | tf_op jit(solution)/shard_map/all_to_all | solution.py:90
  115.3 17.2 %all-to-all-start.6 = ((f32[64,3,128]{2,1,0:T(4,128)}), f32[64,3,128]{2,1,0:T(4,128)S(1)}, u32[]{:S(2)}, u32[]{:S(2)}) async-start(f32[64,3,128]{2,1,0:T(4,128)} %copy.114), calls=%async_computation.6 | async-start | bytes 262144 | tf_op jit(solution)/shard_map/all_to_all | solution.py:111
  133.4 9.6 %all-to-all-start.7 = ((f32[4,136,128]{2,1,0:T(8,128)}), f32[4,136,128]{2,1,0:T(8,128)S(1)}, u32[]{:S(2)}, u32[]{:S(2)}) async-start(f32[4,136,128]{2,1,0:T(8,128)} %broadcast_in_dim.74), calls=%async_computation.7 | async-start | bytes 557056 | tf_op jit(solution)/shard_map/all_to_all | solution.py:118
  145.7 2.5 %copy-start.3 = (bf16[256,4096]{1,0:T(8,128)(2,1)S(1)}, bf16[256,4096]{1,0:T(8,128)(2,1)}, u32[]{:S(2)}) copy-start(bf16[256,4096]{1,0:T(8,128)(2,1)} %copy-done.1) | copy-start | bytes 6291460
  148.2 1.6 %copy-start.5 = (bf16[8,1,32,4096]{3,2,0,1:T(8,128)(2,1)S(1)}, bf16[8,1,32,4096]{3,2,0,1:T(8,128)(2,1)}, u32[]{:S(2)}) copy-start(bf16[8,1,32,4096]{3,2,0,1:T(8,128)(2,1)} %copy-done.4) | copy-start | bytes 6291460

commit v6 on v5

--- a/solution.py
+++ b/solution.py
@@ -69,26 +69,19 @@
     steps_here, planes, channels, plane_cells = values.shape
     sp_count, ch_count = lax.axis_size("sp"), lax.axis_size("ch")
     own = Q // (sp_count * ch_count)
-    blocks = KYZ // (ch_count * own)
     rows_per = own * channels // LANES
     flat = jnp.einsum(
         "qc,rc->qr", yz_table, values.reshape(-1, plane_cells), preferred_element_type=jnp.float32
-    ).reshape(blocks, ch_count, own, steps_here, channels)
-    partial = jnp.einsum("kt,bmqtc->mkbqc", time_table, flat, precision=PRECISE)
-    send = partial.reshape(ch_count, sp_count * rows_per, LANES)
+    ).reshape(KYZ, steps_here, channels)
+    partial = jnp.einsum("kt,ptc->kpc", time_table, flat, precision=PRECISE)
+    send = partial.reshape(sp_count * ch_count, rows_per, LANES)
     if extra is not None:
-        rider = extra.reshape(sp_count, ch_count, own).transpose(1, 0, 2)
-        rider = rider.reshape(ch_count, -1, LANES)
-        rider = jnp.pad(rider, ((0, 0), (0, SUB - rider.shape[1]), (0, 0)))
+        rider = jnp.zeros((sp_count * ch_count, 1, LANES), jnp.float32)
+        rider = rider.at[:, 0, :own].set(extra.reshape(-1, own))
         send = jnp.concatenate([send, rider], axis=1)
-    summed = jnp.sum(lax.all_to_all(send, "ch", 0, 0, tiled=True), axis=0)
-    data = summed[: sp_count * rows_per].reshape(sp_count, rows_per, LANES)
-    if extra is not None:
-        pieces = summed[sp_count * rows_per :].reshape(-1)[: sp_count * own].reshape(sp_count, own)
-        rider = jnp.zeros((sp_count, 1, LANES), jnp.float32).at[:, 0, :own].set(pieces)
-        data = jnp.concatenate([data, rider], axis=1)
-    arrived = lax.all_to_all(data, "sp", 0, 0, tiled=True)
-    owned = jnp.einsum("kx,xrl->krl", x_table, arrived[:, :rows_per], precision=PRECISE)
+    arrived = lax.all_to_all(send, ("sp", "ch"), 0, 0, tiled=True)
+    by_plane = arrived[:, :rows_per].reshape(sp_count, ch_count, rows_per, LANES)
+    owned = jnp.einsum("kx,xmrl->krl", x_table, by_plane, precision=PRECISE)
     owned = owned.reshape(KX, own, channels)
     if extra is None:
         return owned
@@ -99,7 +92,6 @@
     channels = block.shape[2]
     sp_count, ch_count = lax.axis_size("sp"), lax.axis_size("ch")
     own = block.shape[1]
-    blocks = KYZ // (ch_count * own)
     rows_per = own * channels // LANES
     rows = block.reshape(KX, rows_per, LANES)
     spread = jnp.einsum("kx,krl->xrl", x_table, rows, precision=PRECISE)
@@ -108,20 +100,13 @@
             jnp.broadcast_to(extra[None], (sp_count, own))
         )
         spread = jnp.concatenate([spread, rider], axis=1)
-    returned = lax.all_to_all(spread, "sp", 0, 0, tiled=True)
-    local = returned[:, :rows_per].reshape(sp_count * rows_per, LANES)
-    if extra is not None:
-        pieces = returned[:, rows_per, :own].reshape(-1, LANES)
-        pieces = jnp.pad(pieces, ((0, SUB - pieces.shape[0]), (0, 0)))
-        local = jnp.concatenate([local, pieces], axis=0)
-    copies = jnp.broadcast_to(local[None], (ch_count,) + local.shape)
-    gathered = lax.all_to_all(copies, "ch", 0, 0, tiled=True)
-    total = None
-    if extra is not None:
-        tail = gathered[:, sp_count * rows_per :].reshape(ch_count, -1)[:, : sp_count * own]
-        total = tail.reshape(ch_count, sp_count, own).transpose(1, 0, 2).reshape(-1)
-    modes = gathered[:, : sp_count * rows_per].reshape(ch_count, KT, blocks, own, channels)
-    time_spread = jnp.einsum("kt,mkbqo->tobmq", time_table, modes, precision=PRECISE)
+    copies = jnp.broadcast_to(spread[:, None], (sp_count, ch_count) + spread.shape[1:])
+    returned = lax.all_to_all(
+        copies.reshape((-1,) + spread.shape[1:]), ("sp", "ch"), 0, 0, tiled=True
+    )
+    total = returned[:, rows_per, :own].reshape(-1) if extra is not None else None
+    modes = returned[:, :rows_per].reshape(KT, KYZ, channels)
+    time_spread = jnp.einsum("kt,kpo->top", time_table, modes, precision=PRECISE)
     result = split_dot(time_spread.reshape(-1, KYZ), yz_table)
     return result.reshape(steps_here, 1, channels, -1), total
 

time: 155 us -> 147 us (0.948)
  blocking collectives: 41.4 us -> 20.6 us
  waiting for transfers between devices: 29.6 us -> 40.8 us
  local copies, waits for them, and re-layouts: 13.2 us -> 16.5 us
  matrix products: 30.9 us -> 28.5 us
    all_to_all x4 -> x1, blocking collectives: 41.4 us -> 20.6 us  [to_planes(): lax.all_to_all(copies.reshape((-1,) + spread.shape[1:]), ('sp', 'ch'), 0,...]
    all_to_all x4 -> x3, waiting for transfers between devices: 29.6 us -> 40.8 us  [the longest x2 30.2 us: to_spectrum(): arrived = lax.all_to_all(send, ('sp', 'ch'), 0, 0, tiled=True)]
    dot_general x6, matrix products: 6.25 us -> 3.41 us  [the longest x2 1.38 us: to_spectrum(): owned = jnp.einsum('kx,xmrl->krl', x_table, by_plane, precision=PRECISE)]
    dot_general x2 -> x6, local copies, waits for them, and re-layouts: 0.02 us -> 1.8 us  [the longest x4 1.09 us: to_spectrum(): owned = jnp.einsum('kx,xmrl->krl', x_table, by_plane, precision=PRECISE)]
    unnamed x23 -> x36, local copies, waits for them, and re-layouts: 2.38 us -> 3.71 us
    all_to_all x4 -> x3, starting transfers between devices: 29.2 us -> 28.3 us  [the longest x2 21.2 us: to_spectrum(): arrived = lax.all_to_all(send, ('sp', 'ch'), 0, 0, tiled=True)]
  transfers between devices with their start and end apart: 4 -> 3, of which waited for: 4 -> 3; matrix products, arithmetic and copies ran while one was open for 7% -> 8% of each run, Pallas kernels for 0% -> 0%
where the time goes in v6:
time: 147 us; the launch traced here: 144 us
  waiting for transfers between devices  40.8 us (28%)
  matrix products  28.5 us (19%)
  starting transfers between devices  28.3 us (19%)
  blocking collectives  20.6 us (14%)
  local copies, waits for them, and re-layouts  16.5 us (11%)
  other arithmetic  7.74 us (5%)
    all_to_all x2, waiting for transfers between devices, to_spectrum(): arrived = lax.all_to_all(send, ('sp', 'ch'), 0, 0, tiled=True)  30.2 us
    all_to_all x2, starting transfers between devices, to_spectrum(): arrived = lax.all_to_all(send, ('sp', 'ch'), 0, 0, tiled=True)  21.2 us
    all_to_all x1, blocking collectives, to_planes(): lax.all_to_all(copies.reshape((-1,) + spread.shape[1:]), ('sp', 'ch'), 0,...  20.6 us
    all_to_all x1, waiting for transfers between devices, to_planes(): lax.all_to_all(copies.reshape((-1,) + spread.shape[1:]), ('sp', 'ch'), 0,...  10.6 us
    all_to_all x1, starting transfers between devices, to_planes(): lax.all_to_all(copies.reshape((-1,) + spread.shape[1:]), ('sp', 'ch'), 0,...  7.1 us
    dot_general x2, matrix products, to_spectrum(): jnp.einsum('qc,rc->qr', yz_table, values.reshape(-1, plane_cells), prefer...  5.17 us
    dot_general x2, matrix products, split_dot(): jnp.dot(high.astype(jnp.bfloat16), table, preferred_element_type=jnp.floa...  4.91 us
    dot_general x1, matrix products, shards(): jnp.einsum('io,riy->roy', point_weight, field_rows, preferred_element_typ...  4.5 us
  transfers between devices with their start and end apart: 3, of which 3 were waited for; matrix products, arithmetic and copies ran while one was open for 8% of the time, Pallas kernels for 0%

profile of v6, /device:TPU:8, one launch (start us, length us, event | category | flops | bytes accessed | tf_op | source)
XLA Modules:
  0.0 143.7 jit_solution(5342902837735505817)
XLA Ops:
  0.7 0.1 broadcast_multiply_fusion
  1.0 0.3 iota_compare_fusion
  1.3 0.8 fusion.13
  2.1 0.8 fusion.3
  2.9 1.5 %fusion.27 = f32[256,8,32]{0,1,2:T(8,128)S(1)} fusion(bf16[256,4096]{1,0:T(8,128)(2,1)S(1)} %fusion.3, bf16[8,32,4096]{2,1,0:T(8,128)(2,1)S(1)} %bitcast.132), kind=kOutput, calls=%fused_computation.36 | convolution fusion | flops 536870912 | bytes 4456448 | tf_op jit(solution)/shard_map/qc,rc->qr/dot_general | solution.py:73
  4.4 0.5 fusion.81
  4.9 0.4 copy.65
  5.3 1.0 reshape.288
  6.3 14.6 %all-to-all-start = ((f32[256,2,128]{2,1,0:T(2,128)}), f32[256,2,128]{2,1,0:T(2,128)S(1)}, u32[]{:S(2)}, u32[]{:S(2)}) async-start(f32[256,2,128]{2,1,0:T(2,128)} %reshape.288), calls=%async_computation | async-start | bytes 524288 | tf_op jit(solution)/shard_map/all_to_all | solution.py:82
  20.9 1.8 %reshape.290 = bf16[16,8,32,32]{3,2,1,0:T(8,128)(2,1)S(1)} reshape(bf16[16,8,1024]{2,1,0:T(8,128)(2,1)} %param.10) | data formatting | bytes 524288 | tf_op jit(solution)/shard_map/reshape | solution.py:126
  22.8 12.0 %all-to-all-done = f32[256,2,128]{2,1,0:T(2,128)S(1)} async-done(((f32[256,2,128]{2,1,0:T(2,128)}), f32[256,2,128]{2,1,0:T(2,128)S(1)}, u32[]{:S(2)}, u32[]{:S(2)}) %all-to-all-start) | async-done | bytes 262176 | tf_op jit(solution)/shard_map/all_to_all | solution.py:82
  34.8 0.1 bitcast_reduce_fusion.1
  34.8 0.1 copy.66
  35.0 0.7 fusion.64
  35.6 0.6 copy-done.7
  36.3 0.9 fusion.50
  37.2 0.1 reshape.291
  37.3 0.4 fusion.54
  37.9 20.6 %all_to_all.20 = f32[256,2,128]{2,1,0:T(2,128)S(1)} all-to-all(f32[256,2,128]{2,1,0:T(2,128)S(1)} %bitcast.136), channel_id=1, replica_groups=mesh['sp'=64,'ch'=4] {'sp','ch'}, dimensions={0} | all-to-all | bytes 524288 | tf_op jit(solution)/shard_map/all_to_all | solution.py:104
  58.5 0.4 reshape.293
  59.0 0.3 copy.69
  59.3 0.5 convolution_bitcast_fusion.3
  59.8 0.1 copy.70
  59.9 2.5 %fusion.143 = f32[256,4096]{1,0:T(8,128)S(1)} fusion(bf16[256,256]{1,0:T(8,128)(2,1)S(1)} %get-tuple-element.60, bf16[256,4096]{1,0:T(8,128)(2,1)} %copy-done.1), kind=kOutput, calls=%fused_computation.201 | convolution fusion | flops 536870912 | bytes 6422528 | tf_op jit(solution)/shard_map/dot_general | solution.py:63
  62.4 0.7 convolution_add_fusion.1
  63.2 0.8 copy-done.16
  64.0 4.5 %convert_reduce_fusion = (f32[32]{0:T(128)S(1)}, bf16[8,1,32,4096]{3,2,0,1:T(8,128)(2,1)S(1)}, f32[8,32,4096]{2,1,0:T(8,128)}) fusion(bf16[8,1,32,4096]{3,2,1,0:T(8,128)(2,1)S(1)} %copy-done.16, f32[32]{0:T(128)S(1)} %copy-done.17, f32[8,32,4096]{2,1,0:T(8,128)S(1)} %bitcast.135, bf16[32,32]{1,0:T(8,128)(2,1)S(1)} %copy-done.8, ...), kind=kOutput, calls=%fused_computation.19 | convolution fusion | flops 82837472 | bytes 14682368 | tf_op jit(solution)/shard_map/io,riy->roy/dot_general | solution.py:130
  68.5 1.3 copy-done.4
  69.9 0.9 convolution_bitcast_fusion.4
  70.7 0.1 copy.76
  70.9 0.1 reshape.298
  71.0 3.7 %fusion.25 = f32[256,8,32]{0,1,2:T(8,128)S(1)} fusion(bf16[256,4096]{1,0:T(8,128)(2,1)} %copy-done.1, bf16[8,32,4096]{2,1,0:T(8,128)(2,1)} %bitcast.134), kind=kOutput, calls=%fused_computation.34 | convolution fusion | flops 536870912 | bytes 4456448 | tf_op jit(solution)/shard_map/qc,rc->qr/dot_general | solution.py:73
  74.7 0.5 fusion.77
  75.3 0.4 copy.75
  75.6 0.3 reshape.296
  76.0 1.1 select_maximum_fusion
  77.1 6.6 %all-to-all-start.2 = ((f32[256,3,128]{2,1,0:T(4,128)}), f32[256,3,128]{2,1,0:T(4,128)S(1)}, u32[]{:S(2)}, u32[]{:S(2)}) async-start(f32[256,3,128]{2,1,0:T(4,128)} %select_maximum_fusion), calls=%async_computation.2 | async-start | bytes 1048576 | tf_op jit(solution)/shard_map/all_to_all | solution.py:82
  83.7 0.9 copy.83
  84.6 18.2 %all-to-all-done.2 = f32[256,3,128]{2,1,0:T(4,128)S(1)} async-done(((f32[256,3,128]{2,1,0:T(4,128)}), f32[256,3,128]{2,1,0:T(4,128)S(1)}, u32[]{:S(2)}, u32[]{:S(2)}) %all-to-all-start.2) | async-done | bytes 393248 | tf_op jit(solution)/shard_map/all_to_all | solution.py:82
  102.8 0.1 bitcast_reduce_fusion
  102.9 0.1 copy.78
  103.0 0.7 fusion.66
  103.7 3.0 %fusion.48 = f32[16,8,1,32]{3,2,1,0:T(1,128)S(1)} fusion(bf16[16,8,32,32]{3,2,1,0:T(8,128)(2,1)} %copy-done.6, f32[16,8,32,1]{2,0,1,3:T(8,128)S(1)} %bitcast.145), kind=kOutput, calls=%fused_computation.82 | convolution fusion | flops 1572864 | bytes 294912 | tf_op jit(solution)/shard_map/kqio,kqo->kqi/dot_general | solution.py:148
  106.7 0.1 reshape.300
  106.8 0.4 fusion.52
  107.2 0.3 slice_reduce_fusion
  107.5 0.9 broadcast_in_dim.42
  108.4 7.1 %all-to-all-start.3 = ((f32[256,3,128]{2,1,0:T(4,128)}), f32[256,3,128]{2,1,0:T(4,128)S(1)}, u32[]{:S(2)}, u32[]{:S(2)}) async-start(f32[256,3,128]{2,1,0:T(4,128)} %bitcast.35), calls=%async_computation.3 | async-start | bytes 1048576 | tf_op jit(solution)/shard_map/all_to_all | solution.py:104
  115.5 3.6 %fusion.24 = bf16[8,1,32,4096]{3,2,1,0:T(8,128)(2,1)} fusion(f32[8,32,4096]{2,1,0:T(8,128)} %get-tuple-element.69), kind=kLoop, calls=%fused_computation.33 | loop fusion | flops 5242880 | bytes 6291456
  119.2 1.7 %multiply_multiply_fusion.1 = f32[16,8,32,32]{3,2,1,0:T(8,128)} fusion(f32[16,8,32]{2,1,0:T(8,128)S(1)} %copy.84, f32[16,8,32]{2,1,0:T(8,128)S(1)} %copy.83), kind=kLoop, calls=%fused_computation.40 | loop fusion | flops 262144 | bytes 557056 | tf_op jit(solution)/shard_map/mul | solution.py:145
  120.9 3.1 %reshape.305 = f32[16,8,1024]{2,1,0:T(8,128)} reshape(f32[16,8,32,32]{3,2,1,0:T(8,128)} %multiply_multiply_fusion.1) | data formatting | bytes 1048576 | tf_op jit(solution)/shard_map/reshape | solution.py:145
  124.0 10.6 %all-to-all-done.3 = f32[256,3,128]{2,1,0:T(4,128)S(1)} async-done(((f32[256,3,128]{2,1,0:T(4,128)}), f32[256,3,128]{2,1,0:T(4,128)S(1)}, u32[]{:S(2)}, u32[]{:S(2)}) %all-to-all-start.3) | async-done | bytes 393248 | tf_op jit(solution)/shard_map/all_to_all | solution.py:104
  134.6 0.6 mul.246
  135.2 0.2 fusion.47
  135.4 0.7 mul.243
  136.1 0.1 slice.73
  136.2 0.4 reshape.302
  136.7 0.3 copy.81
  137.0 0.5 convolution_bitcast_fusion.2
  137.5 0.1 copy.82
  137.6 2.5 %fusion.144 = f32[256,4096]{1,0:T(8,128)S(1)} fusion(bf16[256,256]{1,0:T(8,128)(2,1)S(1)} %get-tuple-element.58, bf16[256,4096]{1,0:T(8,128)(2,1)} %copy-done.1), kind=kOutput, calls=%fused_computation.202 | convolution fusion | flops 536870912 | bytes 6422528 | tf_op jit(solution)/shard_map/dot_general | solution.py:63
  140.1 0.8 convolution_add_fusion
  140.9 0.8 copy-done.5
  141.7 2.0 %fusion.5 = bf16[8,1,32,4096]{3,2,1,0:T(8,128)(2,1)} fusion(f32[8,32,4096]{2,1,0:T(8,128)S(1)} %bitcast.133, bf16[32,32]{1,0:T(8,128)(2,1)S(1)} %copy-done.8, bf16[8,1,32,4096]{3,2,0,1:T(8,128)(2,1)S(1)} %copy-done.5), kind=kOutput, calls=%fused_computation.11 | convolution fusion | flops 69206016 | bytes 8390656 | tf_op jit(solution)/shard_map/io,roy->riy/dot_general | solution.py:155
  (53 shorter events, 0.6 us)
Async XLA Ops:
  0.6 2.2 %copy-start = (bf16[8,1,32,4096]{3,2,1,0:T(8,128)(2,1)S(1)}, bf16[8,1,32,4096]{3,2,1,0:T(8,128)(2,1)}, u32[]{:S(2)}) copy-start(bf16[8,1,32,4096]{3,2,1,0:T(8,128)(2,1)} %param.9) | copy-start | bytes 6291460
  0.7 36.7 %copy-start.12 = (pred[16]{0:T(512)(128)(4,1)}, pred[16]{0:T(512)(128)(4,1)S(1)}, u32[]{:S(2)}) copy-start(pred[16]{0:T(512)(128)(4,1)S(1)} %iota_compare_fusion.5) | copy-start | bytes 52
  0.7 36.6 %copy-start.14 = (s32[16]{0:T(128)}, s32[16]{0:T(128)S(1)}, u32[]{:S(2)}) copy-start(s32[16]{0:T(128)S(1)} %add_select_fusion.5) | copy-start | bytes 196
  0.7 58.6 %copy-start.9 = (s32[8]{0:T(128)}, s32[8]{0:T(128)S(1)}, u32[]{:S(2)}) copy-start(s32[8]{0:T(128)S(1)} %get-tuple-element.76) | copy-start | bytes 100
  2.9 1.5 %copy-start.1 = (bf16[256,4096]{1,0:T(8,128)(2,1)}, bf16[256,4096]{1,0:T(8,128)(2,1)S(1)}, u32[]{:S(2)}) copy-start(bf16[256,4096]{1,0:T(8,128)(2,1)S(1)} %fusion.3) | copy-start | bytes 6291460
  6.3 28.4 %all-to-all-start = ((f32[256,2,128]{2,1,0:T(2,128)}), f32[256,2,128]{2,1,0:T(2,128)S(1)}, u32[]{:S(2)}, u32[]{:S(2)}) async-start(f32[256,2,128]{2,1,0:T(2,128)} %reshape.288), calls=%async_computation | async-start | bytes 524288 | tf_op jit(solution)/shard_map/all_to_all | solution.py:82
  22.8 15.1 %copy-start.6 = (bf16[16,8,32,32]{3,2,1,0:T(8,128)(2,1)}, bf16[16,8,32,32]{3,2,1,0:T(8,128)(2,1)S(1)}, u32[]{:S(2)}) copy-start(bf16[16,8,32,32]{3,2,1,0:T(8,128)(2,1)S(1)} %reshape.290) | copy-start | bytes 786436
  35.6 0.6 copy-start.7
  59.9 2.5 %copy-start.2 = (bf16[256,4096]{1,0:T(8,128)(2,1)S(1)}, bf16[256,4096]{1,0:T(8,128)(2,1)}, u32[]{:S(2)}) copy-start(bf16[256,4096]{1,0:T(8,128)(2,1)} %copy-done.1) | copy-start | bytes 6291460
  62.4 0.8 copy-start.8
  62.4 1.6 %copy-start.16 = (bf16[8,1,32,4096]{3,2,1,0:T(8,128)(2,1)S(1)}, bf16[8,1,32,4096]{3,2,1,0:T(8,128)(2,1)}, u32[]{:S(2)}) copy-start(bf16[8,1,32,4096]{3,2,1,0:T(8,128)(2,1)} %param.13) | copy-start | bytes 6291460
  62.4 1.6 %copy-start.17 = (f32[32]{0:T(128)S(1)}, f32[32]{0:T(128)}, u32[]{:S(2)}) copy-start(f32[32]{0:T(128)} %param.12) | copy-start | bytes 388
  68.5 1.3 copy-start.4
  71.0 3.7 %copy-start.10 = (s32[8]{0:T(128)S(1)}, s32[8]{0:T(128)}, u32[]{:S(2)}) copy-start(s32[8]{0:T(128)} %copy-done.9) | copy-start | bytes 100
  76.0 27.0 %copy-start.13 = (pred[16]{0:T(512)(128)(4,1)S(1)}, pred[16]{0:T(512)(128)(4,1)}, u32[]{:S(2)}) copy-start(pred[16]{0:T(512)(128)(4,1)} %copy-done.12) | copy-start | bytes 52
  76.0 27.0 %copy-start.15 = (s32[16]{0:T(128)S(1)}, s32[16]{0:T(128)}, u32[]{:S(2)}) copy-start(s32[16]{0:T(128)} %copy-done.14) | copy-start | bytes 196
  77.1 25.7 %all-to-all-start.2 = ((f32[256,3,128]{2,1,0:T(4,128)}), f32[256,3,128]{2,1,0:T(4,128)S(1)}, u32[]{:S(2)}, u32[]{:S(2)}) async-start(f32[256,3,128]{2,1,0:T(4,128)} %select_maximum_fusion), calls=%async_computation.2 | async-start | bytes 1048576 | tf_op jit(solution)/shard_map/all_to_all | solution.py:82
  108.4 26.2 %all-to-all-start.3 = ((f32[256,3,128]{2,1,0:T(4,128)}), f32[256,3,128]{2,1,0:T(4,128)S(1)}, u32[]{:S(2)}, u32[]{:S(2)}) async-start(f32[256,3,128]{2,1,0:T(4,128)} %bitcast.35), calls=%async_computation.3 | async-start | bytes 1048576 | tf_op jit(solution)/shard_map/all_to_all | solution.py:104
  124.0 13.0 %copy-start.11 = (s32[8]{0:T(128)S(1)}, s32[8]{0:T(128)}, u32[]{:S(2)}) copy-start(s32[8]{0:T(128)} %copy-done.9) | copy-start | bytes 100
  137.6 2.5 %copy-start.3 = (bf16[256,4096]{1,0:T(8,128)(2,1)S(1)}, bf16[256,4096]{1,0:T(8,128)(2,1)}, u32[]{:S(2)}) copy-start(bf16[256,4096]{1,0:T(8,128)(2,1)} %copy-done.1) | copy-start | bytes 6291460
  140.1 1.6 %copy-start.5 = (bf16[8,1,32,4096]{3,2,0,1:T(8,128)(2,1)S(1)}, bf16[8,1,32,4096]{3,2,0,1:T(8,128)(2,1)}, u32[]{:S(2)}) copy-start(bf16[8,1,32,4096]{3,2,0,1:T(8,128)(2,1)} %copy-done.4) | copy-start | bytes 6291460

commit v7 on v6

--- a/solution.py
+++ b/solution.py
@@ -88,7 +88,7 @@
     return owned, jnp.sum(arrived[:, rows_per, :own], axis=0)
 
 
-def to_planes(block, x_table, time_table, yz_table, steps_here, extra=None):
+def to_planes(block, x_table, time_table, yz_table, steps_here, extra=None, one_pass=False):
     channels = block.shape[2]
     sp_count, ch_count = lax.axis_size("sp"), lax.axis_size("ch")
     own = block.shape[1]
@@ -107,7 +107,11 @@
     total = returned[:, rows_per, :own].reshape(-1) if extra is not None else None
     modes = returned[:, :rows_per].reshape(KT, KYZ, channels)
     time_spread = jnp.einsum("kt,kpo->top", time_table, modes, precision=PRECISE)
-    result = split_dot(time_spread.reshape(-1, KYZ), yz_table)
+    time_spread = time_spread.reshape(-1, KYZ)
+    if one_pass:
+        result = jnp.dot(time_spread.astype(jnp.bfloat16), yz_table, preferred_element_type=jnp.float32)
+    else:
+        result = split_dot(time_spread, yz_table)
     return result.reshape(steps_here, 1, channels, -1), total
 
 
@@ -147,7 +151,7 @@
     )
     coeff_grad = jnp.einsum("kqio,kqo->kqi", weights, slope_modes, precision=PRECISE)
     grad_spatial, packed_sum = to_planes(
-        coeff_grad, forward_x, forward_t, yz_table, steps_here, extra=packed_part
+        coeff_grad, forward_x, forward_t, yz_table, steps_here, extra=packed_part, one_pass=True
     )
     cell_scale = 1.0 / math.sqrt(grid_x * GY * GZ * GT)
     weight_grad = cell_scale * packed_sum[: channels * channels].reshape(channels, channels)

time: 147 us -> 145 us (0.986)
    dot_general x2 -> x1, matrix products: 4.91 us -> 2.46 us  [split_dot(): jnp.dot(high.astype(jnp.bfloat16), table, preferred_element_type=jnp.floa...]
    dot_general x0 -> x1, matrix products: none -> 2.45 us  [to_planes(): jnp.dot(time_spread.astype(jnp.bfloat16), yz_table, preferred_element_typ...]
    unnamed x36 -> x34, local copies, waits for them, and re-layouts: 3.71 us -> 2.89 us
where the time goes in v7:
time: 145 us; the launch traced here: 142 us
  waiting for transfers between devices  40.8 us (28%)
  starting transfers between devices  28.3 us (20%)
  matrix products  27.8 us (19%)
  blocking collectives  20.6 us (14%)
  local copies, waits for them, and re-layouts  15.6 us (11%)
  other arithmetic  7.71 us (5%)
    all_to_all x2, waiting for transfers between devices, to_spectrum(): arrived = lax.all_to_all(send, ('sp', 'ch'), 0, 0, tiled=True)  30.2 us
    all_to_all x2, starting transfers between devices, to_spectrum(): arrived = lax.all_to_all(send, ('sp', 'ch'), 0, 0, tiled=True)  21.2 us
    all_to_all x1, blocking collectives, to_planes(): lax.all_to_all(copies.reshape((-1,) + spread.shape[1:]), ('sp', 'ch'), 0,...  20.6 us
    all_to_all x1, waiting for transfers between devices, to_planes(): lax.all_to_all(copies.reshape((-1,) + spread.shape[1:]), ('sp', 'ch'), 0,...  10.6 us
    all_to_all x1, starting transfers between devices, to_planes(): lax.all_to_all(copies.reshape((-1,) + spread.shape[1:]), ('sp', 'ch'), 0,...  7.1 us
    dot_general x2, matrix products, to_spectrum(): jnp.einsum('qc,rc->qr', yz_table, values.reshape(-1, plane_cells), prefer...  5.17 us
    dot_general x1, matrix products, shards(): jnp.einsum('io,riy->roy', point_weight, field_rows, preferred_element_typ...  4.51 us
    unnamed x1, other arithmetic  3.6 us
  transfers between devices with their start and end apart: 3, of which 3 were waited for; matrix products, arithmetic and copies ran while one was open for 8% of the time, Pallas kernels for 0%

profile of v7, /device:TPU:8, one launch (start us, length us, event | category | flops | bytes accessed | tf_op | source)
XLA Modules:
  0.0 142.0 jit_solution(10818850883613906570)
XLA Ops:
  0.7 0.1 broadcast_multiply_fusion
  0.9 0.1 reduce-precision_convert_fusion.2
  1.0 0.3 iota_compare_fusion
  1.3 0.8 fusion.13
  2.1 0.8 fusion.3
  2.9 1.5 %fusion.29 = f32[256,8,32]{0,1,2:T(8,128)S(1)} fusion(bf16[256,4096]{1,0:T(8,128)(2,1)S(1)} %fusion.3, bf16[8,32,4096]{2,1,0:T(8,128)(2,1)S(1)} %bitcast.126), kind=kOutput, calls=%fused_computation.37 | convolution fusion | flops 536870912 | bytes 4456448 | tf_op jit(solution)/shard_map/qc,rc->qr/dot_general | solution.py:73
  4.4 0.5 fusion.84
  4.9 0.4 copy.61
  5.3 1.0 reshape.285
  6.3 14.6 %all-to-all-start = ((f32[256,2,128]{2,1,0:T(2,128)}), f32[256,2,128]{2,1,0:T(2,128)S(1)}, u32[]{:S(2)}, u32[]{:S(2)}) async-start(f32[256,2,128]{2,1,0:T(2,128)} %reshape.285), calls=%async_computation | async-start | bytes 524288 | tf_op jit(solution)/shard_map/all_to_all | solution.py:82
  20.9 1.8 %reshape.287 = bf16[16,8,32,32]{3,2,1,0:T(8,128)(2,1)S(1)} reshape(bf16[16,8,1024]{2,1,0:T(8,128)(2,1)} %param.10) | data formatting | bytes 524288 | tf_op jit(solution)/shard_map/reshape | solution.py:130
  22.8 12.0 %all-to-all-done = f32[256,2,128]{2,1,0:T(2,128)S(1)} async-done(((f32[256,2,128]{2,1,0:T(2,128)}), f32[256,2,128]{2,1,0:T(2,128)S(1)}, u32[]{:S(2)}, u32[]{:S(2)}) %all-to-all-start) | async-done | bytes 262176 | tf_op jit(solution)/shard_map/all_to_all | solution.py:82
  34.8 0.1 bitcast_reduce_fusion.1
  34.8 0.1 copy.62
  35.0 0.7 fusion.67
  35.6 0.6 copy-done.6
  36.3 0.9 fusion.53
  37.2 0.1 reshape.288
  37.3 0.4 fusion.57
  37.9 20.6 %all_to_all.20 = f32[256,2,128]{2,1,0:T(2,128)S(1)} all-to-all(f32[256,2,128]{2,1,0:T(2,128)S(1)} %bitcast.129), channel_id=1, replica_groups=mesh['sp'=64,'ch'=4] {'sp','ch'}, dimensions={0} | all-to-all | bytes 524288 | tf_op jit(solution)/shard_map/all_to_all | solution.py:104
  58.5 0.4 reshape.290
  59.0 0.3 copy.65
  59.3 0.5 convolution_bitcast_fusion.2
  59.8 0.1 copy.66
  59.9 2.5 %fusion.146 = f32[256,4096]{1,0:T(8,128)S(1)} fusion(bf16[256,256]{1,0:T(8,128)(2,1)S(1)} %get-tuple-element.58, bf16[256,4096]{1,0:T(8,128)(2,1)} %copy-done.1), kind=kOutput, calls=%fused_computation.201 | convolution fusion | flops 536870912 | bytes 6422528 | tf_op jit(solution)/shard_map/dot_general | solution.py:63
  62.4 0.7 convolution_add_fusion
  63.2 0.8 copy-done.15
  64.0 4.5 %convert_reduce_fusion = (f32[32]{0:T(128)S(1)}, bf16[8,1,32,4096]{3,2,0,1:T(8,128)(2,1)S(1)}, f32[8,32,4096]{2,1,0:T(8,128)}) fusion(bf16[8,1,32,4096]{3,2,1,0:T(8,128)(2,1)S(1)} %copy-done.15, f32[32]{0:T(128)S(1)} %copy-done.16, f32[8,32,4096]{2,1,0:T(8,128)S(1)} %bitcast.128, bf16[32,32]{1,0:T(8,128)(2,1)S(1)} %copy-done.7, ...), kind=kOutput, calls=%fused_computation.18 | convolution fusion | flops 82837472 | bytes 14682368 | tf_op jit(solution)/shard_map/io,riy->roy/dot_general | solution.py:134
  68.5 1.3 copy-done.3
  69.9 0.9 convolution_bitcast_fusion.3
  70.7 0.1 copy.72
  70.8 0.1 reshape.294
  70.9 0.1 reshape.295
  71.0 3.7 %fusion.27 = f32[256,8,32]{0,1,2:T(8,128)S(1)} fusion(bf16[256,4096]{1,0:T(8,128)(2,1)} %copy-done.1, bf16[8,32,4096]{2,1,0:T(8,128)(2,1)} %bitcast.127), kind=kOutput, calls=%fused_computation.35 | convolution fusion | flops 536870912 | bytes 4456448 | tf_op jit(solution)/shard_map/qc,rc->qr/dot_general | solution.py:73
  74.7 0.5 fusion.80
  75.3 0.4 copy.71
  75.6 0.3 reshape.293
  76.0 1.1 select_maximum_fusion
  77.1 6.6 %all-to-all-start.2 = ((f32[256,3,128]{2,1,0:T(4,128)}), f32[256,3,128]{2,1,0:T(4,128)S(1)}, u32[]{:S(2)}, u32[]{:S(2)}) async-start(f32[256,3,128]{2,1,0:T(4,128)} %select_maximum_fusion), calls=%async_computation.2 | async-start | bytes 1048576 | tf_op jit(solution)/shard_map/all_to_all | solution.py:82
  83.7 0.9 copy.79
  84.6 18.2 %all-to-all-done.2 = f32[256,3,128]{2,1,0:T(4,128)S(1)} async-done(((f32[256,3,128]{2,1,0:T(4,128)}), f32[256,3,128]{2,1,0:T(4,128)S(1)}, u32[]{:S(2)}, u32[]{:S(2)}) %all-to-all-start.2) | async-done | bytes 393248 | tf_op jit(solution)/shard_map/all_to_all | solution.py:82
  102.8 0.1 bitcast_reduce_fusion
  102.9 0.1 copy.74
  103.0 0.7 fusion.69
  103.7 3.0 %fusion.51 = f32[16,8,1,32]{3,2,1,0:T(1,128)S(1)} fusion(bf16[16,8,32,32]{3,2,1,0:T(8,128)(2,1)} %copy-done.5, f32[16,8,32,1]{2,0,1,3:T(8,128)S(1)} %bitcast.138), kind=kOutput, calls=%fused_computation.82 | convolution fusion | flops 1572864 | bytes 294912 | tf_op jit(solution)/shard_map/kqio,kqo->kqi/dot_general | solution.py:152
  106.7 0.1 reshape.297
  106.8 0.4 fusion.55
  107.2 0.3 slice_reduce_fusion
  107.5 0.1 copy.76
  107.6 0.9 broadcast_in_dim.42
  108.4 7.1 %all-to-all-start.3 = ((f32[256,3,128]{2,1,0:T(4,128)}), f32[256,3,128]{2,1,0:T(4,128)S(1)}, u32[]{:S(2)}, u32[]{:S(2)}) async-start(f32[256,3,128]{2,1,0:T(4,128)} %bitcast.35), calls=%async_computation.3 | async-start | bytes 1048576 | tf_op jit(solution)/shard_map/all_to_all | solution.py:104
  115.6 3.6 %fusion.24 = bf16[8,1,32,4096]{3,2,1,0:T(8,128)(2,1)} fusion(f32[8,32,4096]{2,1,0:T(8,128)} %get-tuple-element.67), kind=kLoop, calls=%fused_computation.32 | loop fusion | flops 5242880 | bytes 6291456
  119.2 1.7 %multiply_multiply_fusion.1 = f32[16,8,32,32]{3,2,1,0:T(8,128)} fusion(f32[16,8,32]{2,1,0:T(8,128)S(1)} %copy.80, f32[16,8,32]{2,1,0:T(8,128)S(1)} %copy.79), kind=kLoop, calls=%fused_computation.41 | loop fusion | flops 262144 | bytes 557056 | tf_op jit(solution)/shard_map/mul | solution.py:149
  120.9 3.1 %reshape.300 = f32[16,8,1024]{2,1,0:T(8,128)} reshape(f32[16,8,32,32]{3,2,1,0:T(8,128)} %multiply_multiply_fusion.1) | data formatting | bytes 1048576 | tf_op jit(solution)/shard_map/reshape | solution.py:149
  124.0 10.6 %all-to-all-done.3 = f32[256,3,128]{2,1,0:T(4,128)S(1)} async-done(((f32[256,3,128]{2,1,0:T(4,128)}), f32[256,3,128]{2,1,0:T(4,128)S(1)}, u32[]{:S(2)}, u32[]{:S(2)}) %all-to-all-start.3) | async-done | bytes 393248 | tf_op jit(solution)/shard_map/all_to_all | solution.py:104
  134.6 0.6 mul.246
  135.2 0.2 fusion.50
  135.5 0.7 mul.243
  136.2 0.1 slice.73
  136.2 0.4 reshape.299
  136.7 0.3 copy.77
  137.0 0.5 fusion.33
  137.5 2.5 %fusion.25 = f32[8,32,4096]{2,1,0:T(8,128)S(1)} fusion(bf16[256,4096]{1,0:T(8,128)(2,1)} %copy-done.1, bf16[8,32,256]{2,0,1:T(8,128)(2,1)S(1)} %fusion.33), kind=kOutput, calls=%fused_computation.33 | convolution fusion | flops 536870912 | bytes 6422528 | tf_op jit(solution)/shard_map/dot_general | solution.py:112
  140.0 2.0 %fusion.5 = bf16[8,1,32,4096]{3,2,1,0:T(8,128)(2,1)} fusion(f32[8,32,4096]{2,1,0:T(8,128)S(1)} %fusion.25, bf16[32,32]{1,0:T(8,128)(2,1)S(1)} %copy-done.7, bf16[8,1,32,4096]{3,2,0,1:T(8,128)(2,1)S(1)} %copy-done.4), kind=kOutput, calls=%fused_computation.10 | convolution fusion | flops 69206016 | bytes 8390656 | tf_op jit(solution)/shard_map/io,roy->riy/dot_general | solution.py:159
  (48 shorter events, 0.4 us)
Async XLA Ops:
  0.6 2.2 %copy-start = (bf16[8,1,32,4096]{3,2,1,0:T(8,128)(2,1)S(1)}, bf16[8,1,32,4096]{3,2,1,0:T(8,128)(2,1)}, u32[]{:S(2)}) copy-start(bf16[8,1,32,4096]{3,2,1,0:T(8,128)(2,1)} %param.9) | copy-start | bytes 6291460
  0.7 36.7 %copy-start.11 = (pred[16]{0:T(512)(128)(4,1)}, pred[16]{0:T(512)(128)(4,1)S(1)}, u32[]{:S(2)}) copy-start(pred[16]{0:T(512)(128)(4,1)S(1)} %iota_compare_fusion.5) | copy-start | bytes 52
  0.7 36.6 %copy-start.13 = (s32[16]{0:T(128)}, s32[16]{0:T(128)S(1)}, u32[]{:S(2)}) copy-start(s32[16]{0:T(128)S(1)} %add_select_fusion.5) | copy-start | bytes 196
  0.7 58.6 %copy-start.8 = (s32[8]{0:T(128)}, s32[8]{0:T(128)S(1)}, u32[]{:S(2)}) copy-start(s32[8]{0:T(128)S(1)} %get-tuple-element.74) | copy-start | bytes 100
  2.9 1.5 %copy-start.1 = (bf16[256,4096]{1,0:T(8,128)(2,1)}, bf16[256,4096]{1,0:T(8,128)(2,1)S(1)}, u32[]{:S(2)}) copy-start(bf16[256,4096]{1,0:T(8,128)(2,1)S(1)} %fusion.3) | copy-start | bytes 6291460
  6.3 28.4 %all-to-all-start = ((f32[256,2,128]{2,1,0:T(2,128)}), f32[256,2,128]{2,1,0:T(2,128)S(1)}, u32[]{:S(2)}, u32[]{:S(2)}) async-start(f32[256,2,128]{2,1,0:T(2,128)} %reshape.285), calls=%async_computation | async-start | bytes 524288 | tf_op jit(solution)/shard_map/all_to_all | solution.py:82
  22.8 15.1 %copy-start.5 = (bf16[16,8,32,32]{3,2,1,0:T(8,128)(2,1)}, bf16[16,8,32,32]{3,2,1,0:T(8,128)(2,1)S(1)}, u32[]{:S(2)}) copy-start(bf16[16,8,32,32]{3,2,1,0:T(8,128)(2,1)S(1)} %reshape.287) | copy-start | bytes 786436
  35.6 0.6 copy-start.6
  59.9 2.5 %copy-start.2 = (bf16[256,4096]{1,0:T(8,128)(2,1)S(1)}, bf16[256,4096]{1,0:T(8,128)(2,1)}, u32[]{:S(2)}) copy-start(bf16[256,4096]{1,0:T(8,128)(2,1)} %copy-done.1) | copy-start | bytes 6291460
  62.4 0.8 copy-start.7
  62.4 1.6 %copy-start.15 = (bf16[8,1,32,4096]{3,2,1,0:T(8,128)(2,1)S(1)}, bf16[8,1,32,4096]{3,2,1,0:T(8,128)(2,1)}, u32[]{:S(2)}) copy-start(bf16[8,1,32,4096]{3,2,1,0:T(8,128)(2,1)} %param.13) | copy-start | bytes 6291460
  62.4 1.6 %copy-start.16 = (f32[32]{0:T(128)S(1)}, f32[32]{0:T(128)}, u32[]{:S(2)}) copy-start(f32[32]{0:T(128)} %param.12) | copy-start | bytes 388
  68.5 1.3 copy-start.3
  71.0 3.7 %copy-start.9 = (s32[8]{0:T(128)S(1)}, s32[8]{0:T(128)}, u32[]{:S(2)}) copy-start(s32[8]{0:T(128)} %copy-done.8) | copy-start | bytes 100
  76.0 27.0 %copy-start.12 = (pred[16]{0:T(512)(128)(4,1)S(1)}, pred[16]{0:T(512)(128)(4,1)}, u32[]{:S(2)}) copy-start(pred[16]{0:T(512)(128)(4,1)} %copy-done.11) | copy-start | bytes 52
  76.0 27.0 %copy-start.14 = (s32[16]{0:T(128)S(1)}, s32[16]{0:T(128)}, u32[]{:S(2)}) copy-start(s32[16]{0:T(128)} %copy-done.13) | copy-start | bytes 196
  77.1 25.7 %all-to-all-start.2 = ((f32[256,3,128]{2,1,0:T(4,128)}), f32[256,3,128]{2,1,0:T(4,128)S(1)}, u32[]{:S(2)}, u32[]{:S(2)}) async-start(f32[256,3,128]{2,1,0:T(4,128)} %select_maximum_fusion), calls=%async_computation.2 | async-start | bytes 1048576 | tf_op jit(solution)/shard_map/all_to_all | solution.py:82
  108.4 26.2 %all-to-all-start.3 = ((f32[256,3,128]{2,1,0:T(4,128)}), f32[256,3,128]{2,1,0:T(4,128)S(1)}, u32[]{:S(2)}, u32[]{:S(2)}) async-start(f32[256,3,128]{2,1,0:T(4,128)} %bitcast.35), calls=%async_computation.3 | async-start | bytes 1048576 | tf_op jit(solution)/shard_map/all_to_all | solution.py:104
  124.0 13.0 %copy-start.10 = (s32[8]{0:T(128)S(1)}, s32[8]{0:T(128)}, u32[]{:S(2)}) copy-start(s32[8]{0:T(128)} %copy-done.8) | copy-start | bytes 100
  137.5 2.5 %copy-start.4 = (bf16[8,1,32,4096]{3,2,0,1:T(8,128)(2,1)S(1)}, bf16[8,1,32,4096]{3,2,0,1:T(8,128)(2,1)}, u32[]{:S(2)}) copy-start(bf16[8,1,32,4096]{3,2,0,1:T(8,128)(2,1)} %copy-done.3) | copy-start | bytes 6291460

commit v8 on v7

--- a/solution.py
+++ b/solution.py
@@ -131,8 +131,8 @@
     mixed_modes = jnp.einsum("kqi,kqio->kqo", coeffs, weights, precision=PRECISE)
     spatial, _ = to_planes(mixed_modes, inverse_x, inverse_t4, yz_table, steps_here)
     field_rows = field.reshape(-1, channels, plane_cells)
-    linear = jnp.einsum(
-        "io,riy->roy", point_weight, field_rows, preferred_element_type=jnp.float32
+    linear = lax.optimization_barrier(
+        jnp.einsum("io,riy->roy", point_weight, field_rows, preferred_element_type=jnp.float32)
     ).reshape(spatial.shape)
     preact = spatial + linear + bias[None, None, :, None]
     normal_cdf = 0.5 * (1.0 + lax.erf(preact * SQRT_HALF))

time: 145 us -> 148 us (1.021)
  blocking collectives: 20.6 us -> 0 us
  waiting for transfers between devices: 40.8 us -> 50.5 us
  starting transfers between devices: 28.3 us -> 35.3 us
  other arithmetic: 7.71 us -> 11.8 us
  local copies, waits for them, and re-layouts: 15.6 us -> 19 us
    all_to_all x1 -> x0, blocking collectives: 20.6 us -> none  [to_planes(): lax.all_to_all(copies.reshape((-1,) + spread.shape[1:]), ('sp', 'ch'), 0,...]
    all_to_all x1 -> x2, waiting for transfers between devices: 10.6 us -> 20.3 us  [to_planes(): lax.all_to_all(copies.reshape((-1,) + spread.shape[1:]), ('sp', 'ch'), 0,...]
    all_to_all x1 -> x2, starting transfers between devices: 7.1 us -> 13.9 us  [to_planes(): lax.all_to_all(copies.reshape((-1,) + spread.shape[1:]), ('sp', 'ch'), 0,...]
    unnamed x34 -> x36, local copies, waits for them, and re-layouts: 2.89 us -> 5.62 us
    reduce_sum x0 -> x1, other arithmetic: none -> 2.67 us  [shards(): bias_part = jnp.sum(slopes.astype(jnp.float32), axis=(0, 1, 3))]
    dot_general x1, matrix products: 4.51 us -> 2.76 us  [shards(): jnp.einsum('io,riy->roy', point_weight, field_rows, preferred_element_typ...]
  transfers between devices with their start and end apart: 3 -> 4, of which waited for: 3 -> 4; matrix products, arithmetic and copies ran while one was open for 8% -> 11% of each run, Pallas kernels for 0% -> 0%
where the time goes in v8:
time: 148 us; the launch traced here: 145 us
  waiting for transfers between devices  50.5 us (34%)
  starting transfers between devices  35.3 us (24%)
  matrix products  27.4 us (19%)
  local copies, waits for them, and re-layouts  19 us (13%)
  other arithmetic  11.8 us (8%)
    all_to_all x2, waiting for transfers between devices, to_spectrum(): arrived = lax.all_to_all(send, ('sp', 'ch'), 0, 0, tiled=True)  30.2 us
    all_to_all x2, starting transfers between devices, to_spectrum(): arrived = lax.all_to_all(send, ('sp', 'ch'), 0, 0, tiled=True)  21.4 us
    all_to_all x2, waiting for transfers between devices, to_planes(): lax.all_to_all(copies.reshape((-1,) + spread.shape[1:]), ('sp', 'ch'), 0,...  20.3 us
    all_to_all x2, starting transfers between devices, to_planes(): lax.all_to_all(copies.reshape((-1,) + spread.shape[1:]), ('sp', 'ch'), 0,...  13.9 us
    unnamed x36, local copies, waits for them, and re-layouts  5.62 us
    dot_general x2, matrix products, to_spectrum(): jnp.einsum('qc,rc->qr', yz_table, values.reshape(-1, plane_cells), prefer...  5.17 us
    unnamed x1, other arithmetic  5.03 us
    reshape x1, local copies, waits for them, and re-layouts, shards(): (spec_scale * jnp.einsum('kqi,kqo->kqio', coeffs, slope_modes)).reshape(K...  3.07 us
  transfers between devices with their start and end apart: 4, of which 4 were waited for; matrix products, arithmetic and copies ran while one was open for 11% of the time, Pallas kernels for 0%

profile of v8, /device:TPU:8, one launch (start us, length us, event | category | flops | bytes accessed | tf_op | source)
XLA Modules:
  0.0 145.2 jit_solution(15064302346181465049)
XLA Ops:
  0.7 0.1 broadcast_multiply_fusion
  1.0 0.3 iota_compare_fusion
  1.3 0.8 fusion.11
  2.1 0.8 fusion.1
  2.9 1.5 %fusion.27 = f32[256,8,32]{0,1,2:T(8,128)S(1)} fusion(bf16[256,4096]{1,0:T(8,128)(2,1)S(1)} %fusion.1, bf16[8,32,4096]{2,1,0:T(8,128)(2,1)S(1)} %bitcast.119), kind=kOutput, calls=%fused_computation.36 | convolution fusion | flops 536870912 | bytes 4456448 | tf_op jit(solution)/shard_map/qc,rc->qr/dot_general | solution.py:73
  4.4 0.5 fusion.82
  4.9 0.4 copy.61
  5.3 1.0 reshape.285
  6.3 14.6 %all-to-all-start = ((f32[256,2,128]{2,1,0:T(2,128)}), f32[256,2,128]{2,1,0:T(2,128)S(1)}, u32[]{:S(2)}, u32[]{:S(2)}) async-start(f32[256,2,128]{2,1,0:T(2,128)} %reshape.285), calls=%async_computation | async-start | bytes 524288 | tf_op jit(solution)/shard_map/all_to_all | solution.py:82
  20.9 1.8 %reshape.287 = bf16[16,8,32,32]{3,2,1,0:T(8,128)(2,1)S(1)} reshape(bf16[16,8,1024]{2,1,0:T(8,128)(2,1)} %param.10) | data formatting | bytes 524288 | tf_op jit(solution)/shard_map/reshape | solution.py:130
  22.8 12.0 %all-to-all-done = f32[256,2,128]{2,1,0:T(2,128)S(1)} async-done(((f32[256,2,128]{2,1,0:T(2,128)}), f32[256,2,128]{2,1,0:T(2,128)S(1)}, u32[]{:S(2)}, u32[]{:S(2)}) %all-to-all-start) | async-done | bytes 262176 | tf_op jit(solution)/shard_map/all_to_all | solution.py:82
  34.8 0.1 bitcast_reduce_fusion.1
  34.9 0.1 copy.62
  35.0 0.7 fusion.65
  35.7 0.7 copy-done.9
  36.3 0.9 fusion.51
  37.2 0.1 reshape.288
  37.4 0.4 fusion.55
  37.8 0.8 broadcast_in_dim.41
  38.6 6.8 %all-to-all-start.1 = ((f32[256,2,128]{2,1,0:T(2,128)}), f32[256,2,128]{2,1,0:T(2,128)S(1)}, u32[]{:S(2)}, u32[]{:S(2)}) async-start(f32[256,2,128]{2,1,0:T(2,128)} %bitcast.122), calls=%async_computation.1 | async-start | bytes 524288 | tf_op jit(solution)/shard_map/all_to_all | solution.py:104
  45.4 2.8 %convolution_bitcast_fusion.1 = f32[8,32,4096]{2,1,0:T(8,128)} fusion(bf16[32,32]{1,0:T(8,128)(2,1)S(1)} %copy-done.10, bf16[8,1,32,4096]{3,2,1,0:T(8,128)(2,1)S(1)} %copy-done), kind=kOutput, calls=%fused_computation.3 | convolution fusion | flops 67108864 | bytes 6293504 | tf_op jit(solution)/shard_map/io,riy->roy/dot_general | solution.py:135
  48.2 11.1 %all-to-all-done.1 = f32[256,2,128]{2,1,0:T(2,128)S(1)} async-done(((f32[256,2,128]{2,1,0:T(2,128)}), f32[256,2,128]{2,1,0:T(2,128)S(1)}, u32[]{:S(2)}, u32[]{:S(2)}) %all-to-all-start.1) | async-done | bytes 262176 | tf_op jit(solution)/shard_map/all_to_all | solution.py:104
  59.3 0.4 reshape.290
  59.8 0.3 copy.65
  60.1 0.5 convolution_bitcast_fusion.2
  60.6 0.1 copy.66
  60.7 2.3 %fusion.144 = f32[256,4096]{1,0:T(8,128)S(1)} fusion(bf16[256,256]{1,0:T(8,128)(2,1)S(1)} %get-tuple-element.58, bf16[256,4096]{1,0:T(8,128)(2,1)} %copy-done.3), kind=kOutput, calls=%fused_computation.200 | convolution fusion | flops 536870912 | bytes 6422528 | tf_op jit(solution)/shard_map/dot_general | solution.py:63
  63.1 0.8 convolution_add_fusion
  64.0 2.3 %copy-done.1 = f32[8,32,4096]{2,1,0:T(8,128)S(1)} copy-done((f32[8,32,4096]{2,1,0:T(8,128)S(1)}, f32[8,32,4096]{2,1,0:T(8,128)}, u32[]{:S(2)}) %copy-start.1) | copy-done | bytes 4194328
  66.2 1.2 copy-done.7
  67.5 2.7 %convert_reduce_fusion = (f32[32]{0:T(128)S(1)}, bf16[8,1,32,4096]{3,2,0,1:T(8,128)(2,1)S(1)}) fusion(f32[32]{0:T(128)S(1)} %copy-done.16, f32[8,32,4096]{2,1,0:T(8,128)S(1)} %bitcast.120, f32[8,32,4096]{2,1,0:T(8,128)S(1)} %copy-done.1, bf16[8,1,32,4096]{3,2,1,0:T(8,128)(2,1)S(1)} %copy-done.7), kind=kLoop, calls=%fused_computation.16 | loop fusion | flops 15728608 | bytes 12583168 | tf_op jit(solution)/shard_map/reduce_sum | solution.py:144
  70.2 1.4 copy-done.5
  71.5 0.9 convolution_bitcast_fusion.3
  72.6 0.1 reshape.295
  72.7 3.7 %fusion.25 = f32[256,8,32]{0,1,2:T(8,128)S(1)} fusion(bf16[256,4096]{1,0:T(8,128)(2,1)} %copy-done.3, bf16[8,32,4096]{2,1,0:T(8,128)(2,1)} %bitcast.121), kind=kOutput, calls=%fused_computation.34 | convolution fusion | flops 536870912 | bytes 4456448 | tf_op jit(solution)/shard_map/qc,rc->qr/dot_general | solution.py:73
  76.4 0.5 fusion.78
  77.0 0.4 copy.71
  77.3 0.3 reshape.293
  77.7 1.1 select_maximum_fusion
  78.8 6.8 %all-to-all-start.2 = ((f32[256,3,128]{2,1,0:T(4,128)}), f32[256,3,128]{2,1,0:T(4,128)S(1)}, u32[]{:S(2)}, u32[]{:S(2)}) async-start(f32[256,3,128]{2,1,0:T(4,128)} %select_maximum_fusion), calls=%async_computation.2 | async-start | bytes 1048576 | tf_op jit(solution)/shard_map/all_to_all | solution.py:82
  85.6 0.9 copy.79
  86.5 18.3 %all-to-all-done.2 = f32[256,3,128]{2,1,0:T(4,128)S(1)} async-done(((f32[256,3,128]{2,1,0:T(4,128)}), f32[256,3,128]{2,1,0:T(4,128)S(1)}, u32[]{:S(2)}, u32[]{:S(2)}) %all-to-all-start.2) | async-done | bytes 393248 | tf_op jit(solution)/shard_map/all_to_all | solution.py:82
  104.7 0.1 bitcast_reduce_fusion
  104.8 0.1 copy.74
  104.9 1.4 fusion.67
  106.3 3.0 %fusion.49 = f32[16,8,1,32]{3,2,1,0:T(1,128)S(1)} fusion(bf16[16,8,32,32]{3,2,1,0:T(8,128)(2,1)} %copy-done.8, f32[16,8,32,1]{2,0,1,3:T(8,128)S(1)} %bitcast.131), kind=kOutput, calls=%fused_computation.81 | convolution fusion | flops 1572864 | bytes 294912 | tf_op jit(solution)/shard_map/kqio,kqo->kqi/dot_general | solution.py:152
  109.3 0.1 reshape.297
  109.4 1.0 fusion.53
  110.4 0.3 slice_reduce_fusion
  110.8 0.9 broadcast_in_dim.42
  111.7 7.1 %all-to-all-start.3 = ((f32[256,3,128]{2,1,0:T(4,128)}), f32[256,3,128]{2,1,0:T(4,128)S(1)}, u32[]{:S(2)}, u32[]{:S(2)}) async-start(f32[256,3,128]{2,1,0:T(4,128)} %bitcast.35), calls=%async_computation.3 | async-start | bytes 1048576 | tf_op jit(solution)/shard_map/all_to_all | solution.py:104
  118.8 5.0 %fusion.22 = bf16[8,1,32,4096]{3,2,1,0:T(8,128)(2,1)} fusion(f32[32]{0:T(128)S(1)} %copy-done.17, f32[8,32,4096]{2,1,0:T(8,128)} %convolution_bitcast_fusion.1, f32[256,4096]{1,0:T(8,128)} %copy-done.2), kind=kLoop, calls=%fused_computation.31 | loop fusion | flops 7340032 | bytes 10485888
  123.9 1.7 %multiply_multiply_fusion.1 = f32[16,8,32,32]{3,2,1,0:T(8,128)} fusion(f32[16,8,32]{2,1,0:T(8,128)S(1)} %copy.80, f32[16,8,32]{2,1,0:T(8,128)S(1)} %copy.79), kind=kLoop, calls=%fused_computation.40 | loop fusion | flops 262144 | bytes 557056 | tf_op jit(solution)/shard_map/mul | solution.py:149
  125.6 3.1 %reshape.300 = f32[16,8,1024]{2,1,0:T(8,128)} reshape(f32[16,8,32,32]{3,2,1,0:T(8,128)} %multiply_multiply_fusion.1) | data formatting | bytes 1048576 | tf_op jit(solution)/shard_map/reshape | solution.py:149
  128.7 9.1 %all-to-all-done.3 = f32[256,3,128]{2,1,0:T(4,128)S(1)} async-done(((f32[256,3,128]{2,1,0:T(4,128)}), f32[256,3,128]{2,1,0:T(4,128)S(1)}, u32[]{:S(2)}, u32[]{:S(2)}) %all-to-all-start.3) | async-done | bytes 393248 | tf_op jit(solution)/shard_map/all_to_all | solution.py:104
  137.8 0.6 mul.246
  138.4 0.2 fusion.48
  138.7 0.7 mul.243
  139.3 0.1 slice.73
  139.4 0.4 reshape.299
  139.9 0.3 copy.77
  140.2 0.5 fusion.31
  140.7 2.5 %fusion.23 = f32[8,32,4096]{2,1,0:T(8,128)S(1)} fusion(bf16[256,4096]{1,0:T(8,128)(2,1)} %copy-done.3, bf16[8,32,256]{2,0,1:T(8,128)(2,1)S(1)} %fusion.31), kind=kOutput, calls=%fused_computation.32 | convolution fusion | flops 536870912 | bytes 6422528 | tf_op jit(solution)/shard_map/dot_general | solution.py:112
  143.2 2.0 %fusion.3 = bf16[8,1,32,4096]{3,2,1,0:T(8,128)(2,1)} fusion(f32[8,32,4096]{2,1,0:T(8,128)S(1)} %fusion.23, bf16[32,32]{1,0:T(8,128)(2,1)S(1)} %copy-done.10, bf16[8,1,32,4096]{3,2,0,1:T(8,128)(2,1)S(1)} %copy-done.6), kind=kOutput, calls=%fused_computation.8 | convolution fusion | flops 69206016 | bytes 8390656 | tf_op jit(solution)/shard_map/io,roy->riy/dot_general | solution.py:159
  (52 shorter events, 0.6 us)
Async XLA Ops:
  0.6 2.2 %copy-start = (bf16[8,1,32,4096]{3,2,1,0:T(8,128)(2,1)S(1)}, bf16[8,1,32,4096]{3,2,1,0:T(8,128)(2,1)}, u32[]{:S(2)}) copy-start(bf16[8,1,32,4096]{3,2,1,0:T(8,128)(2,1)} %param.9) | copy-start | bytes 6291460
  0.7 36.7 %copy-start.14 = (pred[16]{0:T(512)(128)(4,1)}, pred[16]{0:T(512)(128)(4,1)S(1)}, u32[]{:S(2)}) copy-start(pred[16]{0:T(512)(128)(4,1)S(1)} %iota_compare_fusion.5) | copy-start | bytes 52
  0.7 36.7 %copy-start.15 = (s32[16]{0:T(128)}, s32[16]{0:T(128)S(1)}, u32[]{:S(2)}) copy-start(s32[16]{0:T(128)S(1)} %add_select_fusion.5) | copy-start | bytes 196
  0.7 59.4 %copy-start.11 = (s32[8]{0:T(128)}, s32[8]{0:T(128)S(1)}, u32[]{:S(2)}) copy-start(s32[8]{0:T(128)S(1)} %get-tuple-element.73) | copy-start | bytes 100
  2.9 1.5 %copy-start.3 = (bf16[256,4096]{1,0:T(8,128)(2,1)}, bf16[256,4096]{1,0:T(8,128)(2,1)S(1)}, u32[]{:S(2)}) copy-start(bf16[256,4096]{1,0:T(8,128)(2,1)S(1)} %fusion.1) | copy-start | bytes 6291460
  4.4 41.1 %copy-start.10 = (bf16[32,32]{1,0:T(8,128)(2,1)S(1)}, bf16[32,32]{1,0:T(8,128)(2,1)}, u32[]{:S(2)}) copy-start(bf16[32,32]{1,0:T(8,128)(2,1)} %param.11) | copy-start | bytes 6148
  6.3 28.4 %all-to-all-start = ((f32[256,2,128]{2,1,0:T(2,128)}), f32[256,2,128]{2,1,0:T(2,128)S(1)}, u32[]{:S(2)}, u32[]{:S(2)}) async-start(f32[256,2,128]{2,1,0:T(2,128)} %reshape.285), calls=%async_computation | async-start | bytes 524288 | tf_op jit(solution)/shard_map/all_to_all | solution.py:82
  22.8 25.4 %copy-start.8 = (bf16[16,8,32,32]{3,2,1,0:T(8,128)(2,1)}, bf16[16,8,32,32]{3,2,1,0:T(8,128)(2,1)S(1)}, u32[]{:S(2)}) copy-start(bf16[16,8,32,32]{3,2,1,0:T(8,128)(2,1)S(1)} %reshape.287) | copy-start | bytes 786436
  35.7 0.7 copy-start.9
  38.6 20.7 %all-to-all-start.1 = ((f32[256,2,128]{2,1,0:T(2,128)}), f32[256,2,128]{2,1,0:T(2,128)S(1)}, u32[]{:S(2)}, u32[]{:S(2)}) async-start(f32[256,2,128]{2,1,0:T(2,128)} %bitcast.122), calls=%async_computation.1 | async-start | bytes 524288 | tf_op jit(solution)/shard_map/all_to_all | solution.py:104
  60.1 3.0 %copy-start.4 = (bf16[256,4096]{1,0:T(8,128)(2,1)S(1)}, bf16[256,4096]{1,0:T(8,128)(2,1)}, u32[]{:S(2)}) copy-start(bf16[256,4096]{1,0:T(8,128)(2,1)} %copy-done.3) | copy-start | bytes 6291460
  63.1 3.1 %copy-start.1 = (f32[8,32,4096]{2,1,0:T(8,128)S(1)}, f32[8,32,4096]{2,1,0:T(8,128)}, u32[]{:S(2)}) copy-start(f32[8,32,4096]{2,1,0:T(8,128)} %convolution_bitcast_fusion.1) | copy-start | bytes 12582916
  63.1 4.4 %copy-start.7 = (bf16[8,1,32,4096]{3,2,1,0:T(8,128)(2,1)S(1)}, bf16[8,1,32,4096]{3,2,1,0:T(8,128)(2,1)}, u32[]{:S(2)}) copy-start(bf16[8,1,32,4096]{3,2,1,0:T(8,128)(2,1)} %param.13) | copy-start | bytes 6291460
  63.1 4.4 %copy-start.16 = (f32[32]{0:T(128)S(1)}, f32[32]{0:T(128)}, u32[]{:S(2)}) copy-start(f32[32]{0:T(128)} %param.12) | copy-start | bytes 388
  64.0 6.2 %copy-start.2 = (f32[256,4096]{1,0:T(8,128)}, f32[256,4096]{1,0:T(8,128)S(1)}, u32[]{:S(2)}) copy-start(f32[256,4096]{1,0:T(8,128)S(1)} %convolution_add_fusion) | copy-start | bytes 12582916
  70.2 1.4 copy-start.5
  72.7 3.7 %copy-start.12 = (s32[8]{0:T(128)S(1)}, s32[8]{0:T(128)}, u32[]{:S(2)}) copy-start(s32[8]{0:T(128)} %copy-done.11) | copy-start | bytes 100
  77.7 41.1 %copy-start.17 = (f32[32]{0:T(128)S(1)}, f32[32]{0:T(128)}, u32[]{:S(2)}) copy-start(f32[32]{0:T(128)} %param.12) | copy-start | bytes 388
  78.8 26.0 %all-to-all-start.2 = ((f32[256,3,128]{2,1,0:T(4,128)}), f32[256,3,128]{2,1,0:T(4,128)S(1)}, u32[]{:S(2)}, u32[]{:S(2)}) async-start(f32[256,3,128]{2,1,0:T(4,128)} %select_maximum_fusion), calls=%async_computation.2 | async-start | bytes 1048576 | tf_op jit(solution)/shard_map/all_to_all | solution.py:82
  111.7 26.1 %all-to-all-start.3 = ((f32[256,3,128]{2,1,0:T(4,128)}), f32[256,3,128]{2,1,0:T(4,128)S(1)}, u32[]{:S(2)}, u32[]{:S(2)}) async-start(f32[256,3,128]{2,1,0:T(4,128)} %bitcast.35), calls=%async_computation.3 | async-start | bytes 1048576 | tf_op jit(solution)/shard_map/all_to_all | solution.py:104
  123.8 16.4 %copy-start.13 = (s32[8]{0:T(128)S(1)}, s32[8]{0:T(128)}, u32[]{:S(2)}) copy-start(s32[8]{0:T(128)} %copy-done.11) | copy-start | bytes 100
  140.7 2.5 %copy-start.6 = (bf16[8,1,32,4096]{3,2,0,1:T(8,128)(2,1)S(1)}, bf16[8,1,32,4096]{3,2,0,1:T(8,128)(2,1)}, u32[]{:S(2)}) copy-start(bf16[8,1,32,4096]{3,2,0,1:T(8,128)(2,1)} %copy-done.5) | copy-start | bytes 6291460

commit v9 on v7

--- a/solution.py
+++ b/solution.py
@@ -149,7 +149,7 @@
     spectral_grad = (spec_scale * jnp.einsum("kqi,kqo->kqio", coeffs, slope_modes)).reshape(
         KX, -1, channels * channels
     )
-    coeff_grad = jnp.einsum("kqio,kqo->kqi", weights, slope_modes, precision=PRECISE)
+    coeff_grad = jnp.sum(weights * slope_modes[:, :, None, :], axis=3)
     grad_spatial, packed_sum = to_planes(
         coeff_grad, forward_x, forward_t, yz_table, steps_here, extra=packed_part, one_pass=True
     )

time: 145 us -> 152 us (1.048)
  local copies, waits for them, and re-layouts: 15.6 us -> 20 us
  other arithmetic: 7.71 us -> 10.1 us
  matrix products: 27.8 us -> 25.5 us
    dot_general x1 -> x0, matrix products: 2.97 us -> none  [shards(): jnp.einsum('kqio,kqo->kqi', weights, slope_modes, precision=PRECISE)]
    reshape x4, local copies, waits for them, and re-layouts: 1.55 us -> 3.75 us  [to_planes(): modes = returned[:, :rows_per].reshape(KT, KYZ, channels)]
    all_to_all x1, waiting for transfers between devices: 10.6 us -> 12.4 us  [to_planes(): lax.all_to_all(copies.reshape((-1,) + spread.shape[1:]), ('sp', 'ch'), 0,...]
  transfers between devices with their start and end apart: 3 -> 3, of which waited for: 3 -> 3; matrix products, arithmetic and copies ran while one was open for 8% -> 6% of each run, Pallas kernels for 0% -> 0%
where the time goes in v9:
time: 152 us; the launch traced here: 149 us
  waiting for transfers between devices  41.7 us (27%)
  starting transfers between devices  29.7 us (20%)
  matrix products  25.5 us (17%)
  blocking collectives  20.6 us (14%)
  local copies, waits for them, and re-layouts  20 us (13%)
  other arithmetic  10.1 us (7%)
    all_to_all x2, waiting for transfers between devices, to_spectrum(): arrived = lax.all_to_all(send, ('sp', 'ch'), 0, 0, tiled=True)  29.3 us
    all_to_all x2, starting transfers between devices, to_spectrum(): arrived = lax.all_to_all(send, ('sp', 'ch'), 0, 0, tiled=True)  22.6 us
    all_to_all x1, blocking collectives, to_planes(): lax.all_to_all(copies.reshape((-1,) + spread.shape[1:]), ('sp', 'ch'), 0,...  20.6 us
    all_to_all x1, waiting for transfers between devices, to_planes(): lax.all_to_all(copies.reshape((-1,) + spread.shape[1:]), ('sp', 'ch'), 0,...  12.4 us
    all_to_all x1, starting transfers between devices, to_planes(): lax.all_to_all(copies.reshape((-1,) + spread.shape[1:]), ('sp', 'ch'), 0,...  7.1 us
    dot_general x2, matrix products, to_spectrum(): jnp.einsum('qc,rc->qr', yz_table, values.reshape(-1, plane_cells), prefer...  5.17 us
    dot_general x1, matrix products, shards(): jnp.einsum('io,riy->roy', point_weight, field_rows, preferred_element_typ...  4.52 us
    reshape x4, local copies, waits for them, and re-layouts, to_planes(): modes = returned[:, :rows_per].reshape(KT, KYZ, channels)  3.75 us
  transfers between devices with their start and end apart: 3, of which 3 were waited for; matrix products, arithmetic and copies ran while one was open for 6% of the time, Pallas kernels for 0%

profile of v9, /device:TPU:8, one launch (start us, length us, event | category | flops | bytes accessed | tf_op | source)
XLA Modules:
  0.0 148.9 jit_solution(9595147819599795094)
XLA Ops:
  0.7 0.1 broadcast_multiply_fusion
  0.9 0.1 reduce-precision_convert_fusion.2
  1.0 0.3 iota_compare_fusion
  1.3 0.8 fusion.13
  2.1 0.8 fusion.3
  2.9 1.5 fusion.29
  4.4 0.5 fusion.82
  4.9 0.4 copy.61
  5.3 1.0 reshape.286
  6.3 14.6 %all-to-all-start = ((f32[256,2,128]{2,1,0:T(2,128)}), f32[256,2,128]{2,1,0:T(2,128)S(1)}, u32[]{:S(2)}, u32[]{:S(2)}) async-start(f32[256,2,128]{2,1,0:T(2,128)} %reshape.286), calls=%async_computation | async-start | bytes 524288 | tf_op jit(solution)/shard_map/all_to_all | solution.py:82
  20.9 1.8 %reshape.288 = bf16[16,8,32,32]{3,2,1,0:T(8,128)(2,1)S(1)} reshape(bf16[16,8,1024]{2,1,0:T(8,128)(2,1)} %param.10) | data formatting | bytes 524288 | tf_op jit(solution)/shard_map/reshape | solution.py:130
  22.8 12.0 %all-to-all-done = f32[256,2,128]{2,1,0:T(2,128)S(1)} async-done(((f32[256,2,128]{2,1,0:T(2,128)}), f32[256,2,128]{2,1,0:T(2,128)S(1)}, u32[]{:S(2)}, u32[]{:S(2)}) %all-to-all-start) | async-done | bytes 262176 | tf_op jit(solution)/shard_map/all_to_all | solution.py:82
  34.8 0.1 bitcast_reduce_fusion.1
  34.8 0.1 copy.62
  35.0 0.7 fusion.65
  35.6 0.6 copy-done.5
  36.3 0.9 fusion.51
  37.2 0.1 reshape.289
  37.3 0.4 fusion.55
  37.8 0.1 broadcast_in_dim.41
  37.9 20.6 %all_to_all.20 = f32[256,2,128]{2,1,0:T(2,128)S(1)} all-to-all(f32[256,2,128]{2,1,0:T(2,128)S(1)} %bitcast.125), channel_id=1, replica_groups=mesh['sp'=64,'ch'=4] {'sp','ch'}, dimensions={0} | all-to-all | bytes 524288 | tf_op jit(solution)/shard_map/all_to_all | solution.py:104
  58.5 1.4 reshape.291
  59.9 1.6 %copy.65 = f32[8,256,32]{1,0,2:T(8,128)S(1)} copy(f32[8,256,32]{2,1,0:T(8,128)} %reshape.291) | data formatting | bytes 524288 | tf_op jit(solution)/shard_map/reshape | solution.py:108
  61.5 0.5 convolution_bitcast_fusion.2
  62.0 0.1 copy.66
  62.1 2.5 %fusion.144 = f32[256,4096]{1,0:T(8,128)S(1)} fusion(bf16[256,256]{1,0:T(8,128)(2,1)S(1)} %get-tuple-element.58, bf16[256,4096]{1,0:T(8,128)(2,1)} %copy-done.1), kind=kOutput, calls=%fused_computation.200 | convolution fusion | flops 536870912 | bytes 6422528 | tf_op jit(solution)/shard_map/dot_general | solution.py:63
  64.6 0.7 convolution_add_fusion
  65.4 0.8 copy-done.14
  66.2 4.5 %convert_reduce_fusion = (f32[32]{0:T(128)S(1)}, bf16[8,1,32,4096]{3,2,0,1:T(8,128)(2,1)S(1)}, f32[8,32,4096]{2,1,0:T(8,128)}) fusion(bf16[8,1,32,4096]{3,2,1,0:T(8,128)(2,1)S(1)} %copy-done.14, f32[32]{0:T(128)S(1)} %copy-done.15, f32[8,32,4096]{2,1,0:T(8,128)S(1)} %bitcast.124, bf16[32,32]{1,0:T(8,128)(2,1)S(1)} %copy-done.6, ...), kind=kOutput, calls=%fused_computation.18 | convolution fusion | flops 82837472 | bytes 14682368 | tf_op jit(solution)/shard_map/io,riy->roy/dot_general | solution.py:134
  70.7 1.3 copy-done.3
  72.0 0.9 convolution_bitcast_fusion.3
  72.9 0.1 copy.72
  73.0 0.1 reshape.295
  73.1 0.1 reshape.296
  73.2 3.7 %fusion.27 = f32[256,8,32]{0,1,2:T(8,128)S(1)} fusion(bf16[256,4096]{1,0:T(8,128)(2,1)} %copy-done.1, bf16[8,32,4096]{2,1,0:T(8,128)(2,1)} %bitcast.123), kind=kOutput, calls=%fused_computation.35 | convolution fusion | flops 536870912 | bytes 4456448 | tf_op jit(solution)/shard_map/qc,rc->qr/dot_general | solution.py:73
  76.9 0.5 fusion.78
  77.5 1.3 copy.71
  78.8 1.6 %reshape.294 = f32[256,2,128]{2,1,0:T(2,128)S(1)} reshape(f32[8,256,32]{2,1,0:T(8,128)} %copy.71) | data formatting | bytes 524288 | tf_op jit(solution)/shard_map/reshape | solution.py:77
  80.4 1.1 select_maximum_fusion
  81.5 8.0 %all-to-all-start.2 = ((f32[256,3,128]{2,1,0:T(4,128)}), f32[256,3,128]{2,1,0:T(4,128)}, u32[]{:S(2)}, u32[]{:S(2)}) async-start(f32[256,3,128]{2,1,0:T(4,128)} %select_maximum_fusion), calls=%async_computation.2 | async-start | bytes 1048576 | tf_op jit(solution)/shard_map/all_to_all | solution.py:82
  89.5 0.9 copy.80
  90.4 17.4 %all-to-all-done.2 = f32[256,3,128]{2,1,0:T(4,128)} async-done(((f32[256,3,128]{2,1,0:T(4,128)}), f32[256,3,128]{2,1,0:T(4,128)}, u32[]{:S(2)}, u32[]{:S(2)}) %all-to-all-start.2) | async-done | bytes 393248 | tf_op jit(solution)/shard_map/all_to_all | solution.py:82
  107.8 1.2 bitcast_reduce_fusion
  108.9 0.1 copy.74
  109.0 1.4 fusion.67
  110.4 2.0 %multiply_multiply_fusion.1 = (f32[16,8,32,32]{3,2,1,0:T(8,128)}, f32[16,8,32]{2,1,0:T(8,128)S(1)}) fusion(f32[16,8,32]{2,1,0:T(8,128)S(1)} %copy.80, f32[16,8,32]{2,1,0:T(8,128)S(1)} %copy.75, bf16[16,8,32,32]{3,2,1,0:T(8,128)(2,1)S(1)} %reshape.288), kind=kLoop, calls=%fused_computation.41 | loop fusion | flops 651264 | bytes 835584 | tf_op jit(solution)/shard_map/mul | solution.py:149
  112.5 0.1 reshape.298
  112.6 0.4 fusion.53
  113.0 1.3 slice_reduce_fusion
  114.3 0.1 copy.77
  114.4 0.9 broadcast_in_dim.42
  115.3 7.1 %all-to-all-start.3 = ((f32[256,3,128]{2,1,0:T(4,128)}), f32[256,3,128]{2,1,0:T(4,128)S(1)}, u32[]{:S(2)}, u32[]{:S(2)}) async-start(f32[256,3,128]{2,1,0:T(4,128)} %bitcast.32), calls=%async_computation.3 | async-start | bytes 1048576 | tf_op jit(solution)/shard_map/all_to_all | solution.py:104
  122.4 3.6 %fusion.24 = bf16[8,1,32,4096]{3,2,1,0:T(8,128)(2,1)} fusion(f32[8,32,4096]{2,1,0:T(8,128)} %get-tuple-element.69), kind=kLoop, calls=%fused_computation.32 | loop fusion | flops 5242880 | bytes 6291456
  126.0 3.1 %reshape.301 = f32[16,8,1024]{2,1,0:T(8,128)} reshape(f32[16,8,32,32]{3,2,1,0:T(8,128)} %get-tuple-element.65) | data formatting | bytes 1048576 | tf_op jit(solution)/shard_map/reshape | solution.py:149
  129.1 12.4 %all-to-all-done.3 = f32[256,3,128]{2,1,0:T(4,128)S(1)} async-done(((f32[256,3,128]{2,1,0:T(4,128)}), f32[256,3,128]{2,1,0:T(4,128)S(1)}, u32[]{:S(2)}, u32[]{:S(2)}) %all-to-all-start.3) | async-done | bytes 393248 | tf_op jit(solution)/shard_map/all_to_all | solution.py:104
  141.5 0.6 mul.256
  142.1 0.2 fusion.50
  142.3 0.7 mul.253
  143.0 0.1 slice.73
  143.1 0.4 reshape.300
  143.6 0.3 copy.78
  143.9 0.5 fusion.33
  144.4 2.5 %fusion.25 = f32[8,32,4096]{2,1,0:T(8,128)S(1)} fusion(bf16[256,4096]{1,0:T(8,128)(2,1)} %copy-done.1, bf16[8,32,256]{2,0,1:T(8,128)(2,1)S(1)} %fusion.33), kind=kOutput, calls=%fused_computation.33 | convolution fusion | flops 536870912 | bytes 6422528 | tf_op jit(solution)/shard_map/dot_general | solution.py:112
  146.9 2.0 %fusion.5 = bf16[8,1,32,4096]{3,2,1,0:T(8,128)(2,1)} fusion(f32[8,32,4096]{2,1,0:T(8,128)S(1)} %fusion.25, bf16[32,32]{1,0:T(8,128)(2,1)S(1)} %copy-done.6, bf16[8,1,32,4096]{3,2,0,1:T(8,128)(2,1)S(1)} %copy-done.4), kind=kOutput, calls=%fused_computation.10 | convolution fusion | flops 69206016 | bytes 8390656 | tf_op jit(solution)/shard_map/io,roy->riy/dot_general | solution.py:159
  (45 shorter events, 0.3 us)
Async XLA Ops:
  0.6 2.2 %copy-start = (bf16[8,1,32,4096]{3,2,1,0:T(8,128)(2,1)S(1)}, bf16[8,1,32,4096]{3,2,1,0:T(8,128)(2,1)}, u32[]{:S(2)}) copy-start(bf16[8,1,32,4096]{3,2,1,0:T(8,128)(2,1)} %param.9) | copy-start | bytes 6291460
  0.7 36.7 %copy-start.10 = (pred[16]{0:T(512)(128)(4,1)}, pred[16]{0:T(512)(128)(4,1)S(1)}, u32[]{:S(2)}) copy-start(pred[16]{0:T(512)(128)(4,1)S(1)} %iota_compare_fusion.5) | copy-start | bytes 52
  0.7 36.7 %copy-start.12 = (s32[16]{0:T(128)}, s32[16]{0:T(128)S(1)}, u32[]{:S(2)}) copy-start(s32[16]{0:T(128)S(1)} %add_select_fusion.5) | copy-start | bytes 196
  0.7 60.8 %copy-start.7 = (s32[8]{0:T(128)}, s32[8]{0:T(128)S(1)}, u32[]{:S(2)}) copy-start(s32[8]{0:T(128)S(1)} %get-tuple-element.76) | copy-start | bytes 100
  2.9 1.5 %copy-start.1 = (bf16[256,4096]{1,0:T(8,128)(2,1)}, bf16[256,4096]{1,0:T(8,128)(2,1)S(1)}, u32[]{:S(2)}) copy-start(bf16[256,4096]{1,0:T(8,128)(2,1)S(1)} %fusion.3) | copy-start | bytes 6291460
  6.3 28.4 %all-to-all-start = ((f32[256,2,128]{2,1,0:T(2,128)}), f32[256,2,128]{2,1,0:T(2,128)S(1)}, u32[]{:S(2)}, u32[]{:S(2)}) async-start(f32[256,2,128]{2,1,0:T(2,128)} %reshape.286), calls=%async_computation | async-start | bytes 524288 | tf_op jit(solution)/shard_map/all_to_all | solution.py:82
  35.6 0.6 copy-start.5
  62.1 2.5 %copy-start.2 = (bf16[256,4096]{1,0:T(8,128)(2,1)S(1)}, bf16[256,4096]{1,0:T(8,128)(2,1)}, u32[]{:S(2)}) copy-start(bf16[256,4096]{1,0:T(8,128)(2,1)} %copy-done.1) | copy-start | bytes 6291460
  64.6 0.8 copy-start.6
  64.6 1.6 %copy-start.14 = (bf16[8,1,32,4096]{3,2,1,0:T(8,128)(2,1)S(1)}, bf16[8,1,32,4096]{3,2,1,0:T(8,128)(2,1)}, u32[]{:S(2)}) copy-start(bf16[8,1,32,4096]{3,2,1,0:T(8,128)(2,1)} %param.13) | copy-start | bytes 6291460
  64.6 1.6 %copy-start.15 = (f32[32]{0:T(128)S(1)}, f32[32]{0:T(128)}, u32[]{:S(2)}) copy-start(f32[32]{0:T(128)} %param.12) | copy-start | bytes 388
  70.7 1.3 copy-start.3
  73.2 3.7 %copy-start.8 = (s32[8]{0:T(128)S(1)}, s32[8]{0:T(128)}, u32[]{:S(2)}) copy-start(s32[8]{0:T(128)} %copy-done.7) | copy-start | bytes 100
  81.5 26.3 %all-to-all-start.2 = ((f32[256,3,128]{2,1,0:T(4,128)}), f32[256,3,128]{2,1,0:T(4,128)}, u32[]{:S(2)}, u32[]{:S(2)}) async-start(f32[256,3,128]{2,1,0:T(4,128)} %select_maximum_fusion), calls=%async_computation.2 | async-start | bytes 1048576 | tf_op jit(solution)/shard_map/all_to_all | solution.py:82
  90.4 22.2 %copy-start.11 = (pred[16]{0:T(512)(128)(4,1)S(1)}, pred[16]{0:T(512)(128)(4,1)}, u32[]{:S(2)}) copy-start(pred[16]{0:T(512)(128)(4,1)} %copy-done.10) | copy-start | bytes 52
  90.4 22.2 %copy-start.13 = (s32[16]{0:T(128)S(1)}, s32[16]{0:T(128)}, u32[]{:S(2)}) copy-start(s32[16]{0:T(128)} %copy-done.12) | copy-start | bytes 196
  115.3 26.2 %all-to-all-start.3 = ((f32[256,3,128]{2,1,0:T(4,128)}), f32[256,3,128]{2,1,0:T(4,128)S(1)}, u32[]{:S(2)}, u32[]{:S(2)}) async-start(f32[256,3,128]{2,1,0:T(4,128)} %bitcast.32), calls=%async_computation.3 | async-start | bytes 1048576 | tf_op jit(solution)/shard_map/all_to_all | solution.py:104
  129.1 14.8 %copy-start.9 = (s32[8]{0:T(128)S(1)}, s32[8]{0:T(128)}, u32[]{:S(2)}) copy-start(s32[8]{0:T(128)} %copy-done.7) | copy-start | bytes 100
  144.4 2.5 %copy-start.4 = (bf16[8,1,32,4096]{3,2,0,1:T(8,128)(2,1)S(1)}, bf16[8,1,32,4096]{3,2,0,1:T(8,128)(2,1)}, u32[]{:S(2)}) copy-start(bf16[8,1,32,4096]{3,2,0,1:T(8,128)(2,1)} %copy-done.3) | copy-start | bytes 6291460

commit v10 on v7

--- a/solution.py
+++ b/solution.py
@@ -60,9 +60,9 @@
 def split_dot(values, table):
     high = lax.reduce_precision(values, exponent_bits=8, mantissa_bits=7)
     low = (values - high).astype(jnp.bfloat16)
-    return jnp.dot(high.astype(jnp.bfloat16), table, preferred_element_type=jnp.float32) + jnp.dot(
-        low, table, preferred_element_type=jnp.float32
-    )
+    pieces = jnp.concatenate([high.astype(jnp.bfloat16), low], axis=1)
+    stacked = jnp.concatenate([table, table], axis=0)
+    return jnp.dot(pieces, stacked, preferred_element_type=jnp.float32)
 
 
 def to_spectrum(values, yz_table, time_table, x_table, extra=None):

time: 145 us -> 146 us (level)
  matrix products: 27.8 us -> 29.6 us
    dot_general x2 -> x1, matrix products: 3.18 us -> 3.64 us  [split_dot(): return jnp.dot(pieces, stacked, preferred_element_type=jnp.float32)]
where the time goes in v10:
time: 146 us; the launch traced here: 143 us
  waiting for transfers between devices  40.8 us (28%)
  matrix products  29.6 us (20%)
  starting transfers between devices  28.4 us (19%)
  blocking collectives  20.6 us (14%)
  local copies, waits for them, and re-layouts  14.7 us (10%)
  other arithmetic  7.74 us (5%)
    all_to_all x2, waiting for transfers between devices, to_spectrum(): arrived = lax.all_to_all(send, ('sp', 'ch'), 0, 0, tiled=True)  30.2 us
    all_to_all x2, starting transfers between devices, to_spectrum(): arrived = lax.all_to_all(send, ('sp', 'ch'), 0, 0, tiled=True)  21.3 us
    all_to_all x1, blocking collectives, to_planes(): lax.all_to_all(copies.reshape((-1,) + spread.shape[1:]), ('sp', 'ch'), 0,...  20.6 us
    all_to_all x1, waiting for transfers between devices, to_planes(): lax.all_to_all(copies.reshape((-1,) + spread.shape[1:]), ('sp', 'ch'), 0,...  10.6 us
    all_to_all x1, starting transfers between devices, to_planes(): lax.all_to_all(copies.reshape((-1,) + spread.shape[1:]), ('sp', 'ch'), 0,...  7.1 us
    dot_general x2, matrix products, to_spectrum(): jnp.einsum('qc,rc->qr', yz_table, values.reshape(-1, plane_cells), prefer...  5.17 us
    dot_general x1, matrix products, shards(): jnp.einsum('io,riy->roy', point_weight, field_rows, preferred_element_typ...  4.52 us
    dot_general x1, matrix products, split_dot(): return jnp.dot(pieces, stacked, preferred_element_type=jnp.float32)  3.64 us
  transfers between devices with their start and end apart: 3, of which 3 were waited for; matrix products, arithmetic and copies ran while one was open for 8% of the time, Pallas kernels for 0%

profile of v10, /device:TPU:8, one launch (start us, length us, event | category | flops | bytes accessed | tf_op | source)
XLA Modules:
  0.0 143.0 jit_solution(17551680950356690780)
XLA Ops:
  0.7 0.1 broadcast_multiply_fusion
  0.9 0.1 reduce-precision_convert_fusion.2
  1.0 0.3 iota_compare_fusion
  1.3 0.8 fusion.17
  2.1 0.8 fusion.3
  2.9 1.5 %fusion.33 = f32[256,8,32]{0,1,2:T(8,128)S(1)} fusion(bf16[256,4096]{1,0:T(8,128)(2,1)S(1)} %fusion.3, bf16[8,32,4096]{2,1,0:T(8,128)(2,1)S(1)} %bitcast.122), kind=kOutput, calls=%fused_computation.40 | convolution fusion | flops 536870912 | bytes 4456448 | tf_op jit(solution)/shard_map/qc,rc->qr/dot_general | solution.py:73
  4.4 0.5 fusion.91
  4.9 0.4 copy.61
  5.3 1.0 reshape.285
  6.3 14.6 %all-to-all-start = ((f32[256,2,128]{2,1,0:T(2,128)}), f32[256,2,128]{2,1,0:T(2,128)S(1)}, u32[]{:S(2)}, u32[]{:S(2)}) async-start(f32[256,2,128]{2,1,0:T(2,128)} %reshape.285), calls=%async_computation | async-start | bytes 524288 | tf_op jit(solution)/shard_map/all_to_all | solution.py:82
  20.9 1.8 %reshape.287 = bf16[16,8,32,32]{3,2,1,0:T(8,128)(2,1)S(1)} reshape(bf16[16,8,1024]{2,1,0:T(8,128)(2,1)} %param.10) | data formatting | bytes 524288 | tf_op jit(solution)/shard_map/reshape | solution.py:130
  22.8 12.0 %all-to-all-done = f32[256,2,128]{2,1,0:T(2,128)S(1)} async-done(((f32[256,2,128]{2,1,0:T(2,128)}), f32[256,2,128]{2,1,0:T(2,128)S(1)}, u32[]{:S(2)}, u32[]{:S(2)}) %all-to-all-start) | async-done | bytes 262176 | tf_op jit(solution)/shard_map/all_to_all | solution.py:82
  34.8 0.1 bitcast_reduce_fusion.1
  34.8 0.1 copy.62
  35.0 0.7 fusion.74
  35.6 0.6 copy-done.5
  36.3 0.9 fusion.60
  37.2 0.1 reshape.288
  37.3 0.4 fusion.64
  37.7 0.1 copy.64
  37.8 0.1 broadcast_in_dim.41
  37.9 20.6 %all_to_all.20 = f32[256,2,128]{2,1,0:T(2,128)S(1)} all-to-all(f32[256,2,128]{2,1,0:T(2,128)S(1)} %bitcast.124), channel_id=1, replica_groups=mesh['sp'=64,'ch'=4] {'sp','ch'}, dimensions={0} | all-to-all | bytes 524288 | tf_op jit(solution)/shard_map/all_to_all | solution.py:104
  58.5 0.4 reshape.290
  59.0 0.3 copy.65
  59.3 0.5 convolution_bitcast_fusion.2
  59.8 0.1 copy.66
  60.0 3.6 %fusion.13 = f32[256,4096]{1,0:T(8,128)S(1)} fusion(bf16[256,4096]{1,0:T(8,128)(2,1)} %copy-done.1, bf16[256,256]{1,0:T(8,128)(2,1)S(1)} %get-tuple-element.58, bf16[256,256]{1,0:T(8,128)(2,1)S(1)} %get-tuple-element.57), kind=kOutput, calls=%fused_computation.17 | convolution fusion | flops 1082654720 | bytes 6553600 | tf_op jit(solution)/shard_map/dot_general | solution.py:65
  63.6 4.5 %convert_reduce_fusion = (f32[32]{0:T(128)S(1)}, bf16[8,1,32,4096]{3,2,0,1:T(8,128)(2,1)S(1)}, f32[8,32,4096]{2,1,0:T(8,128)}) fusion(bf16[8,1,32,4096]{3,2,1,0:T(8,128)(2,1)S(1)} %copy-done.12, f32[32]{0:T(128)S(1)} %copy-done.13, f32[8,32,4096]{2,1,0:T(8,128)S(1)} %bitcast.136, bf16[32,32]{1,0:T(8,128)(2,1)S(1)} %copy-done.6, ...), kind=kOutput, calls=%fused_computation.21 | convolution fusion | flops 82837472 | bytes 14682368 | tf_op jit(solution)/shard_map/io,riy->roy/dot_general | solution.py:134
  68.2 1.3 copy-done.2
  69.5 0.9 convolution_bitcast_fusion.3
  70.3 0.1 copy.72
  70.4 0.1 reshape.294
  70.5 0.1 reshape.295
  70.6 3.7 %fusion.31 = f32[256,8,32]{0,1,2:T(8,128)S(1)} fusion(bf16[256,4096]{1,0:T(8,128)(2,1)} %copy-done.1, bf16[8,32,4096]{2,1,0:T(8,128)(2,1)} %bitcast.123), kind=kOutput, calls=%fused_computation.38 | convolution fusion | flops 536870912 | bytes 4456448 | tf_op jit(solution)/shard_map/qc,rc->qr/dot_general | solution.py:73
  74.4 0.5 fusion.87
  74.9 0.4 copy.71
  75.3 0.3 reshape.293
  75.6 1.1 select_maximum_fusion
  76.7 6.6 %all-to-all-start.2 = ((f32[256,3,128]{2,1,0:T(4,128)}), f32[256,3,128]{2,1,0:T(4,128)S(1)}, u32[]{:S(2)}, u32[]{:S(2)}) async-start(f32[256,3,128]{2,1,0:T(4,128)} %select_maximum_fusion), calls=%async_computation.2 | async-start | bytes 1048576 | tf_op jit(solution)/shard_map/all_to_all | solution.py:82
  83.4 0.9 copy.79
  84.2 18.2 %all-to-all-done.2 = f32[256,3,128]{2,1,0:T(4,128)S(1)} async-done(((f32[256,3,128]{2,1,0:T(4,128)}), f32[256,3,128]{2,1,0:T(4,128)S(1)}, u32[]{:S(2)}, u32[]{:S(2)}) %all-to-all-start.2) | async-done | bytes 393248 | tf_op jit(solution)/shard_map/all_to_all | solution.py:82
  102.4 0.1 bitcast_reduce_fusion
  102.5 0.1 copy.74
  102.6 1.4 fusion.76
  104.0 3.0 %fusion.58 = f32[16,8,1,32]{3,2,1,0:T(1,128)S(1)} fusion(bf16[16,8,32,32]{3,2,1,0:T(8,128)(2,1)} %copy-done.4, f32[16,8,32,1]{2,0,1,3:T(8,128)S(1)} %bitcast.133), kind=kOutput, calls=%fused_computation.88 | convolution fusion | flops 1572864 | bytes 294912 | tf_op jit(solution)/shard_map/kqio,kqo->kqi/dot_general | solution.py:152
  107.0 0.1 reshape.297
  107.1 1.0 fusion.62
  108.1 0.3 slice_reduce_fusion
  108.4 0.1 copy.76
  108.5 0.9 broadcast_in_dim.42
  109.4 7.1 %all-to-all-start.3 = ((f32[256,3,128]{2,1,0:T(4,128)}), f32[256,3,128]{2,1,0:T(4,128)S(1)}, u32[]{:S(2)}, u32[]{:S(2)}) async-start(f32[256,3,128]{2,1,0:T(4,128)} %bitcast.35), calls=%async_computation.3 | async-start | bytes 1048576 | tf_op jit(solution)/shard_map/all_to_all | solution.py:104
  116.5 3.6 %fusion.28 = bf16[8,1,32,4096]{3,2,1,0:T(8,128)(2,1)} fusion(f32[8,32,4096]{2,1,0:T(8,128)} %get-tuple-element.67), kind=kLoop, calls=%fused_computation.35 | loop fusion | flops 5242880 | bytes 6291456
  120.1 1.8 %multiply_multiply_fusion.1 = f32[16,8,32,32]{3,2,1,0:T(8,128)} fusion(f32[16,8,32]{2,1,0:T(8,128)S(1)} %copy.80, f32[16,8,32]{2,1,0:T(8,128)S(1)} %copy.79), kind=kLoop, calls=%fused_computation.44 | loop fusion | flops 262144 | bytes 557056 | tf_op jit(solution)/shard_map/mul | solution.py:149
  121.9 3.1 %reshape.300 = f32[16,8,1024]{2,1,0:T(8,128)} reshape(f32[16,8,32,32]{3,2,1,0:T(8,128)} %multiply_multiply_fusion.1) | data formatting | bytes 1048576 | tf_op jit(solution)/shard_map/reshape | solution.py:149
  125.0 10.6 %all-to-all-done.3 = f32[256,3,128]{2,1,0:T(4,128)S(1)} async-done(((f32[256,3,128]{2,1,0:T(4,128)}), f32[256,3,128]{2,1,0:T(4,128)S(1)}, u32[]{:S(2)}, u32[]{:S(2)}) %all-to-all-start.3) | async-done | bytes 393248 | tf_op jit(solution)/shard_map/all_to_all | solution.py:104
  135.6 0.6 mul.246
  136.2 0.2 fusion.57
  136.4 0.7 mul.243
  137.1 0.1 slice.73
  137.2 0.4 reshape.299
  137.6 0.3 copy.77
  138.0 0.5 fusion.37
  138.5 2.5 %fusion.29 = f32[8,32,4096]{2,1,0:T(8,128)S(1)} fusion(bf16[256,4096]{1,0:T(8,128)(2,1)} %copy-done.1, bf16[8,32,256]{2,0,1:T(8,128)(2,1)S(1)} %fusion.37), kind=kOutput, calls=%fused_computation.36 | convolution fusion | flops 536870912 | bytes 6422528 | tf_op jit(solution)/shard_map/dot_general | solution.py:112
  140.9 2.0 %fusion.5 = bf16[8,1,32,4096]{3,2,1,0:T(8,128)(2,1)} fusion(f32[8,32,4096]{2,1,0:T(8,128)S(1)} %fusion.29, bf16[32,32]{1,0:T(8,128)(2,1)S(1)} %copy-done.6, bf16[8,1,32,4096]{3,2,0,1:T(8,128)(2,1)S(1)} %copy-done.3), kind=kOutput, calls=%fused_computation.9 | convolution fusion | flops 69206016 | bytes 8390656 | tf_op jit(solution)/shard_map/io,roy->riy/dot_general | solution.py:159
  (41 shorter events, 0.2 us)
Async XLA Ops:
  0.6 2.2 %copy-start = (bf16[8,1,32,4096]{3,2,1,0:T(8,128)(2,1)S(1)}, bf16[8,1,32,4096]{3,2,1,0:T(8,128)(2,1)}, u32[]{:S(2)}) copy-start(bf16[8,1,32,4096]{3,2,1,0:T(8,128)(2,1)} %param.9) | copy-start | bytes 6291460
  0.7 36.7 %copy-start.10 = (pred[16]{0:T(512)(128)(4,1)}, pred[16]{0:T(512)(128)(4,1)S(1)}, u32[]{:S(2)}) copy-start(pred[16]{0:T(512)(128)(4,1)S(1)} %iota_compare_fusion.5) | copy-start | bytes 52
  0.7 36.7 %copy-start.11 = (s32[16]{0:T(128)}, s32[16]{0:T(128)S(1)}, u32[]{:S(2)}) copy-start(s32[16]{0:T(128)S(1)} %add_select_fusion.5) | copy-start | bytes 196
  0.7 58.6 %copy-start.7 = (s32[8]{0:T(128)}, s32[8]{0:T(128)S(1)}, u32[]{:S(2)}) copy-start(s32[8]{0:T(128)S(1)} %get-tuple-element.74) | copy-start | bytes 100
  2.9 1.5 %copy-start.1 = (bf16[256,4096]{1,0:T(8,128)(2,1)}, bf16[256,4096]{1,0:T(8,128)(2,1)S(1)}, u32[]{:S(2)}) copy-start(bf16[256,4096]{1,0:T(8,128)(2,1)S(1)} %fusion.3) | copy-start | bytes 6291460
  6.3 28.4 %all-to-all-start = ((f32[256,2,128]{2,1,0:T(2,128)}), f32[256,2,128]{2,1,0:T(2,128)S(1)}, u32[]{:S(2)}, u32[]{:S(2)}) async-start(f32[256,2,128]{2,1,0:T(2,128)} %reshape.285), calls=%async_computation | async-start | bytes 524288 | tf_op jit(solution)/shard_map/all_to_all | solution.py:82
  22.8 15.1 %copy-start.4 = (bf16[16,8,32,32]{3,2,1,0:T(8,128)(2,1)}, bf16[16,8,32,32]{3,2,1,0:T(8,128)(2,1)S(1)}, u32[]{:S(2)}) copy-start(bf16[16,8,32,32]{3,2,1,0:T(8,128)(2,1)S(1)} %reshape.287) | copy-start | bytes 786436
  35.6 0.6 copy-start.5
  59.9 3.7 %copy-start.6 = (bf16[32,32]{1,0:T(8,128)(2,1)S(1)}, bf16[32,32]{1,0:T(8,128)(2,1)}, u32[]{:S(2)}) copy-start(bf16[32,32]{1,0:T(8,128)(2,1)} %param.11) | copy-start | bytes 6148
  59.9 3.7 %copy-start.12 = (bf16[8,1,32,4096]{3,2,1,0:T(8,128)(2,1)S(1)}, bf16[8,1,32,4096]{3,2,1,0:T(8,128)(2,1)}, u32[]{:S(2)}) copy-start(bf16[8,1,32,4096]{3,2,1,0:T(8,128)(2,1)} %param.13) | copy-start | bytes 6291460
  60.0 3.7 %copy-start.13 = (f32[32]{0:T(128)S(1)}, f32[32]{0:T(128)}, u32[]{:S(2)}) copy-start(f32[32]{0:T(128)} %param.12) | copy-start | bytes 388
  68.2 1.3 copy-start.2
  70.6 3.7 %copy-start.8 = (s32[8]{0:T(128)S(1)}, s32[8]{0:T(128)}, u32[]{:S(2)}) copy-start(s32[8]{0:T(128)} %copy-done.7) | copy-start | bytes 100
  76.7 25.7 %all-to-all-start.2 = ((f32[256,3,128]{2,1,0:T(4,128)}), f32[256,3,128]{2,1,0:T(4,128)S(1)}, u32[]{:S(2)}, u32[]{:S(2)}) async-start(f32[256,3,128]{2,1,0:T(4,128)} %select_maximum_fusion), calls=%async_computation.2 | async-start | bytes 1048576 | tf_op jit(solution)/shard_map/all_to_all | solution.py:82
  109.4 26.2 %all-to-all-start.3 = ((f32[256,3,128]{2,1,0:T(4,128)}), f32[256,3,128]{2,1,0:T(4,128)S(1)}, u32[]{:S(2)}, u32[]{:S(2)}) async-start(f32[256,3,128]{2,1,0:T(4,128)} %bitcast.35), calls=%async_computation.3 | async-start | bytes 1048576 | tf_op jit(solution)/shard_map/all_to_all | solution.py:104
  120.1 17.9 %copy-start.9 = (s32[8]{0:T(128)S(1)}, s32[8]{0:T(128)}, u32[]{:S(2)}) copy-start(s32[8]{0:T(128)} %copy-done.7) | copy-start | bytes 100
  138.5 2.5 %copy-start.3 = (bf16[8,1,32,4096]{3,2,0,1:T(8,128)(2,1)S(1)}, bf16[8,1,32,4096]{3,2,0,1:T(8,128)(2,1)}, u32[]{:S(2)}) copy-start(bf16[8,1,32,4096]{3,2,0,1:T(8,128)(2,1)} %copy-done.2) | copy-start | bytes 6291460
